TPU v7x, 32 devices: a whole 2x2x4 slice. The times are simulated.
32 devices in a mesh: grp: 4 (over y, x), seq: 8 (over z, core).
Axes of the slice: x: 2, y: 2, z: 4, core: 2. Of those that a mesh axis runs over, the one named last changes fastest.
Arguments:
- tokens: bfloat16 [4, 4096, 768], P('grp', 'seq'), may hold values from -6 to 6
- first_values: bfloat16 [4, 4096, 384], P('grp', 'seq'), may hold values from -6 to 6
- placement: int32 [4, 8], P('grp'), may hold values from 0 to 7, each once within a row
- cotangent: bfloat16 [4, 4096, 768], P('grp', 'seq'), may hold values from -6 to 6
- first_norm_gain: bfloat16 [768], P(('grp', 'seq')), may hold values from 0.25 to 1.75
- first_norm_bias: bfloat16 [768], P(('grp', 'seq')), may hold values from -2 to 2
- query_weight: bfloat16 [768, 768], P(('grp', 'seq')), may hold values from -0.25 to 0.25
- query_bias: bfloat16 [768], P(('grp', 'seq')), may hold values from -2 to 2
- key_weight: bfloat16 [768, 768], P(('grp', 'seq')), may hold values from -0.25 to 0.25
- value_weight: bfloat16 [768, 384], P(('grp', 'seq')), may hold values from -0.21875 to 0.21875
- value_bias: bfloat16 [384], P(('grp', 'seq')), may hold values from -2 to 2
- output_weight: bfloat16 [768, 768], P(('grp', 'seq')), may hold values from -1.5 to 1.5
- output_bias: bfloat16 [768], P(('grp', 'seq')), may hold values from -2 to 2
- second_norm_gain: bfloat16 [768], P(('grp', 'seq')), may hold values from 0.25 to 1.75
- second_norm_bias: bfloat16 [768], P(('grp', 'seq')), may hold values from -2 to 2
- expand_weight: bfloat16 [768, 3072], P(('grp', 'seq')), may hold values from -0.21875 to 0.21875
- expand_bias: bfloat16 [3072], P(('grp', 'seq')), may hold values from -2 to 2
- reduce_weight: bfloat16 [3072, 768], P(('grp', 'seq')), may hold values from -0.109375 to 0.109375
- reduce_bias: bfloat16 [768], P(('grp', 'seq')), may hold values from -2 to 2
Outputs:
- layer_output: bfloat16 [4, 4096, 768], P('grp', 'seq')
- token_grad: float32 [4, 4096, 768], P('grp', 'seq')
- first_values_grad: float32 [4, 4096, 384], P('grp', 'seq')
- first_norm_gain_grad: float32 [768], P(('grp', 'seq'))
- first_norm_bias_grad: float32 [768], P(('grp', 'seq'))
- query_weight_grad: float32 [768, 768], P(('grp', 'seq'))
- query_bias_grad: float32 [768], P(('grp', 'seq'))
- key_weight_grad: float32 [768, 768], P(('grp', 'seq'))
- value_weight_grad: float32 [768, 384], P(('grp', 'seq'))
- value_bias_grad: float32 [384], P(('grp', 'seq'))
- output_weight_grad: float32 [768, 768], P(('grp', 'seq'))
- output_bias_grad: float32 [768], P(('grp', 'seq'))
- second_norm_gain_grad: float32 [768], P(('grp', 'seq'))
- second_norm_bias_grad: float32 [768], P(('grp', 'seq'))
- expand_weight_grad: float32 [768, 3072], P(('grp', 'seq'))
- expand_bias_grad: float32 [3072], P(('grp', 'seq'))
- reduce_weight_grad: float32 [3072, 768], P(('grp', 'seq'))
- reduce_bias_grad: float32 [768], P(('grp', 'seq'))
Inputs may be any that keep to these rules, and one draw needn't show every extreme that they name: Each row of placement names every piece of its group once; pieces below 4 are prompt pieces in order, the others continuations.
All inputs are finite; a program needn't handle non-finite values.
Results may differ from a plain program's by a relative error of at most 0.019.
Values may be sent and summed in bfloat16 or wider, within the bound.
A program may use at most 256 MiB of HBM per device.

v0:
```python
import math

import jax
import jax.numpy as jnp
from jax import lax
from jax.sharding import PartitionSpec as P

HEAD = 64
FRESH = 6


EPS = 1e-05
NEG = -1e30


def normalize(v, gain, shift):
    mean = jnp.mean(v, axis=-1, keepdims=True)
    centred = v - mean
    var = jnp.mean(centred * centred, axis=-1, keepdims=True)
    return centred * lax.rsqrt(var + EPS) * gain + shift


def gelu_tanh(v):
    return jax.nn.gelu(v, approximate=True)


def matmul(a, b):
    return jnp.dot(a, b, preferred_element_type=jnp.float32)


def matmul_left(a, b):
    return lax.dot_general(a, b, (((0,), (0,)), ((), ())), preferred_element_type=jnp.float32)


def matmul_right(a, b):
    return lax.dot_general(a, b, (((1,), (1,)), ((), ())), preferred_element_type=jnp.float32)


def collect(parts):
    whole = (
        lax.all_gather(parts[0], ("grp", "seq"), axis=0, tiled=True),
        lax.all_gather(parts[1], ("grp", "seq"), axis=0, tiled=True),
        lax.all_gather(parts[2], ("grp", "seq"), axis=0, tiled=True),
        lax.all_gather(parts[3], ("grp", "seq"), axis=0, tiled=True),
        lax.all_gather(parts[4], ("grp", "seq"), axis=0, tiled=True),
        lax.all_gather(parts[5], ("grp", "seq"), axis=0, tiled=True),
        lax.all_gather(parts[6], ("grp", "seq"), axis=0, tiled=True),
        lax.all_gather(parts[7], ("grp", "seq"), axis=0, tiled=True),
        lax.all_gather(parts[8], ("grp", "seq"), axis=0, tiled=True),
        lax.all_gather(parts[9], ("grp", "seq"), axis=0, tiled=True),
        lax.all_gather(parts[10], ("grp", "seq"), axis=0, tiled=True),
        lax.all_gather(parts[11], ("grp", "seq"), axis=0, tiled=True),
        lax.all_gather(parts[12], ("grp", "seq"), axis=0, tiled=True),
        lax.all_gather(parts[13], ("grp", "seq"), axis=0, tiled=True),
        lax.all_gather(parts[14], ("grp", "seq"), axis=0, tiled=True),
    )
    return whole


def own_piece_of(table, slot):
    places = jnp.arange(table.shape[0], dtype=jnp.int32)
    return jnp.sum(jnp.where(places == slot, table, 0))


def layout_whole(table, slot, rows, total):
    count = table.shape[0]
    places = jnp.arange(count, dtype=jnp.int32)
    key_matrix = jnp.arange(total, dtype=jnp.int32)
    key_slot = key_matrix // rows
    piece = jnp.sum(jnp.where(key_slot[:, None] == places[None, :], table[None, :], 0), axis=1)
    return (piece, key_matrix % rows, own_piece_of(table, slot))


def key_mask(layout, half, start, block, rows):
    piece_all, pos_all, own = layout
    piece = lax.dynamic_slice_in_dim(piece_all, start, block, 0)
    key_pos = lax.dynamic_slice_in_dim(pos_all, start, block, 0)
    early = (piece < half) & ((piece < own) | (own >= half))
    same = piece == own
    query_pos = jnp.arange(rows, dtype=jnp.int32)
    allow = early[None, :] | same[None, :] & (key_pos[None, :] <= query_pos[:, None])
    return (allow, jnp.any(early | same))


def attend_forward(query_matrix, key_matrix, value_matrix, layout, half, rows, block):
    heads = query_matrix.shape[1]
    depth = query_matrix.shape[2]
    total = key_matrix.shape[0]

    def step(carry, index):
        start = index * block
        allow, live = key_mask(layout, half, start, block, rows)

        def work(state):
            top, denom, accum = state
            key_portion = lax.dynamic_slice_in_dim(key_matrix, start, block, 0)
            value_portion = lax.dynamic_slice_in_dim(value_matrix, start, block, 0)
            logit_score = (
                jnp.einsum(
                    "vwa,ewa->wve", query_matrix, key_portion, preferred_element_type=jnp.float32
                )
                * 0.125
            )
            logit_score = jnp.where(allow[None], logit_score, NEG)
            new_top = jnp.maximum(top, jnp.max(logit_score, axis=-1))
            weight = jnp.where(allow[None], jnp.exp(logit_score - new_top[..., None]), 0.0)
            factor = jnp.exp(top - new_top)
            denom = denom * factor + jnp.sum(weight, axis=-1)
            accum = accum * factor[..., None] + jnp.einsum(
                "paq,qpc->pac",
                weight.astype(jnp.bfloat16),
                value_portion,
                preferred_element_type=jnp.float32,
            )
            return (new_top, denom, accum)

        return (lax.cond(live, work, lambda state: state, carry), None)

    init = (
        jnp.full((heads, rows), NEG, jnp.float32),
        jnp.zeros((heads, rows), jnp.float32),
        jnp.zeros((heads, rows, depth), jnp.float32),
    )
    (top, denom, accum), _ = lax.scan(step, init, jnp.arange(total // block))
    out = accum / denom[..., None]
    return (jnp.transpose(out, (1, 0, 2)), top + jnp.log(denom))


def attend_backward(
    query_matrix,
    key_matrix,
    value_matrix,
    output_gradient_rows,
    delta,
    logsum,
    layout,
    half,
    rows,
    block,
):
    heads = query_matrix.shape[1]
    depth = query_matrix.shape[2]
    total = key_matrix.shape[0]

    def step(grad_query, index):
        start = index * block
        allow, live = key_mask(layout, half, start, block, rows)

        def work(grad_query):
            key_portion = lax.dynamic_slice_in_dim(key_matrix, start, block, 0)
            value_portion = lax.dynamic_slice_in_dim(value_matrix, start, block, 0)
            logit_score = (
                jnp.einsum(
                    "vwa,ewa->wve", query_matrix, key_portion, preferred_element_type=jnp.float32
                )
                * 0.125
            )
            attention_probability = jnp.where(
                allow[None], jnp.exp(logit_score - logsum[..., None]), 0.0
            )
            grad_prob = jnp.einsum(
                "vwa,ewa->wve",
                output_gradient_rows,
                value_portion,
                preferred_element_type=jnp.float32,
            )
            score_gradient_terms = (attention_probability * (grad_prob - delta[..., None])).astype(
                jnp.bfloat16
            )
            grad_query = (
                grad_query
                + jnp.einsum(
                    "qjy,yqk->jqk",
                    score_gradient_terms,
                    key_portion,
                    preferred_element_type=jnp.float32,
                )
                * 0.125
            )
            grad_key = (
                jnp.einsum(
                    "oae,aoj->eoj",
                    score_gradient_terms,
                    query_matrix,
                    preferred_element_type=jnp.float32,
                )
                * 0.125
            )
            grad_value = jnp.einsum(
                "oae,aoj->eoj",
                attention_probability.astype(jnp.bfloat16),
                output_gradient_rows,
                preferred_element_type=jnp.float32,
            )
            return (grad_query, (grad_key, grad_value))

        def skip(grad_query):
            zeros = jnp.zeros((block, heads, depth), jnp.float32)
            return (grad_query, (zeros, zeros))

        return lax.cond(live, work, skip, grad_query)

    start_grad = jnp.zeros((rows, heads, depth), jnp.float32)
    grad_query, (key_grads, value_grads) = lax.scan(step, start_grad, jnp.arange(total // block))
    return (
        grad_query,
        key_grads.reshape(total, heads * depth),
        value_grads.reshape(total, heads * depth),
    )


def body(
    tokens,
    first_values,
    placement,
    cotangent,
    first_norm_gain,
    first_norm_bias,
    query_weight,
    query_bias,
    key_weight,
    value_weight,
    value_bias,
    output_weight,
    output_bias,
    second_norm_gain,
    second_norm_bias,
    expand_weight,
    expand_bias,
    reduce_weight,
    reduce_bias,
):
    groups, rows, width = tokens.shape
    heads = width // HEAD
    fresh_width = FRESH * HEAD
    count = placement.shape[1]
    half = count // 2
    slot = lax.axis_index("seq")
    parts = (
        first_norm_gain,
        first_norm_bias,
        query_weight,
        query_bias,
        key_weight,
        value_weight,
        value_bias,
        output_weight,
        output_bias,
        second_norm_gain,
        second_norm_bias,
        expand_weight,
        expand_bias,
        reduce_weight,
        reduce_bias,
    )
    whole = collect(parts)
    gain_one = whole[0].astype(jnp.float32)
    bias_one = whole[1].astype(jnp.float32)
    gain_two = whole[9].astype(jnp.float32)
    bias_two = whole[10].astype(jnp.float32)
    flat = tokens.reshape(groups * rows, width).astype(jnp.float32)
    normed, norm_one_back = jax.vjp(normalize, flat, gain_one, bias_one)
    hidden = normed.astype(jnp.bfloat16)
    query_matrix = (matmul(hidden, whole[2]) + whole[3].astype(jnp.float32)).astype(jnp.bfloat16)
    keyed = matmul(hidden, whole[4]).astype(jnp.bfloat16)
    valued = (matmul(hidden, whole[5]) + whole[6].astype(jnp.float32)).astype(jnp.bfloat16)
    keys_local = keyed.reshape(groups, rows, width)
    values_local = jnp.concatenate(
        [valued.reshape(groups, rows, fresh_width), first_values], axis=2
    )
    gathered_keys, gathered_values = (
        lax.all_gather(keys_local, "seq", axis=1, tiled=True),
        lax.all_gather(values_local, "seq", axis=1, tiled=True),
    )
    total = gathered_keys.shape[1]
    block = math.gcd(total, 512)
    layouts = [layout_whole(placement[0], slot, rows, total)]
    query_heads = query_matrix.reshape(groups, rows, heads, HEAD)
    index = 0
    out, logsum = attend_forward(
        query_heads[index],
        gathered_keys[index].reshape(total, heads, HEAD),
        gathered_values[index].reshape(total, heads, HEAD),
        layouts[index],
        half,
        rows,
        block,
    )
    sums = [logsum]
    attended = out.reshape(groups * rows, width)
    attended_low = attended.astype(jnp.bfloat16)
    middle = flat + matmul(attended_low, whole[7]) + whole[8].astype(jnp.float32)
    normed_two, norm_two_back = jax.vjp(normalize, middle, gain_two, bias_two)
    second = normed_two.astype(jnp.bfloat16)
    pre = matmul(second, whole[11]) + whole[12].astype(jnp.float32)
    post_full, gelu_back = jax.vjp(gelu_tanh, pre)
    post = post_full.astype(jnp.bfloat16)
    result = middle + matmul(post, whole[13]) + whole[14].astype(jnp.float32)
    layer_output = result.astype(jnp.bfloat16).reshape(groups, rows, width)
    again = collect(parts)
    seed = cotangent.reshape(groups * rows, width)
    seed_full = seed.astype(jnp.float32)
    grad_reduce_bias = jnp.sum(seed_full, axis=0)
    grad_reduce = matmul_left(post, seed)
    grad_post = matmul_right(seed, again[13])
    grad_pre = gelu_back(grad_post)[0].astype(jnp.bfloat16)
    grad_expand_bias = jnp.sum(grad_pre.astype(jnp.float32), axis=0)
    grad_expand = matmul_left(second, grad_pre)
    grad_second = matmul_right(grad_pre, again[11])
    grad_mid_norm, grad_gain_two, grad_bias_two = norm_two_back(grad_second)
    grad_mid = grad_mid_norm + seed_full
    grad_branch = grad_mid.astype(jnp.bfloat16)
    grad_output_bias = jnp.sum(grad_branch.astype(jnp.float32), axis=0)
    grad_output = matmul_left(attended_low, grad_branch)
    grad_attended = matmul_right(grad_branch, again[7]).astype(jnp.bfloat16)
    full_keys, full_values = (
        lax.all_gather(keys_local, "seq", axis=1, tiled=True),
        lax.all_gather(values_local, "seq", axis=1, tiled=True),
    )
    gathered_keys, gathered_values = (full_keys, full_values)
    grad_attended_heads = grad_attended.reshape(groups, rows, heads, HEAD)
    attended_heads = attended.reshape(groups, rows, heads, HEAD)
    index = 0
    delta = jnp.transpose(
        jnp.sum(grad_attended_heads[index].astype(jnp.float32) * attended_heads[index], axis=-1)
    )
    grad_query, grad_keys, grad_values = attend_backward(
        query_heads[index],
        gathered_keys[index].reshape(total, heads, HEAD),
        gathered_values[index].reshape(total, heads, HEAD),
        grad_attended_heads[index],
        delta,
        sums[index],
        layouts[index],
        half,
        rows,
        block,
    )
    key_terms = [grad_keys]
    value_terms = [grad_values]
    key_stack = jnp.stack(key_terms)
    value_stack = jnp.stack(value_terms)
    key_sums, value_sums = (
        lax.psum_scatter(
            key_stack.astype(jnp.bfloat16), "seq", scatter_dimension=1, tiled=True
        ).astype(jnp.float32),
        lax.psum_scatter(
            value_stack.astype(jnp.bfloat16), "seq", scatter_dimension=1, tiled=True
        ).astype(jnp.float32),
    )
    grad_key = key_sums.reshape(groups * rows, width).astype(jnp.bfloat16)
    grad_fresh = (
        value_sums[:, :, :fresh_width].reshape(groups * rows, fresh_width).astype(jnp.bfloat16)
    )
    first_values_grad = value_sums[:, :, fresh_width:]
    grad_query_all = grad_query.reshape(groups * rows, width).astype(jnp.bfloat16)
    grad_query_bias = jnp.sum(grad_query_all.astype(jnp.float32), axis=0)
    grad_query_weight = matmul_left(hidden, grad_query_all)
    grad_key_weight = matmul_left(hidden, grad_key)
    grad_value_weight = matmul_left(hidden, grad_fresh)
    grad_value_bias = jnp.sum(grad_fresh.astype(jnp.float32), axis=0)
    grad_hidden = (
        matmul_right(grad_query_all, again[2])
        + matmul_right(grad_key, again[4])
        + matmul_right(grad_fresh, again[5])
    )
    grad_in, grad_gain_one, grad_bias_one = norm_one_back(grad_hidden)
    token_grad = (grad_in + grad_mid).reshape(groups, rows, width)
    owned = (
        lax.psum_scatter(grad_gain_one, ("grp", "seq"), scatter_dimension=0, tiled=True),
        lax.psum_scatter(grad_bias_one, ("grp", "seq"), scatter_dimension=0, tiled=True),
        lax.psum_scatter(grad_query_weight, ("grp", "seq"), scatter_dimension=0, tiled=True),
        lax.psum_scatter(grad_query_bias, ("grp", "seq"), scatter_dimension=0, tiled=True),
        lax.psum_scatter(grad_key_weight, ("grp", "seq"), scatter_dimension=0, tiled=True),
        lax.psum_scatter(grad_value_weight, ("grp", "seq"), scatter_dimension=0, tiled=True),
        lax.psum_scatter(grad_value_bias, ("grp", "seq"), scatter_dimension=0, tiled=True),
        lax.psum_scatter(grad_output, ("grp", "seq"), scatter_dimension=0, tiled=True),
        lax.psum_scatter(grad_output_bias, ("grp", "seq"), scatter_dimension=0, tiled=True),
        lax.psum_scatter(grad_gain_two, ("grp", "seq"), scatter_dimension=0, tiled=True),
        lax.psum_scatter(grad_bias_two, ("grp", "seq"), scatter_dimension=0, tiled=True),
        lax.psum_scatter(grad_expand, ("grp", "seq"), scatter_dimension=0, tiled=True),
        lax.psum_scatter(grad_expand_bias, ("grp", "seq"), scatter_dimension=0, tiled=True),
        lax.psum_scatter(grad_reduce, ("grp", "seq"), scatter_dimension=0, tiled=True),
        lax.psum_scatter(grad_reduce_bias, ("grp", "seq"), scatter_dimension=0, tiled=True),
    )
    return (
        layer_output,
        token_grad,
        first_values_grad,
        owned[0],
        owned[1],
        owned[2],
        owned[3],
        owned[4],
        owned[5],
        owned[6],
        owned[7],
        owned[8],
        owned[9],
        owned[10],
        owned[11],
        owned[12],
        owned[13],
        owned[14],
    )


def solution(mesh):
    in_specs = (
        P("grp", "seq", None),
        P("grp", "seq", None),
        P("grp", None),
        P("grp", "seq", None),
        P(("grp", "seq")),
        P(("grp", "seq")),
        P(("grp", "seq"), None),
        P(("grp", "seq")),
        P(("grp", "seq"), None),
        P(("grp", "seq"), None),
        P(("grp", "seq")),
        P(("grp", "seq"), None),
        P(("grp", "seq")),
        P(("grp", "seq")),
        P(("grp", "seq")),
        P(("grp", "seq"), None),
        P(("grp", "seq")),
        P(("grp", "seq"), None),
        P(("grp", "seq")),
    )
    out_specs = (
        P("grp", "seq", None),
        P("grp", "seq", None),
        P("grp", "seq", None),
        P(("grp", "seq")),
        P(("grp", "seq")),
        P(("grp", "seq"), None),
        P(("grp", "seq")),
        P(("grp", "seq"), None),
        P(("grp", "seq"), None),
        P(("grp", "seq")),
        P(("grp", "seq"), None),
        P(("grp", "seq")),
        P(("grp", "seq")),
        P(("grp", "seq")),
        P(("grp", "seq"), None),
        P(("grp", "seq")),
        P(("grp", "seq"), None),
        P(("grp", "seq")),
    )
    return jax.shard_map(body, mesh=mesh, in_specs=in_specs, out_specs=out_specs, check_vma=False)
```

profile of v0, /device:TPU:0, one launch (start us, length us, event | category | flops | bytes accessed | tf_op | source)
XLA Modules:
  0.0 1508.5 jit_solution(9225255534261117554)
XLA Ops:
  16.3 42.6 %all-reduce.20 = (bf16[768]{0:T(1024)(128)(2,1)S(1)}, bf16[768]{0:T(1024)(128)(2,1)S(1)}, bf16[768]{0:T(1024)(128)(2,1)S(1)}, bf16[384]{0:T(512)(128)(2,1)S(1)},...) all-reduce(bf16[768]{0:T(1024)(128)(2,1)S(1)} %dynamic-update-slice, ...), channel_id=1, replica_groups=mesh['grp'=4,'seq'=8] {'grp','seq'}, use_global_device_ids=true, to_apply=%add.1 | all-reduce | flops 8832 | bytes 35328
  60.3 1.5 fusion.57
  61.8 6.2 all-gather.9.cloned.1.call-done
  68.0 3.1 convolution_convert_fusion.1
  71.8 42.2 %all_gather.65 = bf16[768,384]{1,0:T(8,128)(2,1)S(1)} all-gather(bf16[24,384]{1,0:T(8,128)(2,1)S(1)} %copy-done.38), channel_id=1, replica_groups=mesh['grp'=4,'seq'=8] {'grp','seq'}, dimensions={0}, use_global_device_ids=true | all-gather | bytes 608256 | tf_op jit(solution)/shard_map/all_gather | solution.py:46
  119.4 5.3 all-gather.11.cloned.1.call-done
  124.7 2.2 add_convert_fusion.2
  127.2 63.5 %all-gather.21.cloned.1.call-done = bf16[4096,768]{1,0:T(8,128)(2,1)} async-done(((bf16[512,768]{1,0:T(8,128)(2,1)}), bf16[4096,768]{1,0:T(8,128)(2,1)}) %all-gather.21.cloned.1.call-update) | async-done | bytes 6291472 | tf_op jit(solution)/shard_map/all_gather | solution.py:272
  190.6 8.9 copy.75
  199.5 56.6 %all-gather.13.cloned.1.call-done = bf16[1,4096,768]{1,2,0:T(8,128)(2,1)} async-done(((bf16[1,512,768]{1,2,0:T(8,128)(2,1)}), bf16[1,4096,768]{1,2,0:T(8,128)(2,1)}) %all-gather.13.cloned.1.call-update) | async-done | bytes 6291472 | tf_op jit(solution)/shard_map/all_gather | solution.py:273
  257.4 57.1 %while.35 = (s32[]{:T(128)}, f32[12,512]{1,0:T(8,128)S(1)}, f32[12,512]{1,0:T(8,128)S(1)}, f32[12,512,64]{1,2,0:T(8,128)}, s32[8]{0:T(128)S(1)}, /*index=5*/s32[...) while((s32[]{:T(128)}, f32[12,512]{1,0:T(8,128)S(1)}, ...), condition=%wide.region_10.11_spmd.clone, body=%wide.region_4.10_spmd.clone.sunk | while | flops 847796224 | bytes 59427328 | solution.py:124
  260.8 14.8 conditional.6
  261.2 5.0 fusion.4
  266.2 3.1 fusion.6
  269.4 5.0 multiply_add_fusion
  285.9 14.8 conditional.6
  286.3 5.0 fusion.4
  291.4 3.1 fusion.6
  294.6 5.0 multiply_add_fusion
  314.5 1.6 bitcast_convert_fusion
  316.2 2.5 fusion.103
  320.1 57.2 %all-gather.17.cloned.1.call-done = bf16[768,3072]{1,0:T(8,128)(2,1)} async-done(((bf16[24,3072]{1,0:T(8,128)(2,1)}), bf16[768,3072]{1,0:T(8,128)(2,1)}) %all-gather.17.cloned.1.call-update) | async-done | bytes 4718608 | tf_op jit(solution)/shard_map/all_gather | solution.py:52
  377.4 8.2 fusion.92
  385.6 57.3 %all-gather.19.cloned.1.call-done = bf16[3072,768]{1,0:T(8,128)(2,1)} async-done(((bf16[96,768]{1,0:T(8,128)(2,1)}), bf16[3072,768]{1,0:T(8,128)(2,1)}) %all-gather.19.cloned.1.call-update) | async-done | bytes 4718608 | tf_op jit(solution)/shard_map/all_gather | solution.py:54
  442.9 9.9 convert_reduce_fusion
  452.9 3.5 multiply_reduce_fusion
  459.2 1.7 convolution_convert_fusion
  460.9 2.4 copy.78
  466.1 96.0 %while.36 = (s32[]{:T(128)}, f32[512,12,64]{0,2,1:T(8,128)}, bf16[8,512,12,64]{1,3,2,0:T(8,128)(2,1)}, bf16[8,512,12,64]{1,3,2,0:T(8,128)(2,1)}, s32[8]{0:T(128)...) while((s32[]{:T(128)}, f32[512,12,64]{0,2,1:T(8,128)}, ...), condition=%wide.region_20.21_spmd.clone, body=%wide.region_16.20_spmd.clone.sunk | while | flops 2047092736 | bytes 88730152 | solution.py:204
  469.9 28.3 %conditional.7 = (f32[512,12,64]{0,2,1:T(8,128)}, bf16[1,512,12,64]{1,3,2,0:T(8,128)(2,1)S(1)}, bf16[1,512,12,64]{1,3,2,0:T(8,128)(2,1)S(1)}) conditional(s32[]{:T(128)} %convert_element_type.327, f32[512,12,64]{0,2,1:T(8,128)} %get-tuple-element.958, (s32[]{:T(128)}, bf16[4096,12,64]{0,2,1:T(8,128)(2,1)}, pred[512]{0:T(512)(128)(4,1)S(1)}, ...), branch_computations={%region_18.18_spmd, %region_19.19_spmd.clone} | conditional | flops 2047085056 | bytes 84499616 | solution.py:201
  470.3 9.4 fusion.31
  479.7 7.7 fusion.21
  487.4 6.2 fusion.26
  493.6 2.6 bitcast_add_fusion
  496.2 2.0 multiply_bitcast_fusion
  512.7 28.3 %conditional.7 = (f32[512,12,64]{0,2,1:T(8,128)}, bf16[1,512,12,64]{1,3,2,0:T(8,128)(2,1)S(1)}, bf16[1,512,12,64]{1,3,2,0:T(8,128)(2,1)S(1)}) conditional(s32[]{:T(128)} %convert_element_type.327, f32[512,12,64]{0,2,1:T(8,128)} %get-tuple-element.958, (s32[]{:T(128)}, bf16[4096,12,64]{0,2,1:T(8,128)(2,1)}, pred[512]{0:T(512)(128)(4,1)S(1)}, ...), branch_computations={%region_18.18_spmd, %region_19.19_spmd.clone} | conditional | flops 2047085056 | bytes 84499616 | solution.py:201
  513.1 9.4 fusion.31
  522.5 7.7 fusion.21
  530.3 6.2 fusion.26
  536.5 2.6 bitcast_add_fusion
  539.0 2.0 multiply_bitcast_fusion
  562.1 9.5 copy.80
  571.6 10.5 convert_element_type.198
  582.2 9.5 copy.79
  591.7 10.4 convert_element_type.195
  603.5 2.2 fusion.105
  608.2 2.5 fusion.98
  611.0 10.0 fusion.74
  622.5 7.2 fusion.91
  629.7 105.7 %reduce-scatter.13.cloned.1.call-done = bf16[1,512,768]{1,2,0:T(8,128)(2,1)} async-done(((bf16[1,4096,768]{1,2,0:T(8,128)(2,1)}), bf16[1,512,768]{1,2,0:T(8,128)(2,1)}) %reduce-scatter.13.cloned.1.call-update) | async-done | bytes 786448 | tf_op jit(solution)/shard_map/reduce_scatter | solution.py:347
  735.4 2.9 fusion.87
  738.4 67.6 %reduce-scatter.11.cloned.1.call-done = bf16[1,512,768]{1,2,0:T(8,128)(2,1)} async-done(((bf16[1,4096,768]{1,2,0:T(8,128)(2,1)}), bf16[1,512,768]{1,2,0:T(8,128)(2,1)}) %reduce-scatter.11.cloned.1.call-update) | async-done | bytes 786448 | tf_op jit(solution)/shard_map/reduce_scatter | solution.py:344
  805.9 3.6 fusion.70
  809.6 3.5 fusion.104
  813.2 9.1 fusion.65
  823.7 2.5 fusion.72
  828.1 38.6 %all-reduce.19 = (f32[768]{0:T(1024)S(1)}, f32[768]{0:T(1024)S(1)}, f32[768]{0:T(1024)S(1)}, f32[384]{0:T(512)S(1)}, f32[768]{0:T(1024)S(1)}, /*index=5*/f32[768...) all-reduce(f32[768]{0:T(1024)S(1)} %get-tuple-element.604, ...), channel_id=5, replica_groups=mesh['grp'=4,'seq'=8] {'grp','seq'}, use_global_device_ids=true, to_apply=%region_26.27.clone | all-reduce | flops 8832 | bytes 70656
  872.0 3.2 add_bitcast_fusion
  875.2 34.1 %reduce-scatter.19.cloned.1.call-done = f32[24,768]{1,0:T(8,128)} async-done(((f32[768,768]{1,0:T(8,128)}), f32[24,768]{1,0:T(8,128)}) %reduce-scatter.19.cloned.1.call-update) | async-done | bytes 73744 | tf_op jit(solution)/shard_map/reduce_scatter | solution.py:377
  909.4 104.7 %reduce-scatter.15.cloned.1.call-done = f32[24,768]{1,0:T(8,128)} async-done(((f32[768,768]{1,0:T(8,128)}), f32[24,768]{1,0:T(8,128)}) %reduce-scatter.15.cloned.1.call-update) | async-done | bytes 73744 | tf_op jit(solution)/shard_map/reduce_scatter | solution.py:372
  1014.1 141.1 %reduce-scatter.23.cloned.1.call-done = f32[96,768]{1,0:T(8,128)} async-done(((f32[3072,768]{1,0:T(8,128)}), f32[96,768]{1,0:T(8,128)}) %reduce-scatter.23.cloned.1.call-update) | async-done | bytes 294928 | tf_op jit(solution)/shard_map/reduce_scatter | solution.py:383
  1155.2 142.0 %reduce-scatter.21.cloned.1.call-done = f32[24,3072]{1,0:T(8,128)} async-done(((f32[768,3072]{1,0:T(8,128)}), f32[24,3072]{1,0:T(8,128)}) %reduce-scatter.21.cloned.1.call-update) | async-done | bytes 294928 | tf_op jit(solution)/shard_map/reduce_scatter | solution.py:381
  1297.2 100.8 %reduce-scatter.25.cloned.1.call-done = f32[24,384]{1,0:T(8,128)} async-done(((f32[768,384]{1,0:T(8,128)}), f32[24,384]{1,0:T(8,128)}) %reduce-scatter.25.cloned.1.call-update) | async-done | bytes 36880
  1398.0 103.8 %reduce-scatter.17.cloned.1.call-done = f32[24,768]{1,0:T(8,128)} async-done(((f32[768,768]{1,0:T(8,128)}), f32[24,768]{1,0:T(8,128)}) %reduce-scatter.17.cloned.1.call-update) | async-done | bytes 73744 | tf_op jit(solution)/shard_map/reduce_scatter | solution.py:374
  (353 shorter events, 87.9 us)
Async XLA Ops:
  7.2 60.8 %copy-start.3 = (bf16[1,512,768]{2,1,0:T(8,128)(2,1)S(1)}, bf16[1,512,768]{2,1,0:T(8,128)(2,1)}, u32[]{:S(2)}) copy-start(bf16[1,512,768]{2,1,0:T(8,128)(2,1)} %param.27) | copy-start | bytes 2359300
  7.2 60.8 %all-gather.9.cloned.1.call-start = ((), (), s32[]{:S(2)}) async-start(), calls=%async_computation.8 | async-start | bytes 1216512 | tf_op jit(solution)/shard_map/all_gather | solution.py:45
  7.9 116.7 %all-gather.11.cloned.1.call-start = ((), (), s32[]{:S(2)}) async-start(), calls=%async_computation.9 | async-start | bytes 1216512 | tf_op jit(solution)/shard_map/all_gather | solution.py:43
  8.7 181.9 %all-gather.21.cloned.1.call-start = ((), (), s32[]{:S(2)}) async-start(), calls=%async_computation.21 | async-start | bytes 7077888 | tf_op jit(solution)/shard_map/all_gather | solution.py:272
  58.9 65.8 %copy-start.46 = (f32[768]{0:T(1024)}, f32[768]{0:T(1024)S(1)}, u32[]{:S(2)}) copy-start(f32[768]{0:T(1024)S(1)} %convert_element_type.170) | copy-start | bytes 9220
  58.9 65.8 %copy-start.26 = (f32[768]{0:T(1024)}, f32[768]{0:T(1024)S(1)}, u32[]{:S(2)}) copy-start(f32[768]{0:T(1024)S(1)} %convert_element_type.169) | copy-start | bytes 9220
  60.2 64.4 %copy-start.28 = (f32[512]{0:T(512)}, f32[512]{0:T(512)S(1)}, u32[]{:S(2)}) copy-start(f32[512]{0:T(512)S(1)} %broadcast_multiply_fusion.1) | copy-start | bytes 6148
  61.7 9.3 copy-start.36
  61.8 62.9 %copy-start.30 = (f32[512]{0:T(512)}, f32[512]{0:T(512)S(1)}, u32[]{:S(2)}) copy-start(f32[512]{0:T(512)S(1)} %fusion.84) | copy-start | bytes 6148
  61.8 9.4 copy-start.25
  71.1 185.0 %all-gather.13.cloned.1.call-start = ((), (), s32[]{:S(2)}) async-start(), calls=%async_computation.10 | async-start | bytes 7077888 | tf_op jit(solution)/shard_map/all_gather | solution.py:273
  114.8 3.2 copy-start.53
  115.7 200.5 %all-gather.15.cloned.1.call-start = ((), (), s32[]{:S(2)}) async-start(), calls=%async_computation.11 | async-start | bytes 1216512 | tf_op jit(solution)/shard_map/all_gather | solution.py:48
  116.3 261.0 %all-gather.17.cloned.1.call-start = ((), (), s32[]{:S(2)}) async-start(), calls=%async_computation.12 | async-start | bytes 4866048 | tf_op jit(solution)/shard_map/all_gather | solution.py:52
  116.9 326.0 %all-gather.19.cloned.1.call-start = ((), (), s32[]{:S(2)}) async-start(), calls=%async_computation.13 | async-start | bytes 4866048 | tf_op jit(solution)/shard_map/all_gather | solution.py:54
  117.6 617.8 %reduce-scatter.13.cloned.1.call-start = ((), (), s32[]{:S(2)}) async-start(), calls=%async_computation.15 | async-start | bytes 7077888 | tf_op jit(solution)/shard_map/reduce_scatter | solution.py:347
  117.9 338.5 %copy-start.41 = (f32[768]{0:T(1024)}, f32[768]{0:T(1024)S(1)}, u32[]{:S(2)}) copy-start(f32[768]{0:T(1024)S(1)} %convert_element_type.180) | copy-start | bytes 9220
  117.9 259.5 %copy-start.48 = (f32[768]{0:T(1024)}, f32[768]{0:T(1024)S(1)}, u32[]{:S(2)}) copy-start(f32[768]{0:T(1024)S(1)} %convert_element_type.181) | copy-start | bytes 9220
  266.2 3.2 copy-start.5
  274.5 1.1 copy-start.6
  291.4 3.2 copy-start.5
  316.1 2.5 copy-start.17
  318.7 137.7 %copy-start.34 = (f32[512]{0:T(512)}, f32[512]{0:T(512)S(1)}, u32[]{:S(2)}) copy-start(f32[512]{0:T(512)S(1)} %broadcast_multiply_fusion) | copy-start | bytes 6148
  320.1 136.3 %copy-start.44 = (f32[512]{0:T(512)}, f32[512]{0:T(512)S(1)}, u32[]{:S(2)}) copy-start(f32[512]{0:T(512)S(1)} %fusion.85) | copy-start | bytes 6148
  320.1 122.8 %copy-start.12 = (bf16[1,512,768]{2,1,0:T(8,128)(2,1)S(1)}, bf16[1,512,768]{2,1,0:T(8,128)(2,1)}, u32[]{:S(2)}) copy-start(bf16[1,512,768]{2,1,0:T(8,128)(2,1)} %param.30) | copy-start | bytes 2359300
  385.6 67.3 %copy-start.10 = (f32[512,768]{1,0:T(8,128)S(1)}, f32[512,768]{1,0:T(8,128)}, u32[]{:S(2)}) copy-start(f32[512,768]{1,0:T(8,128)} %copy-done.9) | copy-start | bytes 4718596
  442.9 10.0 copy-start.54
  452.8 3.5 copy-start.56
  457.0 1.3 copy-start.8
  457.0 1.2 copy-start.32
  457.0 2.1 copy-start.55
  460.9 2.4 copy-start.7
  470.3 9.4 copy-start.16
  487.4 6.2 copy-start
  496.2 2.0 copy-start.1
  513.1 9.4 copy-start.16
  530.2 6.2 copy-start
  539.0 2.0 copy-start.1
  582.1 223.8 %reduce-scatter.11.cloned.1.call-start = ((), (), s32[]{:S(2)}) async-start(), calls=%async_computation.14 | async-start | bytes 7077888 | tf_op jit(solution)/shard_map/reduce_scatter | solution.py:344
  602.2 1.4 copy-start.20
  602.2 307.2 %reduce-scatter.19.cloned.1.call-start = ((), (), s32[]{:S(2)}) async-start(), calls=%async_computation.18 | async-start | bytes 2433024 | tf_op jit(solution)/shard_map/reduce_scatter | solution.py:377
  605.7 1.4 copy-start.2
  605.7 2.5 copy-start.4
  605.7 2.5 copy-start.27
  605.8 2.5 copy-start.29
  605.8 2.4 copy-start.31
  605.8 2.4 copy-start.47
  605.8 408.3 %reduce-scatter.15.cloned.1.call-start = ((), (), s32[]{:S(2)}) async-start(), calls=%async_computation.16 | async-start | bytes 2433024 | tf_op jit(solution)/shard_map/reduce_scatter | solution.py:372
  610.7 544.4 %reduce-scatter.23.cloned.1.call-start = ((), (), s32[]{:S(2)}) async-start(), calls=%async_computation.20 | async-start | bytes 9732096 | tf_op jit(solution)/shard_map/reduce_scatter | solution.py:383
  621.0 1.4 copy-start.11
  621.0 1.4 copy-start.35
  621.0 1.4 copy-start.42
  621.0 1.4 copy-start.45
  621.0 1.4 copy-start.49
  621.1 676.1 %reduce-scatter.21.cloned.1.call-start = ((), (), s32[]{:S(2)}) async-start(), calls=%async_computation.19 | async-start | bytes 9732096 | tf_op jit(solution)/shard_map/reduce_scatter | solution.py:381
  629.6 108.7 %copy-start.52 = (bf16[768]{0:T(1024)(128)(2,1)S(1)}, bf16[768]{0:T(1024)(128)(2,1)}, u32[]{:S(2)}) copy-start(bf16[768]{0:T(1024)(128)(2,1)} %get-tuple-element.673) | copy-start | bytes 4612
  629.7 768.3 %reduce-scatter.25.cloned.1.call-start = ((), (), s32[]{:S(2)}) async-start(), calls=%async_computation.22 | async-start | bytes 1216512
  738.3 763.5 %reduce-scatter.17.cloned.1.call-start = ((), (), s32[]{:S(2)}) async-start(), calls=%async_computation.17 | async-start | bytes 2433024 | tf_op jit(solution)/shard_map/reduce_scatter | solution.py:374
  813.2 9.1 copy-start.13
  822.3 1.2 copy-start.14
  823.7 2.5 copy-start.15
  823.7 2.6 copy-start.22
  823.7 2.6 copy-start.23
  827.3 44.7 %copy-start.33 = (f32[512]{0:T(512)S(1)}, f32[512]{0:T(512)}, u32[]{:S(2)}) copy-start(f32[512]{0:T(512)} %copy-done.32) | copy-start | bytes 6148
  (13 other events, 12.0 us)
Sparse Core Ops, SparseCore 0:
  11.1 56.8 all-gather.8
  71.0 53.6 all-gather.10
  126.9 63.6 all-gather.20
  192.6 63.3 all-gather.12
  258.9 52.9 all-gather.14
  314.8 62.5 all-gather.16
  380.4 62.4 all-gather.18
  582.3 153.1 reduce-scatter.12
  737.7 68.1 reduce-scatter.10
  811.6 97.6 reduce-scatter.18
  916.1 97.9 reduce-scatter.14
  1020.4 134.6 reduce-scatter.22
  1162.7 134.4 reduce-scatter.20
  1302.7 95.2 reduce-scatter.24
  1403.7 98.0 reduce-scatter.16
where the time goes:
time: 1520 us; the launch traced here: 1510 us
  waiting for transfers between devices  1050 us (69%)
  matrix products  152 us (10%)
  blocking collectives  123 us (8%)
  local copies, waits for them, and re-layouts  101 us (7%)
  other arithmetic  43.5 us (3%)
  loops' own time  22.8 us (2%)
  between operations  15.5 us (1%)
    reduce_scatter x1, waiting for transfers between devices, body(): lax.psum_scatter(grad_expand, ('grp', 'seq'), scatter_dimension=0, tiled=...  142 us
    reduce_scatter x1, waiting for transfers between devices, body(): lax.psum_scatter(grad_reduce, ('grp', 'seq'), scatter_dimension=0, tiled=...  141 us
    reduce_scatter x1, waiting for transfers between devices, body(): lax.psum_scatter(value_stack.astype(jnp.bfloat16), 'seq', scatter_dimensi...  106 us
    reduce_scatter x1, waiting for transfers between devices, body(): lax.psum_scatter(grad_query_weight, ('grp', 'seq'), scatter_dimension=0,...  105 us
    unnamed x16, waiting for transfers between devices  104 us
    reduce_scatter x1, waiting for transfers between devices, body(): lax.psum_scatter(grad_key_weight, ('grp', 'seq'), scatter_dimension=0, ti...  104 us
    unnamed x2, blocking collectives  81.2 us
    reduce_scatter x1, waiting for transfers between devices, body(): lax.psum_scatter(key_stack.astype(jnp.bfloat16), 'seq', scatter_dimension...  67.6 us
  transfers between devices with their start and end apart: 15, of which 14 were waited for; matrix products, arithmetic and copies ran while one was open for 11% of the time, Pallas kernels for 0%

commit v1 on v0

--- a/solution.py
+++ b/solution.py
@@ -1,8 +1,11 @@
+import functools
 import math
 
 import jax
 import jax.numpy as jnp
 from jax import lax
+from jax.experimental import pallas as pl
+from jax.experimental.pallas import tpu as pltpu
 from jax.sharding import PartitionSpec as P
 
 HEAD = 64
@@ -36,25 +39,228 @@
     return lax.dot_general(a, b, (((1,), (1,)), ((), ())), preferred_element_type=jnp.float32)
 
 
+MESH = pl.DeviceIdType.MESH
+
+
+def powers(count):
+    out, bit = [], 1
+    while bit < count:
+        out.append(bit)
+        bit *= 2
+    return out
+
+
+def remote(src, dst, send, recv, device):
+    return pltpu.make_async_remote_copy(
+        src_ref=src, dst_ref=dst, send_sem=send, recv_sem=recv,
+        device_id=device, device_id_type=MESH,
+    )
+
+
+def enter(devices):
+    barrier = pltpu.get_barrier_semaphore()
+    for device in devices:
+        pl.semaphore_signal(barrier, inc=1, device_id=device, device_id_type=MESH)
+    pl.semaphore_wait(barrier, len(devices))
+
+
+class Gather:
+    def __init__(self, groups, chips, bits, shard, full, chain_send, level_send, recv, pair, own):
+        self.groups, self.chips, self.bits = groups, chips, bits
+        self.shard, self.full = shard, full
+        self.chain_send, self.level_send, self.recv, self.pair, self.own = chain_send, level_send, recv, pair, own
+        self.g = lax.axis_index("grp")
+        seq = lax.axis_index("seq")
+        self.s, self.z, self.c = seq, seq // 2, seq % 2
+
+    def block(self, g, z, c):
+        return self.full.at[g, z, c]
+
+    def source(self, mask, z, first):
+        return self.shard if first else self.block(self.g ^ mask, z, self.c)
+
+    def chain(self, z, step, first):
+        side = 0 if step < 0 else 1
+        return remote(self.source(0, z, first), self.block(self.g, z, self.c),
+                      self.chain_send.at[z, side], self.recv.at[self.g, z],
+                      {"seq": self.s + 2 * step})
+
+    def cross(self, level, mask, z, first):
+        g = self.g ^ mask
+        return remote(self.source(mask, z, first), self.block(g, z, self.c),
+                      self.level_send.at[level], self.recv.at[g, z],
+                      {"grp": self.g ^ self.bits[level]})
+
+    def held(self, level):
+        masks = [0]
+        for bit in self.bits[:level]:
+            masks = masks + [m ^ bit for m in masks]
+        return masks
+
+    def here(self, mask, z):
+        g = self.g ^ mask
+        pltpu.make_async_copy(self.block(g, z, self.c), self.block(g, z, self.c), self.recv.at[g, z]).wait()
+
+    def begin(self):
+        copy = pltpu.make_async_copy(self.shard, self.block(self.g, self.z, self.c), self.own)
+        copy.start()
+
+        @pl.when(self.z > 0)
+        def _():
+            self.chain(self.z, -1, True).start()
+
+        @pl.when(self.z < self.chips - 1)
+        def _():
+            self.chain(self.z, 1, True).start()
+
+        for level in range(len(self.bits)):
+            self.cross(level, 0, self.z, True).start()
+
+    def at(self, distance, body):
+        if distance == 0:
+            body(self.z, 0)
+            return
+
+        @pl.when(self.z >= distance)
+        def _():
+            body(self.z - distance, 1)
+
+        @pl.when(self.z + distance < self.chips)
+        def _():
+            body(self.z + distance, -1)
+
+    def along(self, distance):
+        def body(z, step):
+            self.here(0, z)
+            onward = self.z < self.chips - 1 if step > 0 else self.z > 0
+
+            @pl.when(onward)
+            def _():
+                self.chain(z, step, False).start()
+
+            for level in range(len(self.bits)):
+                self.cross(level, 0, z, False).start()
+
+        if distance > 0:
+            self.at(distance, body)
+
+    def over(self, level, distance):
+        def body(z, step):
+            for mask in self.held(level):
+                mask = mask ^ self.bits[level]
+                self.here(mask, z)
+                for later in range(level + 1, len(self.bits)):
+                    self.cross(later, mask, z, False).start()
+
+        self.at(distance, body)
+
+    def swap_copy(self):
+        mine = self.full.at[:, :, self.c]
+        return remote(mine, mine, self.pair.at[0], self.pair.at[1], {"seq": self.s ^ 1})
+
+    def swap(self):
+        pltpu.make_async_copy(self.shard, self.shard, self.own).wait()
+        self.swap_copy().start()
+
+    def finish(self):
+        self.swap_copy().wait_send()
+        other = self.full.at[:, :, 1 - self.c]
+        pltpu.make_async_copy(other, other, self.pair.at[1]).wait()
+
+        @pl.when(self.z > 0)
+        def _():
+            self.chain(self.z, -1, True).wait_send()
+
+        @pl.when(self.z < self.chips - 1)
+        def _():
+            self.chain(self.z, 1, True).wait_send()
+
+        for distance in range(1, self.chips):
+            def body(z, step):
+                onward = self.z < self.chips - 1 if step > 0 else self.z > 0
+
+                @pl.when(onward)
+                def _():
+                    self.chain(z, step, False).wait_send()
+
+            self.at(distance, body)
+        for level in range(len(self.bits)):
+            sent = self.full.at[pl.ds(0, 2 ** level), :, 0]
+            pltpu.make_async_copy(sent, sent, self.level_send.at[level]).wait()
+
+
+def gather_semaphores(count, groups, chips):
+    dma = pltpu.SemaphoreType.DMA
+    levels = max(len(powers(groups)), 1)
+    return [dma((count, chips, 2)), dma((count, levels)), dma((count, groups, chips)), dma((count, 2)), dma((count,))]
+
+
+def neighbours(groups, n):
+    g, s = lax.axis_index("grp"), lax.axis_index("seq")
+    out = [{"grp": g ^ bit} for bit in powers(groups)]
+    out += [{"seq": s ^ 1}, {"seq": lax.rem(s + 2, n)}, {"seq": lax.rem(s + n - 2, n)}]
+    return out
+
+
+def gather_kernel(groups, chips, orders, *refs):
+    count = len(orders)
+    shards, fulls, sems = refs[:count], refs[count:2 * count], refs[2 * count:]
+    enter(neighbours(groups, 2 * chips))
+    gathers = [Gather(groups, chips, orders[i], shards[i], fulls[i], *[s.at[i] for s in sems]) for i in range(count)]
+    run_gathers(gathers)
+
+
+def run_gathers(gathers):
+    chips, levels = gathers[0].chips, len(gathers[0].bits)
+    for g in gathers:
+        g.begin()
+    for distance in range(chips + levels):
+        for g in gathers:
+            if distance + 1 < chips:
+                g.along(distance + 1)
+            for level in range(levels):
+                if 0 <= distance - level < chips:
+                    g.over(level, distance - level)
+    for g in gathers:
+        g.swap()
+    for g in gathers:
+        g.finish()
+
+
+def gather_call(groups, chips, shards, orders):
+    count = len(shards)
+    return pl.pallas_call(
+        functools.partial(gather_kernel, groups, chips, orders),
+        out_shape=[jax.ShapeDtypeStruct((groups, chips, 2) + x.shape, x.dtype) for x in shards],
+        in_specs=[pl.BlockSpec(memory_space=pl.ANY)] * count,
+        out_specs=[pl.BlockSpec(memory_space=pl.ANY)] * count,
+        scratch_shapes=gather_semaphores(count, groups, chips),
+        compiler_params=pltpu.CompilerParams(collective_id=0, has_side_effects=True),
+        name="gather_parameters",
+    )(*shards)
+
+
 def collect(parts):
-    whole = (
-        lax.all_gather(parts[0], ("grp", "seq"), axis=0, tiled=True),
-        lax.all_gather(parts[1], ("grp", "seq"), axis=0, tiled=True),
-        lax.all_gather(parts[2], ("grp", "seq"), axis=0, tiled=True),
-        lax.all_gather(parts[3], ("grp", "seq"), axis=0, tiled=True),
-        lax.all_gather(parts[4], ("grp", "seq"), axis=0, tiled=True),
-        lax.all_gather(parts[5], ("grp", "seq"), axis=0, tiled=True),
-        lax.all_gather(parts[6], ("grp", "seq"), axis=0, tiled=True),
-        lax.all_gather(parts[7], ("grp", "seq"), axis=0, tiled=True),
-        lax.all_gather(parts[8], ("grp", "seq"), axis=0, tiled=True),
-        lax.all_gather(parts[9], ("grp", "seq"), axis=0, tiled=True),
-        lax.all_gather(parts[10], ("grp", "seq"), axis=0, tiled=True),
-        lax.all_gather(parts[11], ("grp", "seq"), axis=0, tiled=True),
-        lax.all_gather(parts[12], ("grp", "seq"), axis=0, tiled=True),
-        lax.all_gather(parts[13], ("grp", "seq"), axis=0, tiled=True),
-        lax.all_gather(parts[14], ("grp", "seq"), axis=0, tiled=True),
-    )
-    return whole
+    groups = lax.axis_size("grp")
+    n = lax.axis_size("seq")
+    small = (0, 1, 3, 6, 8, 9, 10, 12, 14)
+    packed = jnp.concatenate([parts[i] for i in small])
+    sizes = [parts[i].shape[0] for i in small]
+    length = packed.shape[0]
+    packed = jnp.pad(packed, (0, 2048 - length)).reshape(16, 128)
+    bits = powers(groups)
+    forth, back = bits, bits[::-1]
+    shards = [packed, parts[2], parts[5], parts[4], parts[7], parts[11], parts[13]]
+    fulls = gather_call(groups, n // 2, shards, [forth, forth, forth, back, back, forth, back])
+    flat = fulls[0].reshape(groups * n, 2048)
+    whole = [None] * 15
+    at = 0
+    for i, size in zip(small, sizes):
+        whole[i] = flat[:, at : at + size].reshape(groups * n * size)
+        at += size
+    for i, full in zip((2, 5, 4, 7, 11, 13), fulls[1:]):
+        whole[i] = full.reshape(-1, full.shape[-1])
+    return tuple(whole)
 
 
 def own_piece_of(table, slot):
@@ -297,7 +503,7 @@
     post = post_full.astype(jnp.bfloat16)
     result = middle + matmul(post, whole[13]) + whole[14].astype(jnp.float32)
     layer_output = result.astype(jnp.bfloat16).reshape(groups, rows, width)
-    again = collect(parts)
+    again = whole
     seed = cotangent.reshape(groups * rows, width)
     seed_full = seed.astype(jnp.float32)
     grad_reduce_bias = jnp.sum(seed_full, axis=0)
@@ -313,11 +519,6 @@
     grad_output_bias = jnp.sum(grad_branch.astype(jnp.float32), axis=0)
     grad_output = matmul_left(attended_low, grad_branch)
     grad_attended = matmul_right(grad_branch, again[7]).astype(jnp.bfloat16)
-    full_keys, full_values = (
-        lax.all_gather(keys_local, "seq", axis=1, tiled=True),
-        lax.all_gather(values_local, "seq", axis=1, tiled=True),
-    )
-    gathered_keys, gathered_values = (full_keys, full_values)
     grad_attended_heads = grad_attended.reshape(groups, rows, heads, HEAD)
     attended_heads = attended.reshape(groups, rows, heads, HEAD)
     index = 0

time: 1520 us -> 1400 us (0.921)
  waiting for transfers between devices: 1050 us -> 827 us
  matrix products: 152 us -> 258 us
  blocking collectives: 123 us -> 38.6 us
  Pallas kernels: 0 us -> 76.2 us
    all_gather x5 -> x0, waiting for transfers between devices: 126 us -> none  [the longest x1 57.3 us: collect(): lax.all_gather(parts[13], ('grp', 'seq'), axis=0, tiled=True)]
    reduce_scatter x1, waiting for transfers between devices: 106 us -> 21.3 us  [body(): lax.psum_scatter(value_stack.astype(jnp.bfloat16), 'seq', scatter_dimensi...]
    pallas_call x0 -> x1, Pallas kernels: none -> 76.2 us  [gather_call(): pl.pallas_call(functools.partial(gather_kernel, groups, chips, orders), o...]
    reduce_scatter x1, waiting for transfers between devices: 105 us -> 34.1 us  [body(): lax.psum_scatter(grad_query_weight, ('grp', 'seq'), scatter_dimension=0,...]
    reduce_scatter x1, waiting for transfers between devices: 34.1 us -> 105 us  [body(): lax.psum_scatter(grad_output, ('grp', 'seq'), scatter_dimension=0, tiled=...]
    dot_general x4 -> x10, matrix products: 28.8 us -> 71.9 us  [work(): jnp.einsum('vwa,ewa->wve', query_matrix, key_portion, preferred_element_t...]
    unnamed x2 -> x1, blocking collectives: 81.2 us -> 38.6 us
    all_gather x1 -> x0, blocking collectives: 42.2 us -> none  [collect(): lax.all_gather(parts[5], ('grp', 'seq'), axis=0, tiled=True)]
  transfers between devices with their start and end apart: 15 -> 10, of which waited for: 14 -> 10; matrix products, arithmetic and copies ran while one was open for 11% -> 6% of each run, Pallas kernels for 0% -> 0%
where the time goes in v1:
time: 1400 us; the launch traced here: 1390 us
  waiting for transfers between devices  827 us (59%)
  matrix products  258 us (18%)
  local copies, waits for them, and re-layouts  98.9 us (7%)
  Pallas kernels  76.2 us (5%)
  other arithmetic  56.4 us (4%)
  blocking collectives  38.6 us (3%)
  loops' own time  23 us (2%)
  between operations  16 us (1%)
    reduce_scatter x1, waiting for transfers between devices, body(): lax.psum_scatter(grad_expand, ('grp', 'seq'), scatter_dimension=0, tiled=...  142 us
    reduce_scatter x1, waiting for transfers between devices, body(): lax.psum_scatter(grad_reduce, ('grp', 'seq'), scatter_dimension=0, tiled=...  141 us
    reduce_scatter x1, waiting for transfers between devices, body(): lax.psum_scatter(grad_output, ('grp', 'seq'), scatter_dimension=0, tiled=...  105 us
    reduce_scatter x1, waiting for transfers between devices, body(): lax.psum_scatter(grad_key_weight, ('grp', 'seq'), scatter_dimension=0, ti...  104 us
    unnamed x11, waiting for transfers between devices  101 us
    pallas_call x1, Pallas kernels, gather_call(): pl.pallas_call(functools.partial(gather_kernel, groups, chips, orders), o...  76.2 us
    dot_general x10, matrix products, work(): jnp.einsum('vwa,ewa->wve', query_matrix, key_portion, preferred_element_t...  71.9 us
    reduce_scatter x1, waiting for transfers between devices, body(): lax.psum_scatter(key_stack.astype(jnp.bfloat16), 'seq', scatter_dimension...  67.3 us
  transfers between devices with their start and end apart: 10, of which 10 were waited for; matrix products, arithmetic and copies ran while one was open for 6% of the time, Pallas kernels for 0%

profile of v1, /device:TPU:0, one launch (start us, length us, event | category | flops | bytes accessed | tf_op | source)
XLA Modules:
  0.0 1394.9 jit_solution(2545101243816521615)
XLA Ops:
  11.1 76.2 %gather_parameters.1 = (bf16[4,4,2,16,128]{4,3,2,1,0:T(8,128)(2,1)}, bf16[4,4,2,24,768]{4,3,2,1,0:T(8,128)(2,1)}, bf16[4,4,2,24,384]{4,3,2,1,0:T(8,128)(2,1)}, b...) custom-call(bf16[16,128]{1,0:T(8,128)(2,1)} %pad_bitcast_fusion.refs, ...), custom_call_target="tpu_custom_call" | custom-call | tf_op jit(solution)/shard_map/gather_parameters/pallas_call | solution.py:232
  99.9 55.1 %all-gather.6.cloned.1.call-done = bf16[4096,768]{1,0:T(8,128)(2,1)} async-done(((bf16[512,768]{1,0:T(8,128)(2,1)}), bf16[4096,768]{1,0:T(8,128)(2,1)}) %all-gather.6.cloned.1.call-update) | async-done | bytes 6291472 | tf_op jit(solution)/shard_map/all_gather | solution.py:478
  155.0 9.3 copy.75
  164.3 56.2 %all-gather.4.cloned.1.call-done = bf16[1,4096,768]{1,2,0:T(8,128)(2,1)} async-done(((bf16[1,512,768]{1,2,0:T(8,128)(2,1)}), bf16[1,4096,768]{1,2,0:T(8,128)(2,1)}) %all-gather.4.cloned.1.call-update) | async-done | bytes 6291472 | tf_op jit(solution)/shard_map/all_gather | solution.py:479
  221.9 101.3 %while.35 = (s32[]{:T(128)}, f32[12,512]{1,0:T(8,128)S(1)}, f32[12,512]{1,0:T(8,128)S(1)}, f32[12,512,64]{1,2,0:T(8,128)}, s32[8]{0:T(128)S(1)}, /*index=5*/s32[...) while((s32[]{:T(128)}, f32[12,512]{1,0:T(8,128)S(1)}, ...), condition=%wide.region_10.11_spmd.clone, body=%wide.region_4.10_spmd.clone.sunk | while | flops 847796224 | bytes 59427328 | solution.py:330
  225.3 14.8 %conditional.6 = ((f32[12,512]{1,0:T(8,128)S(1)}, f32[12,512]{1,0:T(8,128)S(1)}, f32[12,512,64]{1,2,0:T(8,128)})) conditional(s32[]{:T(128)} %convert_element_type.419, (f32[12,512]{1,0:T(8,128)S(1)}, f32[12,512]{1,0:T(8,128)S(1)}, f32[12,512,64]{1,2,0:T(8,128)}) %tuple.114, (pred[512]{0:T(512)(128)(4,1)S(1)}, pred[512]{0:T(512)(128)(4,1)S(1)}, ...), branch_computations={%region_6.6_spmd, %region_7.9_spmd.clone} | conditional | flops 847788544 | bytes 58342536 | solution.py:323
  225.7 5.0 fusion.4
  230.7 3.1 fusion.6
  233.9 5.0 multiply_add_fusion
  246.9 14.8 %conditional.6 = ((f32[12,512]{1,0:T(8,128)S(1)}, f32[12,512]{1,0:T(8,128)S(1)}, f32[12,512,64]{1,2,0:T(8,128)})) conditional(s32[]{:T(128)} %convert_element_type.419, (f32[12,512]{1,0:T(8,128)S(1)}, f32[12,512]{1,0:T(8,128)S(1)}, f32[12,512,64]{1,2,0:T(8,128)}) %tuple.114, (pred[512]{0:T(512)(128)(4,1)S(1)}, pred[512]{0:T(512)(128)(4,1)S(1)}, ...), branch_computations={%region_6.6_spmd, %region_7.9_spmd.clone} | conditional | flops 847788544 | bytes 58342536 | solution.py:323
  247.3 5.0 fusion.4
  255.6 5.0 multiply_add_fusion
  268.6 14.8 %conditional.6 = ((f32[12,512]{1,0:T(8,128)S(1)}, f32[12,512]{1,0:T(8,128)S(1)}, f32[12,512,64]{1,2,0:T(8,128)})) conditional(s32[]{:T(128)} %convert_element_type.419, (f32[12,512]{1,0:T(8,128)S(1)}, f32[12,512]{1,0:T(8,128)S(1)}, f32[12,512,64]{1,2,0:T(8,128)}) %tuple.114, (pred[512]{0:T(512)(128)(4,1)S(1)}, pred[512]{0:T(512)(128)(4,1)S(1)}, ...), branch_computations={%region_6.6_spmd, %region_7.9_spmd.clone} | conditional | flops 847788544 | bytes 58342536 | solution.py:323
  269.0 5.0 fusion.4
  277.2 5.0 multiply_add_fusion
  290.3 14.8 %conditional.6 = ((f32[12,512]{1,0:T(8,128)S(1)}, f32[12,512]{1,0:T(8,128)S(1)}, f32[12,512,64]{1,2,0:T(8,128)})) conditional(s32[]{:T(128)} %convert_element_type.419, (f32[12,512]{1,0:T(8,128)S(1)}, f32[12,512]{1,0:T(8,128)S(1)}, f32[12,512,64]{1,2,0:T(8,128)}) %tuple.114, (pred[512]{0:T(512)(128)(4,1)S(1)}, pred[512]{0:T(512)(128)(4,1)S(1)}, ...), branch_computations={%region_6.6_spmd, %region_7.9_spmd.clone} | conditional | flops 847788544 | bytes 58342536 | solution.py:323
  290.7 5.0 fusion.4
  298.9 5.0 multiply_add_fusion
  308.5 14.7 %conditional.6 = ((f32[12,512]{1,0:T(8,128)S(1)}, f32[12,512]{1,0:T(8,128)S(1)}, f32[12,512,64]{1,2,0:T(8,128)})) conditional(s32[]{:T(128)} %convert_element_type.419, (f32[12,512]{1,0:T(8,128)S(1)}, f32[12,512]{1,0:T(8,128)S(1)}, f32[12,512,64]{1,2,0:T(8,128)}) %tuple.114, (pred[512]{0:T(512)(128)(4,1)S(1)}, pred[512]{0:T(512)(128)(4,1)S(1)}, ...), branch_computations={%region_6.6_spmd, %region_7.9_spmd.clone} | conditional | flops 847788544 | bytes 58342536 | solution.py:323
  308.9 4.9 fusion.4
  317.0 4.9 multiply_add_fusion
  326.3 5.5 fusion.88
  331.9 7.1 convert_reduce_fusion
  339.0 3.5 multiply_reduce_fusion
  352.2 180.3 %while.36 = (s32[]{:T(128)}, f32[512,12,64]{0,2,1:T(8,128)}, bf16[8,512,12,64]{1,3,2,0:T(8,128)(2,1)}, bf16[8,512,12,64]{1,3,2,0:T(8,128)(2,1)}, s32[8]{0:T(128)...) while((s32[]{:T(128)}, f32[512,12,64]{0,2,1:T(8,128)}, ...), condition=%wide.region_20.21_spmd.clone, body=%wide.region_16.20_spmd.clone.sunk | while | flops 2047092736 | bytes 88730152 | solution.py:410
  355.6 28.3 %conditional.7 = (f32[512,12,64]{0,2,1:T(8,128)}, bf16[1,512,12,64]{1,3,2,0:T(8,128)(2,1)S(1)}, bf16[1,512,12,64]{1,3,2,0:T(8,128)(2,1)S(1)}) conditional(s32[]{:T(128)} %convert_element_type.420, f32[512,12,64]{0,2,1:T(8,128)} %get-tuple-element.970, (s32[]{:T(128)}, bf16[4096,12,64]{0,2,1:T(8,128)(2,1)}, pred[512]{0:T(512)(128)(4,1)S(1)}, ...), branch_computations={%region_18.18_spmd, %region_19.19_spmd.clone} | conditional | flops 2047085056 | bytes 84499616 | solution.py:407
  356.1 9.4 fusion.31
  365.5 7.7 fusion.21
  373.2 6.2 fusion.26
  393.6 28.3 %conditional.7 = (f32[512,12,64]{0,2,1:T(8,128)}, bf16[1,512,12,64]{1,3,2,0:T(8,128)(2,1)S(1)}, bf16[1,512,12,64]{1,3,2,0:T(8,128)(2,1)S(1)}) conditional(s32[]{:T(128)} %convert_element_type.420, f32[512,12,64]{0,2,1:T(8,128)} %get-tuple-element.970, (s32[]{:T(128)}, bf16[4096,12,64]{0,2,1:T(8,128)(2,1)}, pred[512]{0:T(512)(128)(4,1)S(1)}, ...), branch_computations={%region_18.18_spmd, %region_19.19_spmd.clone} | conditional | flops 2047085056 | bytes 84499616 | solution.py:407
  394.0 9.4 fusion.31
  403.4 7.7 fusion.21
  411.2 6.2 fusion.26
  431.6 28.3 %conditional.7 = (f32[512,12,64]{0,2,1:T(8,128)}, bf16[1,512,12,64]{1,3,2,0:T(8,128)(2,1)S(1)}, bf16[1,512,12,64]{1,3,2,0:T(8,128)(2,1)S(1)}) conditional(s32[]{:T(128)} %convert_element_type.420, f32[512,12,64]{0,2,1:T(8,128)} %get-tuple-element.970, (s32[]{:T(128)}, bf16[4096,12,64]{0,2,1:T(8,128)(2,1)}, pred[512]{0:T(512)(128)(4,1)S(1)}, ...), branch_computations={%region_18.18_spmd, %region_19.19_spmd.clone} | conditional | flops 2047085056 | bytes 84499616 | solution.py:407
  432.0 9.4 fusion.31
  441.4 7.7 fusion.21
  449.1 6.2 fusion.26
  469.6 28.3 %conditional.7 = (f32[512,12,64]{0,2,1:T(8,128)}, bf16[1,512,12,64]{1,3,2,0:T(8,128)(2,1)S(1)}, bf16[1,512,12,64]{1,3,2,0:T(8,128)(2,1)S(1)}) conditional(s32[]{:T(128)} %convert_element_type.420, f32[512,12,64]{0,2,1:T(8,128)} %get-tuple-element.970, (s32[]{:T(128)}, bf16[4096,12,64]{0,2,1:T(8,128)(2,1)}, pred[512]{0:T(512)(128)(4,1)S(1)}, ...), branch_computations={%region_18.18_spmd, %region_19.19_spmd.clone} | conditional | flops 2047085056 | bytes 84499616 | solution.py:407
  470.1 9.4 fusion.31
  479.5 7.7 fusion.21
  487.2 6.2 fusion.26
  502.7 28.2 %conditional.7 = (f32[512,12,64]{0,2,1:T(8,128)}, bf16[1,512,12,64]{1,3,2,0:T(8,128)(2,1)S(1)}, bf16[1,512,12,64]{1,3,2,0:T(8,128)(2,1)S(1)}) conditional(s32[]{:T(128)} %convert_element_type.420, f32[512,12,64]{0,2,1:T(8,128)} %get-tuple-element.970, (s32[]{:T(128)}, bf16[4096,12,64]{0,2,1:T(8,128)(2,1)}, pred[512]{0:T(512)(128)(4,1)S(1)}, ...), branch_computations={%region_18.18_spmd, %region_19.19_spmd.clone} | conditional | flops 2047085056 | bytes 84499616 | solution.py:407
  503.1 9.3 fusion.31
  512.4 7.7 fusion.21
  520.1 6.2 fusion.26
  532.5 9.6 copy.80
  542.1 10.5 convert_element_type.280
  552.6 9.5 copy.79
  562.2 10.4 convert_element_type.277
  581.5 10.0 fusion.74
  593.0 7.2 fusion.87
  600.3 21.3 %reduce-scatter.13.cloned.1.call-done = bf16[1,512,768]{1,2,0:T(8,128)(2,1)} async-done(((bf16[1,4096,768]{1,2,0:T(8,128)(2,1)}), bf16[1,512,768]{1,2,0:T(8,128)(2,1)}) %reduce-scatter.13.cloned.1.call-update) | async-done | bytes 786448 | tf_op jit(solution)/shard_map/reduce_scatter | solution.py:548
  624.6 67.3 %reduce-scatter.11.cloned.1.call-done = bf16[1,512,768]{1,2,0:T(8,128)(2,1)} async-done(((bf16[1,4096,768]{1,2,0:T(8,128)(2,1)}), bf16[1,512,768]{1,2,0:T(8,128)(2,1)}) %reduce-scatter.11.cloned.1.call-update) | async-done | bytes 786448 | tf_op jit(solution)/shard_map/reduce_scatter | solution.py:545
  691.9 3.6 fusion.70
  695.5 3.5 fusion.100
  699.1 9.1 fusion.65
  714.1 38.6 %all-reduce.11 = (f32[768]{0:T(1024)S(1)}, f32[768]{0:T(1024)S(1)}, f32[768]{0:T(1024)S(1)}, f32[384]{0:T(512)S(1)}, f32[768]{0:T(1024)S(1)}, /*index=5*/f32[768...) all-reduce(f32[768]{0:T(1024)S(1)} %get-tuple-element.618, ...), channel_id=5, replica_groups=mesh['grp'=4,'seq'=8] {'grp','seq'}, use_global_device_ids=true, to_apply=%region_26.27.clone | all-reduce | flops 8832 | bytes 70656
  758.0 3.2 add_bitcast_fusion
  761.2 34.1 %reduce-scatter.15.cloned.1.call-done = f32[24,768]{1,0:T(8,128)} async-done(((f32[768,768]{1,0:T(8,128)}), f32[24,768]{1,0:T(8,128)}) %reduce-scatter.15.cloned.1.call-update) | async-done | bytes 73744 | tf_op jit(solution)/shard_map/reduce_scatter | solution.py:573
  795.3 104.6 %reduce-scatter.19.cloned.1.call-done = f32[24,768]{1,0:T(8,128)} async-done(((f32[768,768]{1,0:T(8,128)}), f32[24,768]{1,0:T(8,128)}) %reduce-scatter.19.cloned.1.call-update) | async-done | bytes 73744 | tf_op jit(solution)/shard_map/reduce_scatter | solution.py:578
  900.0 141.2 %reduce-scatter.23.cloned.1.call-done = f32[96,768]{1,0:T(8,128)} async-done(((f32[3072,768]{1,0:T(8,128)}), f32[96,768]{1,0:T(8,128)}) %reduce-scatter.23.cloned.1.call-update) | async-done | bytes 294928 | tf_op jit(solution)/shard_map/reduce_scatter | solution.py:584
  1041.2 142.1 %reduce-scatter.21.cloned.1.call-done = f32[24,3072]{1,0:T(8,128)} async-done(((f32[768,3072]{1,0:T(8,128)}), f32[24,3072]{1,0:T(8,128)}) %reduce-scatter.21.cloned.1.call-update) | async-done | bytes 294928 | tf_op jit(solution)/shard_map/reduce_scatter | solution.py:582
  1183.3 100.8 %reduce-scatter.25.cloned.1.call-done = f32[24,384]{1,0:T(8,128)} async-done(((f32[768,384]{1,0:T(8,128)}), f32[24,384]{1,0:T(8,128)}) %reduce-scatter.25.cloned.1.call-update) | async-done | bytes 36880
  1284.1 103.8 %reduce-scatter.17.cloned.1.call-done = f32[24,768]{1,0:T(8,128)} async-done(((f32[768,768]{1,0:T(8,128)}), f32[24,768]{1,0:T(8,128)}) %reduce-scatter.17.cloned.1.call-update) | async-done | bytes 73744 | tf_op jit(solution)/shard_map/reduce_scatter | solution.py:575
  (418 shorter events, 143.6 us)
Async XLA Ops:
  7.2 81.9 %copy-start.3 = (bf16[1,512,768]{2,1,0:T(8,128)(2,1)S(1)}, bf16[1,512,768]{2,1,0:T(8,128)(2,1)}, u32[]{:S(2)}) copy-start(bf16[1,512,768]{2,1,0:T(8,128)(2,1)} %param.27) | copy-start | bytes 2359300
  7.2 3.0 copy-start.60
  7.2 3.0 copy-start.59
  7.2 3.0 copy-start.58
  7.2 3.0 copy-start.57
  7.2 3.0 copy-start.56
  7.3 3.0 copy-start.55
  7.3 3.0 copy-start.54
  7.3 3.0 copy-start.53
  7.3 3.0 copy-start.52
  7.3 147.7 %all-gather.6.cloned.1.call-start = ((), (), s32[]{:S(2)}) async-start(), calls=%async_computation.16 | async-start | bytes 7077888 | tf_op jit(solution)/shard_map/all_gather | solution.py:478
  8.7 86.8 %copy-start.28 = (f32[512]{0:T(512)}, f32[512]{0:T(512)S(1)}, u32[]{:S(2)}) copy-start(f32[512]{0:T(512)S(1)} %broadcast_multiply_fusion.1) | copy-start | bytes 6148
  10.2 82.0 %copy-start.36 = (f32[512]{0:T(512)}, f32[512]{0:T(512)S(1)}, u32[]{:S(2)}) copy-start(f32[512]{0:T(512)S(1)} %fusion.55) | copy-start | bytes 6148
  10.3 85.2 %copy-start.30 = (f32[512]{0:T(512)}, f32[512]{0:T(512)S(1)}, u32[]{:S(2)}) copy-start(f32[512]{0:T(512)S(1)} %fusion.83) | copy-start | bytes 6148
  89.0 6.6 copy-start.26
  89.1 6.5 copy-start.45
  89.1 3.2 copy-start.24
  92.3 128.3 %all-gather.4.cloned.1.call-start = ((), (), s32[]{:S(2)}) async-start(), calls=%async_computation.8 | async-start | bytes 7077888 | tf_op jit(solution)/shard_map/all_gather | solution.py:479
  95.0 526.6 %reduce-scatter.13.cloned.1.call-start = ((), (), s32[]{:S(2)}) async-start(), calls=%async_computation.10 | async-start | bytes 7077888 | tf_op jit(solution)/shard_map/reduce_scatter | solution.py:548
  95.3 247.3 %copy-start.40 = (f32[768]{0:T(1024)}, f32[768]{0:T(1024)S(1)}, u32[]{:S(2)}) copy-start(f32[768]{0:T(1024)S(1)} %reshape.460) | copy-start | bytes 9220
  95.4 230.9 %copy-start.47 = (f32[768]{0:T(1024)}, f32[768]{0:T(1024)S(1)}, u32[]{:S(2)}) copy-start(f32[768]{0:T(1024)S(1)} %reshape.461) | copy-start | bytes 9220
  230.7 3.2 copy-start.5
  252.4 3.2 copy-start.5
  274.0 3.2 copy-start.5
  295.7 3.2 copy-start.5
  313.8 3.2 copy-start.5
  324.9 6.9 slice-start
  325.9 16.7 %copy-start.9 = (f32[512,768]{1,0:T(8,128)}, f32[512,768]{1,0:T(8,128)S(1)}, u32[]{:S(2)}) copy-start(f32[512,768]{1,0:T(8,128)S(1)} %get-tuple-element.709) | copy-start | bytes 4718596
  325.9 16.7 %copy-start.34 = (f32[512]{0:T(512)}, f32[512]{0:T(512)S(1)}, u32[]{:S(2)}) copy-start(f32[512]{0:T(512)S(1)} %broadcast_multiply_fusion) | copy-start | bytes 6148
  326.2 16.3 %copy-start.43 = (f32[512]{0:T(512)}, f32[512]{0:T(512)S(1)}, u32[]{:S(2)}) copy-start(f32[512]{0:T(512)S(1)} %fusion.84) | copy-start | bytes 6148
  326.2 5.6 copy-start.11
  326.2 5.6 slice-start.1
  326.2 12.8 slice-start.2
  331.8 7.2 copy-start.62
  331.9 7.1 slice-start.3
  339.0 3.5 copy-start.63
  356.1 9.4 copy-start.15
  373.2 6.2 copy-start
  394.0 9.4 copy-start.15
  411.1 6.2 copy-start
  432.0 9.4 copy-start.15
  449.1 6.2 copy-start
  470.1 9.4 copy-start.15
  487.2 6.2 copy-start
  503.1 9.3 copy-start.15
  520.1 6.2 copy-start
  552.6 139.3 %reduce-scatter.11.cloned.1.call-start = ((), (), s32[]{:S(2)}) async-start(), calls=%async_computation.9 | async-start | bytes 7077888 | tf_op jit(solution)/shard_map/reduce_scatter | solution.py:545
  572.6 2.5 copy-start.4
  572.6 2.5 copy-start.27
  572.7 2.5 copy-start.29
  572.7 2.5 copy-start.31
  572.7 2.5 copy-start.46
  572.7 222.6 %reduce-scatter.15.cloned.1.call-start = ((), (), s32[]{:S(2)}) async-start(), calls=%async_computation.11 | async-start | bytes 2433024 | tf_op jit(solution)/shard_map/reduce_scatter | solution.py:573
  577.7 322.2 %reduce-scatter.19.cloned.1.call-start = ((), (), s32[]{:S(2)}) async-start(), calls=%async_computation.13 | async-start | bytes 2433024 | tf_op jit(solution)/shard_map/reduce_scatter | solution.py:578
  581.3 459.9 %reduce-scatter.23.cloned.1.call-start = ((), (), s32[]{:S(2)}) async-start(), calls=%async_computation.15 | async-start | bytes 9732096 | tf_op jit(solution)/shard_map/reduce_scatter | solution.py:584
  591.6 591.7 %reduce-scatter.21.cloned.1.call-start = ((), (), s32[]{:S(2)}) async-start(), calls=%async_computation.14 | async-start | bytes 9732096 | tf_op jit(solution)/shard_map/reduce_scatter | solution.py:582
  600.2 24.3 %copy-start.25 = (f32[32,24]{1,0:T(8,128)S(1)}, f32[32,24]{1,0:T(8,128)}, u32[]{:S(2)}) copy-start(f32[32,24]{1,0:T(8,128)} %get-tuple-element.702) | copy-start | bytes 9220
  600.2 683.9 %reduce-scatter.25.cloned.1.call-start = ((), (), s32[]{:S(2)}) async-start(), calls=%async_computation.17 | async-start | bytes 1216512
  624.5 763.4 %reduce-scatter.17.cloned.1.call-start = ((), (), s32[]{:S(2)}) async-start(), calls=%async_computation.12 | async-start | bytes 2433024 | tf_op jit(solution)/shard_map/reduce_scatter | solution.py:575
  699.1 9.1 copy-start.12
  709.6 2.6 copy-start.14
  709.6 2.6 copy-start.20
  709.7 2.6 copy-start.23
  713.2 44.8 %copy-start.33 = (f32[512]{0:T(512)S(1)}, f32[512]{0:T(512)}, u32[]{:S(2)}) copy-start(f32[512]{0:T(512)} %copy-done.32) | copy-start | bytes 6148
  (34 other events, 44.7 us)
Sparse Core Ops, SparseCore 0:
  92.4 62.6 all-gather.5
  157.2 63.2 all-gather.3
  552.7 68.8 reduce-scatter.12
  623.7 68.1 reduce-scatter.10
  697.6 97.6 reduce-scatter.14
  801.9 98.0 reduce-scatter.18
  906.4 134.6 reduce-scatter.22
  1048.7 134.5 reduce-scatter.20
  1188.9 95.1 reduce-scatter.24
  1289.8 98.0 reduce-scatter.16

commit v2 on v1

v2 whole, which is shorter than its diff:
```python
import functools

import jax
import jax.numpy as jnp
from jax import lax
from jax.experimental import pallas as pl
from jax.experimental.pallas import tpu as pltpu
from jax.sharding import PartitionSpec as P

MESH = pl.DeviceIdType.MESH


def powers(count):
    out, bit = [], 1
    while bit < count:
        out.append(bit)
        bit *= 2
    return out


def remote(src, dst, send, recv, device):
    return pltpu.make_async_remote_copy(
        src_ref=src, dst_ref=dst, send_sem=send, recv_sem=recv,
        device_id=device, device_id_type=MESH,
    )


def enter(devices):
    barrier = pltpu.get_barrier_semaphore()
    for device in devices:
        pl.semaphore_signal(barrier, inc=1, device_id=device, device_id_type=MESH)
    pl.semaphore_wait(barrier, len(devices))


class Gather:
    def __init__(self, groups, chips, bits, shard, full, chain_send, level_send, recv, pair, own):
        self.groups, self.chips, self.bits = groups, chips, bits
        self.shard, self.full = shard, full
        self.chain_send, self.level_send, self.recv, self.pair, self.own = chain_send, level_send, recv, pair, own
        self.g = lax.axis_index("grp")
        seq = lax.axis_index("seq")
        self.s, self.z, self.c = seq, seq // 2, seq % 2

    def block(self, g, z, c):
        return self.full.at[g, z, c]

    def source(self, mask, z, first):
        return self.shard if first else self.block(self.g ^ mask, z, self.c)

    def chain(self, z, step, first):
        side = 0 if step < 0 else 1
        return remote(self.source(0, z, first), self.block(self.g, z, self.c),
                      self.chain_send.at[z, side], self.recv.at[self.g, z],
                      {"seq": self.s + 2 * step})

    def cross(self, level, mask, z, first):
        g = self.g ^ mask
        return remote(self.source(mask, z, first), self.block(g, z, self.c),
                      self.level_send.at[level], self.recv.at[g, z],
                      {"grp": self.g ^ self.bits[level]})

    def held(self, level):
        masks = [0]
        for bit in self.bits[:level]:
            masks = masks + [m ^ bit for m in masks]
        return masks

    def here(self, mask, z):
        g = self.g ^ mask
        pltpu.make_async_copy(self.block(g, z, self.c), self.block(g, z, self.c), self.recv.at[g, z]).wait()

    def begin(self):
        copy = pltpu.make_async_copy(self.shard, self.block(self.g, self.z, self.c), self.own)
        copy.start()

        @pl.when(self.z > 0)
        def _():
            self.chain(self.z, -1, True).start()

        @pl.when(self.z < self.chips - 1)
        def _():
            self.chain(self.z, 1, True).start()

        for level in range(len(self.bits)):
            self.cross(level, 0, self.z, True).start()

    def at(self, distance, body):
        if distance == 0:
            body(self.z, 0)
            return

        @pl.when(self.z >= distance)
        def _():
            body(self.z - distance, 1)

        @pl.when(self.z + distance < self.chips)
        def _():
            body(self.z + distance, -1)

    def along(self, distance):
        def body(z, step):
            self.here(0, z)
            onward = self.z < self.chips - 1 if step > 0 else self.z > 0

            @pl.when(onward)
            def _():
                self.chain(z, step, False).start()

            for level in range(len(self.bits)):
                self.cross(level, 0, z, False).start()

        if distance > 0:
            self.at(distance, body)

    def over(self, level, distance):
        def body(z, step):
            for mask in self.held(level):
                mask = mask ^ self.bits[level]
                self.here(mask, z)
                for later in range(level + 1, len(self.bits)):
                    self.cross(later, mask, z, False).start()

        self.at(distance, body)

    def swap_copy(self):
        mine = self.full.at[:, :, self.c]
        return remote(mine, mine, self.pair.at[0], self.pair.at[1], {"seq": self.s ^ 1})

    def swap(self):
        pltpu.make_async_copy(self.shard, self.shard, self.own).wait()
        self.swap_copy().start()

    def finish(self):
        self.swap_copy().wait_send()
        other = self.full.at[:, :, 1 - self.c]
        pltpu.make_async_copy(other, other, self.pair.at[1]).wait()

        @pl.when(self.z > 0)
        def _():
            self.chain(self.z, -1, True).wait_send()

        @pl.when(self.z < self.chips - 1)
        def _():
            self.chain(self.z, 1, True).wait_send()

        for distance in range(1, self.chips):
            def body(z, step):
                onward = self.z < self.chips - 1 if step > 0 else self.z > 0

                @pl.when(onward)
                def _():
                    self.chain(z, step, False).wait_send()

            self.at(distance, body)
        for level in range(len(self.bits)):
            sent = self.full.at[pl.ds(0, 2 ** level), :, 0]
            pltpu.make_async_copy(sent, sent, self.level_send.at[level]).wait()


def gather_semaphores(count, groups, chips):
    dma = pltpu.SemaphoreType.DMA
    levels = max(len(powers(groups)), 1)
    return [dma((count, chips, 2)), dma((count, levels)), dma((count, groups, chips)), dma((count, 2)), dma((count,))]


def neighbours(groups, n):
    g, s = lax.axis_index("grp"), lax.axis_index("seq")
    out = [{"grp": g ^ bit} for bit in powers(groups)]
    out += [{"seq": s ^ 1}, {"seq": lax.rem(s + 2, n)}, {"seq": lax.rem(s + n - 2, n)}]
    return out


def gather_kernel(groups, chips, orders, *refs):
    count = len(orders)
    shards, fulls, sems = refs[:count], refs[count:2 * count], refs[2 * count:]
    enter(neighbours(groups, 2 * chips))
    gathers = [Gather(groups, chips, orders[i], shards[i], fulls[i], *[s.at[i] for s in sems]) for i in range(count)]
    run_gathers(gathers)


def run_gathers(gathers):
    chips, levels = gathers[0].chips, len(gathers[0].bits)
    for g in gathers:
        g.begin()
    for distance in range(chips + levels):
        for g in gathers:
            if distance + 1 < chips:
                g.along(distance + 1)
            for level in range(levels):
                if 0 <= distance - level < chips:
                    g.over(level, distance - level)
    for g in gathers:
        g.swap()
    for g in gathers:
        g.finish()


def gather_call(groups, chips, shards, orders):
    count = len(shards)
    return pl.pallas_call(
        functools.partial(gather_kernel, groups, chips, orders),
        out_shape=[jax.ShapeDtypeStruct((groups, chips, 2) + x.shape, x.dtype) for x in shards],
        in_specs=[pl.BlockSpec(memory_space=pl.ANY)] * count,
        out_specs=[pl.BlockSpec(memory_space=pl.ANY)] * count,
        scratch_shapes=gather_semaphores(count, groups, chips),
        compiler_params=pltpu.CompilerParams(collective_id=0, has_side_effects=True),
        name="gather_parameters",
    )(*shards)


class Reduce:
    def __init__(self, groups, chips, bits, partial, shard, own, landed, halves, left, right, sems):
        self.groups, self.chips, self.bits = groups, chips, bits
        self.partial, self.shard, self.own, self.landed = partial, shard, own, landed
        self.halves, self.left, self.right = halves, left, right
        self.load, self.pair, self.level_send, self.level_recv, self.chain_send, self.chain_recv = sems
        self.g = lax.axis_index("grp")
        self.s = lax.axis_index("seq")
        self.z, self.c = self.s // 2, self.s % 2

    def masks(self, level):
        out = [0]
        for bit in self.bits[level:]:
            out = out + [m ^ bit for m in out]
        return out

    def load_copy(self):
        return pltpu.make_async_copy(self.partial.at[:, :, self.c], self.own, self.load.at[0])

    def pair_copy(self):
        return remote(self.partial.at[:, :, 1 - self.c], self.landed, self.pair.at[0], self.pair.at[1],
                      {"seq": self.s ^ 1})

    def begin(self):
        self.pair_copy().start()
        self.load_copy().start()

    def paired(self):
        self.load_copy().wait()
        self.pair_copy().wait_recv()

        @pl.loop(0, self.groups)
        def _(g):
            self.own[g] = self.add(self.own[g], self.landed[g])

        self.cross_start(0)

    def add(self, a, b):
        return (a.astype(jnp.float32) + b.astype(jnp.float32)).astype(a.dtype)

    def cross_copies(self, level):
        bit = self.bits[level]
        out = []
        for where, mask in enumerate(self.masks(level + 1)):
            out.append(remote(self.own.at[self.g ^ bit ^ mask], self.halves[level].at[where],
                              self.level_send.at[level, where], self.level_recv.at[level, where],
                              {"grp": self.g ^ bit}))
        return out

    def cross_start(self, level):
        if level < len(self.bits):
            for copy in self.cross_copies(level):
                copy.start()
        else:
            self.chain_first()

    def crossed(self, level):
        copies = self.cross_copies(level)
        for where, mask in enumerate(self.masks(level + 1)):
            copies[where].wait_recv()
            g = self.g ^ mask
            self.own[g] = self.add(self.own[g], self.halves[level][where])
        self.cross_start(level + 1)

    def chain_copy(self, block, step):
        side = 0 if step < 0 else 1
        return remote(self.own.at[self.g, block], (self.right if step < 0 else self.left).at[block],
                      self.chain_send.at[block], self.chain_recv.at[1 - side, block],
                      {"seq": self.s + 2 * step})

    def chain_wait(self, block, side):
        landed = (self.left if side == 0 else self.right).at[block]
        pltpu.make_async_copy(landed, landed, self.chain_recv.at[side, block]).wait()

    def chain_first(self):
        last = self.chips - 1

        @pl.when(self.z == 0)
        def _():
            for block in range(last, 0, -1):
                self.chain_copy(block, 1).start()

        @pl.when(self.z == last)
        def _():
            for block in range(last):
                self.chain_copy(block, -1).start()

    def chained(self, k):
        last = self.chips - 1
        block = last - k

        @pl.when((self.z > 0) & (self.z < block))
        def _():
            self.chain_wait(block, 0)
            self.own[self.g, block] = self.add(self.own[self.g, block], self.left[block])
            self.chain_copy(block, 1).start()

        @pl.when((self.z < last) & (self.z > k))
        def _():
            self.chain_wait(k, 1)
            self.own[self.g, k] = self.add(self.own[self.g, k], self.right[k])
            self.chain_copy(k, -1).start()

    def finish(self):
        last = self.chips - 1
        self.shard[...] = self.own[self.g, self.z].astype(jnp.float32)

        @pl.when(self.z > 0)
        def _():
            self.chain_wait(self.z, 0)
            self.shard[...] = self.shard[...] + self.left[self.z].astype(jnp.float32)

        @pl.when(self.z < last)
        def _():
            self.chain_wait(self.z, 1)
            self.shard[...] = self.shard[...] + self.right[self.z].astype(jnp.float32)

    def drain(self):
        self.pair_copy().wait_send()
        for level in range(len(self.bits)):
            for copy in self.cross_copies(level):
                copy.wait_send()
        for block in range(self.chips):
            @pl.when(self.z < block)
            def _():
                self.chain_copy(block, 1).wait_send()

            @pl.when(self.z > block)
            def _():
                self.chain_copy(block, -1).wait_send()


def reduce_steps(reduces):
    chips, levels = reduces[0].chips, len(reduces[0].bits)
    stages = [lambda r: r.begin(), lambda r: r.paired()]
    for level in range(levels):
        stages.append(lambda r, level=level: r.crossed(level))
    for k in range(chips - 1):
        stages.append(lambda r, k=k: r.chained(k))
    stages.append(lambda r: r.finish())
    stages.append(lambda r: r.drain())
    out = []
    for time in range(len(stages) + len(reduces) - 1):
        for i, r in enumerate(reduces):
            if 0 <= time - i < len(stages):
                out.append(functools.partial(stages[time - i], r))
    return out


def reduce_scratch(groups, chips, shapes):
    vmem, dma = pltpu.VMEM, pltpu.SemaphoreType.DMA
    levels = len(powers(groups))
    out = []
    for _, _, _, rows, cols, dtype in shapes:
        out += [vmem((groups, chips, rows, cols), dtype), vmem((groups, chips, rows, cols), dtype)]
        out += [vmem((groups >> (level + 1), chips, rows, cols), dtype) for level in range(levels)]
        out += [vmem((chips, rows, cols), dtype)] * 2
        out += [dma((1,)), dma((2,)), dma((max(levels, 1), max(groups // 2, 1))),
                dma((max(levels, 1), max(groups // 2, 1))), dma((chips,)), dma((2, chips))]
    return out


def make_reduces(groups, chips, orders, partials, shards, scratch):
    levels = len(powers(groups))
    each = 2 + levels + 2 + 6
    out = []
    for i, (partial, shard) in enumerate(zip(partials, shards)):
        refs = scratch[i * each : (i + 1) * each]
        out.append(Reduce(groups, chips, orders[i], partial, shard, refs[0], refs[1], refs[2 : 2 + levels],
                          refs[2 + levels], refs[3 + levels], refs[4 + levels :]))
    return out


def reduce_kernel(groups, chips, orders, *refs):
    count = len(orders)
    enter(neighbours(groups, 2 * chips))
    for step in reduce_steps(make_reduces(groups, chips, orders, refs[:count], refs[count : 2 * count],
                                          refs[2 * count :])):
        step()


def reduce_call(groups, chips, partials, orders):
    count = len(partials)
    shapes = [p.shape + (p.dtype,) for p in partials]
    return pl.pallas_call(
        functools.partial(reduce_kernel, groups, chips, orders),
        out_shape=[jax.ShapeDtypeStruct(p.shape[3:], jnp.float32) for p in partials],
        in_specs=[pl.BlockSpec(memory_space=pl.ANY)] * count,
        out_specs=[pl.BlockSpec(memory_space=pltpu.VMEM)] * count,
        scratch_shapes=reduce_scratch(groups, chips, shapes),
        compiler_params=pltpu.CompilerParams(collective_id=3, has_side_effects=True, vmem_limit_bytes=64000000),
        name="reduce_gradients",
    )(*partials)


PARTS = 4
NEG = -1e30
EPS = 1e-05


def lanes(shape):
    return lax.broadcasted_iota(jnp.int32, shape, len(shape) - 1)


def swap_lanes(v):
    return pltpu.roll(v, 64, 1)


def fold(v, high):
    half = v.shape[0] // 2
    top, bottom = v[:half], v[half:]
    low = lanes(top.shape) < 64
    if high:
        return jnp.where(low, swap_lanes(top), bottom)
    return jnp.where(low, top, swap_lanes(bottom))


def unfold(v, high):
    low = lanes(v.shape) < 64
    zero = jnp.zeros_like(v)
    if high:
        return jnp.concatenate([jnp.where(low, zero, swap_lanes(v)), jnp.where(low, zero, v)], axis=0)
    return jnp.concatenate([jnp.where(low, v, zero), jnp.where(low, swap_lanes(v), zero)], axis=0)


def product(a, b):
    return lax.dot_general(a, b, (((1,), (0,)), ((), ())), preferred_element_type=jnp.float32)


def product_right(a, b):
    return lax.dot_general(a, b, (((1,), (1,)), ((), ())), preferred_element_type=jnp.float32)


def product_left(a, b):
    return lax.dot_general(a, b, (((0,), (0,)), ((), ())), preferred_element_type=jnp.float32)


def normal_rows(v):
    mean = jnp.mean(v, axis=-1, keepdims=True)
    centred = v - mean
    var = jnp.mean(centred * centred, axis=-1, keepdims=True)
    scale = lax.rsqrt(var + EPS)
    return centred * scale, scale


def pack_heads(v, splits, store):
    size = v.shape[0] // splits
    for tile in range(v.shape[1] // 128):
        for split in range(splits):
            part = v[split * size : (split + 1) * size, tile * 128 : (tile + 1) * 128]
            store(2 * tile, split, fold(part, False))
            store(2 * tile + 1, split, fold(part, True))


def slots_of(table, count):
    out = []
    for piece in range(count):
        slot = jnp.int32(0)
        for place in range(count):
            slot = slot + jnp.where(table[0, place] == piece, place, 0)
        out.append(jnp.minimum(slot, count - 1))
    return out


def pick(values, index):
    out = values[0]
    for i in range(1, len(values)):
        out = jnp.where(index == i, values[i], out)
    return out


class Exchange:
    def __init__(self, n):
        self.n = n
        self.splits = n // PARTS
        self.s = lax.axis_index("seq")
        self.part, self.split = self.s // self.splits, lax.rem(self.s, self.splits)

    def peers(self):
        return [{"seq": lax.rem(self.s + off, self.n)} for off in range(1, self.n)]

    def other(self, off):
        return lax.rem(self.s + off, self.n)

    def scatter(self, j, staged, landed, send, recv):
        out = []
        for off in range(1, self.n):
            t = self.other(off)
            out.append(remote(staged.at[t // self.splits, j, lax.rem(t, self.splits)], landed.at[j, self.s],
                              send.at[j, off - 1], recv.at[j, self.s], {"seq": t}))
        return out

    def own(self, j, staged, landed, recv):
        return pltpu.make_async_copy(staged.at[self.part, j, self.split], landed.at[j, self.s], recv.at[j, self.s])

    def spread(self, j, staged, landed, send, recv):
        out = []
        for off in range(1, PARTS):
            part = lax.rem(self.part + off, PARTS)
            out.append(remote(staged.at[part, j], landed.at[j, self.s], send.at[j, off - 1],
                              recv.at[j, self.s], {"seq": part * self.splits + self.split}))
        return out

    def own_rows(self, j, staged, landed, recv):
        return pltpu.make_async_copy(staged.at[self.part, j], landed.at[j, self.s], recv.at[j, self.s])

    def relay(self, j, off, landed, send, recv):
        slot = lax.rem(self.part + off, PARTS) * self.splits + self.split
        out = []
        for hop in range(1, self.splits):
            split = lax.rem(self.split + hop, self.splits)
            out.append(remote(landed.at[j, slot], landed.at[j, slot], send.at[j, off, hop - 1],
                              recv.at[j, slot], {"seq": self.part * self.splits + split}))
        return slot, out

    def give_back(self, j, heads, staged, landed, send, recv):
        out = []
        row = self.part * heads + j
        for off in range(1, self.n):
            t = self.other(off)
            out.append(remote(staged.at[j, t], landed.at[row, self.split], send.at[j, off - 1],
                              recv.at[j, self.s], {"seq": t}))
        return out

    def keep_own(self, j, heads, staged, landed, recv):
        return pltpu.make_async_copy(staged.at[j, self.s], landed.at[self.part * heads + j, self.split],
                                     recv.at[j, self.s])


def here(ref, sem):
    pltpu.make_async_copy(ref, ref, sem).wait()


def forward_kernel(
    n, heads, table, x, first, gain, shift, wq, bq, wk, wv, bv,
    hidden_out, q_all, kv_all, ol_all, back,
    q_staged, kv_staged, o_staged, q_work, kv_work,
    q_send, kv_send, relay_send, o_send, q_recv, kv_recv, o_recv,
):
    ex = Exchange(n)
    enter(ex.peers())
    splits = ex.splits
    rows, width = x.shape
    share = rows // splits
    half = n // 2
    fresh = wv.shape[1]
    normed, _ = normal_rows(x[...].astype(jnp.float32))
    hidden = (normed * gain[...].astype(jnp.float32) + shift[...].astype(jnp.float32)).astype(jnp.bfloat16)
    hidden_out[...] = hidden
    for step in range(width // 256):
        cols = slice(step * 256, (step + 1) * 256)
        q = product(hidden, wq[:, cols]) + bq[:, cols].astype(jnp.float32)

        def store(head, split, v, step=step):
            head = head + 4 * step
            q_staged[head // heads, head % heads, split] = (v * 0.125).astype(jnp.bfloat16)

        pack_heads(q, splits, store)
        k = product(hidden, wk[:, cols])
        for tile in range(2):
            at = step * 256 + tile * 128
            if at < fresh:
                v = product(hidden, wv[:, at : at + 128]) + bv[:, at : at + 128].astype(jnp.float32)
            else:
                v = first[:, at - fresh : at - fresh + 128].astype(jnp.float32)
            kt = k[:, tile * 128 : (tile + 1) * 128]
            low = lanes(kt.shape) < 64
            head = at // 64
            kv_staged[head // heads, head % heads] = jnp.where(low, kt, swap_lanes(v)).astype(jnp.bfloat16)
            head = head + 1
            kv_staged[head // heads, head % heads] = jnp.where(low, swap_lanes(kt), v).astype(jnp.bfloat16)

    @pl.loop(0, heads)
    def _(j):
        for copy in ex.spread(j, kv_staged, kv_all, kv_send, kv_recv):
            copy.start()
        for copy in ex.scatter(j, q_staged, q_all, q_send, q_recv):
            copy.start()
        ex.own(j, q_staged, q_all, q_recv).start()
        ex.own_rows(j, kv_staged, kv_all, kv_recv).start()

    slot = slots_of(table, n)
    row = lax.broadcasted_iota(jnp.int32, (share, rows), 0) + ex.split * share
    own_mask = lax.broadcasted_iota(jnp.int32, (share, rows), 1) <= row

    def piece(j, place, at, keys):
        q = unfold(q_work[at].astype(jnp.float32), False).astype(jnp.bfloat16)
        blocks = [kv_work[k] for k in keys] + [kv_work[at]]
        scores = [product_right(q, block) for block in blocks]
        scores[-1] = jnp.where(own_mask, scores[-1], NEG)
        top = scores[0]
        for s in scores[1:]:
            top = jnp.maximum(top, s)
        top = jnp.max(top, axis=1, keepdims=True)
        total = jnp.zeros((share, rows), jnp.float32)
        out = jnp.zeros((share, 128), jnp.float32)
        for s, block in zip(scores, blocks):
            weight = jnp.exp(s - top)
            total = total + weight
            out = out + product(weight.astype(jnp.bfloat16), block)
        denom = jnp.sum(total, axis=1, keepdims=True)
        out = out / denom
        ol_all[j, place] = jnp.where(lanes(out.shape) < 64, top + jnp.log(denom), out)

    @pl.loop(0, heads)
    def _(j):
        for off in range(PARTS):
            at, copies = ex.relay(j, off, kv_all, relay_send, kv_recv)
            here(kv_all.at[j, at], kv_recv.at[j, at])
            for copy in copies:
                copy.start()
        for t in range(n):
            here(q_all.at[j, t], q_recv.at[j, t])
        for off in range(PARTS):
            for hop in range(1, splits):
                at = lax.rem(ex.part + off, PARTS) * splits + lax.rem(ex.split + hop, splits)
                here(kv_all.at[j, at], kv_recv.at[j, at])
        for t in range(n):
            q_work[t] = q_all[j, t]
            kv_work[t] = kv_all[j, t]

        @pl.loop(0, half)
        def _(c):
            piece(j, half + c, pick(slot[half:], c), slot[:half])

        for p in range(half):
            piece(j, p, slot[p], slot[:p])
        for t in range(n):
            o_staged[j, t] = fold(ol_all[j, table[0, t]], True).astype(jnp.bfloat16)
        for copy in ex.give_back(j, heads, o_staged, back, o_send, o_recv):
            copy.start()
        ex.keep_own(j, heads, o_staged, back, o_recv).start()

    @pl.loop(0, heads)
    def _(j):
        for copy in ex.spread(j, kv_staged, kv_all, kv_send, kv_recv):
            copy.wait_send()
        for copy in ex.scatter(j, q_staged, q_all, q_send, q_recv):
            copy.wait_send()
        for off in range(PARTS):
            for copy in ex.relay(j, off, kv_all, relay_send, kv_recv)[1]:
                copy.wait_send()
        for copy in ex.give_back(j, heads, o_staged, back, o_send, o_recv):
            copy.wait_send()
        for t in range(n):
            landed = back.at[t // splits * heads + j, t % splits]
            here(landed, o_recv.at[j, t])


def forward_call(n, table, x, first, gain, shift, wq, bq, wk, wv, bv):
    rows, width = x.shape
    splits = n // PARTS
    heads = width // 64 // PARTS
    share = rows // splits
    low = jnp.bfloat16
    vmem, dma = pltpu.VMEM, pltpu.SemaphoreType.DMA
    inside = pl.BlockSpec(memory_space=vmem)
    shape = jax.ShapeDtypeStruct
    return pl.pallas_call(
        functools.partial(forward_kernel, n, heads),
        out_shape=[
            shape((rows, width), low),
            shape((heads, n, share // 2, 128), low),
            shape((heads, n, rows, 128), low),
            shape((heads, n, share, 128), jnp.float32),
            shape((PARTS * heads, splits, share // 2, 128), low),
        ],
        in_specs=[pl.BlockSpec(memory_space=pltpu.SMEM)] + [inside] * 9,
        out_specs=[inside] * 5,
        scratch_shapes=[
            vmem((PARTS, heads, splits, share // 2, 128), low),
            vmem((PARTS, heads, rows, 128), low),
            vmem((heads, n, share // 2, 128), low),
            vmem((n, share // 2, 128), low),
            vmem((n, rows, 128), low),
            dma((heads, n - 1)),
            dma((heads, PARTS - 1)),
            dma((heads, PARTS, max(splits - 1, 1))),
            dma((heads, n - 1)),
            dma((heads, n)),
            dma((heads, n)),
            dma((heads, n)),
        ],
        compiler_params=pltpu.CompilerParams(
            collective_id=1, has_side_effects=True, vmem_limit_bytes=64000000
        ),
        name="attention_forward",
    )(table, x, first, gain, shift, wq, bq, wk, wv, bv)


def backward_kernel(
    n, heads, table, do_in, q_all, kv_all, ol_all,
    dq_back, dkv_back,
    do_all, do_work, acc, dq_piece, dq_staged, part_staged, part_all, dkv_staged,
    do_send, do_recv, dq_send, dq_recv, part_send, part_recv, dkv_send, dkv_recv,
):
    ex = Exchange(n)
    enter(ex.peers())
    splits = ex.splits
    rows = kv_all.shape[2]
    share = rows // splits
    half = n // 2

    @pl.loop(0, heads)
    def _(j):
        for copy in ex.scatter(j, do_in, do_all, do_send, do_recv):
            copy.start()
        ex.own(j, do_in, do_all, do_recv).start()

    slot = slots_of(table, n)
    column = lax.broadcasted_iota(jnp.int32, (rows, share), 1) + ex.split * share
    own_mask = lax.broadcasted_iota(jnp.int32, (rows, share), 0) <= column

    def piece(j, place, at, keys):
        q = unfold(q_all[j, at].astype(jnp.float32), False).astype(jnp.bfloat16)
        grad = unfold(do_work[at].astype(jnp.float32), True)
        ol = ol_all[j, place]
        delta = jnp.sum(jnp.transpose(grad * ol), axis=0, keepdims=True)
        logsum = jnp.transpose(ol)[0:1]
        grad = grad.astype(jnp.bfloat16)
        dq = jnp.zeros((128, share), jnp.float32)
        for where, (key_place, key_slot) in enumerate(keys + [(place, at)]):
            block = kv_all[j, key_slot]
            weight = jnp.exp(product_right(block, q) - logsum)
            if where == len(keys):
                weight = jnp.where(own_mask, weight, 0.0)
            change = (weight * (product_right(block, grad) - delta)).astype(jnp.bfloat16)
            term = product(weight.astype(jnp.bfloat16), grad) + product(change, q)
            acc[key_place] = acc[key_place] + term
            dq = dq + product_left(block, change)
        dq_piece[place] = fold(jnp.transpose(dq) * 0.125, False).astype(jnp.bfloat16)

    def part_copies(j):
        out = []
        for hop in range(1, splits):
            split = lax.rem(ex.split + hop, splits)
            for part in range(PARTS):
                out.append(remote(part_staged.at[j, split, part], part_all.at[j, ex.split, part],
                                  part_send.at[j, split, part], part_recv.at[j, ex.split, part],
                                  {"seq": ex.part * splits + split}))
        return out

    def back_copies(j):
        out = []
        row = ex.part * heads + j
        for off in range(1, PARTS):
            part = lax.rem(ex.part + off, PARTS)
            out.append(remote(dkv_staged.at[j, part], dkv_back.at[row], dkv_send.at[j, off - 1],
                              dkv_recv.at[j, ex.part], {"seq": part * splits + ex.split}))
        return out

    @pl.loop(0, heads)
    def _(j):
        for t in range(n):
            here(do_all.at[j, t], do_recv.at[j, t])
        for t in range(n):
            do_work[t] = do_all[j, t]
            acc[t] = jnp.zeros((rows, 128), jnp.float32)

        @pl.loop(0, half)
        def _(c):
            piece(j, half + c, pick(slot[half:], c), [(p, slot[p]) for p in range(half)])

        for p in range(half):
            piece(j, p, slot[p], [(k, slot[k]) for k in range(p)])
        for hop in range(1, splits):
            split = lax.rem(ex.split + hop, splits)
            for part in range(PARTS):
                part_staged[j, split, part] = acc[table[0, part * splits + split]].astype(jnp.bfloat16)
        for copy in part_copies(j):
            copy.start()
        for t in range(n):
            dq_staged[j, t] = dq_piece[table[0, t]]
        for hop in range(1, splits):
            split = lax.rem(ex.split + hop, splits)
            for part in range(PARTS):
                here(part_all.at[j, split, part], part_recv.at[j, split, part])
        for part in range(PARTS):
            total = acc[table[0, part * splits + ex.split]]
            for hop in range(1, splits):
                total = total + part_all[j, lax.rem(ex.split + hop, splits), part].astype(jnp.float32)
            dkv_staged[j, part] = total.astype(jnp.bfloat16)
        for copy in back_copies(j):
            copy.start()
        pltpu.make_async_copy(dkv_staged.at[j, ex.part], dkv_back.at[ex.part * heads + j],
                              dkv_recv.at[j, ex.part]).start()
        for copy in ex.give_back(j, heads, dq_staged, dq_back, dq_send, dq_recv):
            copy.start()
        ex.keep_own(j, heads, dq_staged, dq_back, dq_recv).start()

    @pl.loop(0, heads)
    def _(j):
        for copy in ex.scatter(j, do_in, do_all, do_send, do_recv):
            copy.wait_send()
        for copy in part_copies(j):
            copy.wait_send()
        for copy in back_copies(j):
            copy.wait_send()
        for copy in ex.give_back(j, heads, dq_staged, dq_back, dq_send, dq_recv):
            copy.wait_send()
        for t in range(n):
            here(dq_back.at[t // splits * heads + j, t % splits], dq_recv.at[j, t])
        for part in range(PARTS):
            here(dkv_back.at[part * heads + j], dkv_recv.at[j, part])


def backward_call(n, table, do_in, q_all, kv_all, ol_all):
    heads, _, rows, _ = kv_all.shape
    splits = n // PARTS
    share = rows // splits
    low = jnp.bfloat16
    vmem, dma = pltpu.VMEM, pltpu.SemaphoreType.DMA
    inside = pl.BlockSpec(memory_space=vmem)
    shape = jax.ShapeDtypeStruct
    return pl.pallas_call(
        functools.partial(backward_kernel, n, heads),
        out_shape=[
            shape((PARTS * heads, splits, share // 2, 128), low),
            shape((PARTS * heads, rows, 128), low),
        ],
        in_specs=[pl.BlockSpec(memory_space=pltpu.SMEM)] + [inside] * 4,
        out_specs=[inside] * 2,
        scratch_shapes=[
            vmem((heads, n, share // 2, 128), low),
            vmem((n, share // 2, 128), low),
            vmem((n, rows, 128), jnp.float32),
            vmem((n, share // 2, 128), low),
            vmem((heads, n, share // 2, 128), low),
            vmem((heads, splits, PARTS, rows, 128), low),
            vmem((heads, splits, PARTS, rows, 128), low),
            vmem((heads, PARTS, rows, 128), low),
            dma((heads, n - 1)),
            dma((heads, n)),
            dma((heads, n - 1)),
            dma((heads, n)),
            dma((heads, splits, PARTS)),
            dma((heads, splits, PARTS)),
            dma((heads, PARTS - 1)),
            dma((heads, PARTS)),
        ],
        compiler_params=pltpu.CompilerParams(
            collective_id=2, has_side_effects=True, vmem_limit_bytes=64000000
        ),
        name="attention_backward",
    )(table, do_in, q_all, kv_all, ol_all)


def collect(parts):
    groups = lax.axis_size("grp")
    n = lax.axis_size("seq")
    small = (0, 1, 3, 6, 8, 9, 10, 12, 14)
    packed = jnp.concatenate([parts[i] for i in small])
    sizes = [parts[i].shape[0] for i in small]
    length = packed.shape[0]
    packed = jnp.pad(packed, (0, 2048 - length)).reshape(16, 128)
    bits = powers(groups)
    forth, back = bits, bits[::-1]
    shards = [packed, parts[2], parts[5], parts[4], parts[7], parts[11], parts[13]]
    fulls = gather_call(groups, n // 2, shards, [forth, forth, forth, back, back, forth, back])
    flat = fulls[0].reshape(groups * n, 2048)
    whole = [None] * 15
    at = 0
    for i, size in zip(small, sizes):
        whole[i] = flat[:, at : at + size].reshape(groups * n * size)
        at += size
    for i, full in zip((2, 5, 4, 7, 11, 13), fulls[1:]):
        whole[i] = full.reshape(-1, full.shape[-1])
    return tuple(whole)


def normalize(v, gain, shift):
    mean = jnp.mean(v, axis=-1, keepdims=True)
    centred = v - mean
    var = jnp.mean(centred * centred, axis=-1, keepdims=True)
    return centred * lax.rsqrt(var + EPS) * gain + shift


def gelu_tanh(v):
    return jax.nn.gelu(v, approximate=True)


def unpack_rows(v):
    heads, splits, size, _ = v.shape
    v = v.reshape(heads, splits, size, 2, 64)
    return jnp.transpose(v, (1, 3, 2, 0, 4)).reshape(splits * 2 * size, heads * 64)


def pack_rows(v, splits):
    rows, width = v.shape
    heads = width // 64
    v = v.reshape(splits, 2, rows // splits // 2, heads, 64)
    v = jnp.transpose(v, (3, 0, 2, 1, 4))
    return v.reshape(PARTS, heads // PARTS, splits, rows // splits // 2, 128)


def body(
    tokens,
    first_values,
    placement,
    cotangent,
    *parts,
):
    groups, rows, width = tokens.shape
    n = lax.axis_size("seq")
    splits = n // PARTS
    whole = collect(parts)
    gain_one = whole[0].astype(jnp.float32)
    bias_one = whole[1].astype(jnp.float32)
    gain_two = whole[9].astype(jnp.float32)
    bias_two = whole[10].astype(jnp.float32)
    hidden, q_all, kv_all, ol_all, back = forward_call(
        n, placement, tokens[0], first_values[0], whole[0][None], whole[1][None],
        whole[2], whole[3][None], whole[4], whole[5], whole[6][None],
    )
    attended_low = unpack_rows(back)
    flat = tokens[0].astype(jnp.float32)
    middle = flat + product(attended_low, whole[7]) + whole[8].astype(jnp.float32)
    normed_two, norm_two_back = jax.vjp(normalize, middle, gain_two, bias_two)
    second = normed_two.astype(jnp.bfloat16)
    pre = product(second, whole[11]) + whole[12].astype(jnp.float32)
    post_full, gelu_back = jax.vjp(gelu_tanh, pre)
    post = post_full.astype(jnp.bfloat16)
    result = middle + product(post, whole[13]) + whole[14].astype(jnp.float32)
    layer_output = result.astype(jnp.bfloat16)[None]
    seed = cotangent[0]
    seed_full = seed.astype(jnp.float32)
    grad_reduce_bias = jnp.sum(seed_full, axis=0)
    grad_reduce = product_left(post, seed)
    grad_post = product_right(seed, whole[13])
    grad_pre = gelu_back(grad_post)[0].astype(jnp.bfloat16)
    grad_expand_bias = jnp.sum(grad_pre.astype(jnp.float32), axis=0)
    grad_expand = product_left(second, grad_pre)
    grad_second = product_right(grad_pre, whole[11])
    grad_mid_norm, grad_gain_two, grad_bias_two = norm_two_back(grad_second)
    grad_mid = grad_mid_norm + seed_full
    grad_branch = grad_mid.astype(jnp.bfloat16)
    grad_output_bias = jnp.sum(grad_branch.astype(jnp.float32), axis=0)
    grad_output = product_left(attended_low, grad_branch)
    grad_attended = product_right(grad_branch, whole[7]).astype(jnp.bfloat16)
    dq_back, dkv_back = backward_call(n, placement, pack_rows(grad_attended, splits), q_all, kv_all, ol_all)
    grad_query_all = unpack_rows(dq_back)
    heads = width // 64
    pair = jnp.transpose(dkv_back.reshape(heads, rows, 2, 64), (2, 1, 0, 3)).reshape(2, rows, width)
    fresh_width = whole[5].shape[1]
    grad_key, grad_fresh = pair[0], pair[1][:, :fresh_width]
    first_values_grad = pair[1][:, fresh_width:].astype(jnp.float32)[None]
    grad_query_bias = jnp.sum(grad_query_all.astype(jnp.float32), axis=0)
    grad_query_weight = product_left(hidden, grad_query_all)
    grad_key_weight = product_left(hidden, grad_key)
    grad_value_weight = product_left(hidden, grad_fresh)
    grad_value_bias = jnp.sum(grad_fresh.astype(jnp.float32), axis=0)
    grad_hidden = (
        product_right(grad_query_all, whole[2])
        + product_right(grad_key, whole[4])
        + product_right(grad_fresh, whole[5])
    )
    _, norm_one_back = jax.vjp(normalize, flat, gain_one, bias_one)
    grad_in, grad_gain_one, grad_bias_one = norm_one_back(grad_hidden)
    token_grad = (grad_in + grad_mid)[None]
    owned = reduce_gradients((
        grad_gain_one, grad_bias_one, grad_query_weight, grad_query_bias, grad_key_weight,
        grad_value_weight, grad_value_bias, grad_output, grad_output_bias, grad_gain_two, grad_bias_two,
        grad_expand, grad_expand_bias, grad_reduce, grad_reduce_bias,
    ))
    return (layer_output, token_grad, first_values_grad) + owned


def reduce_gradients(grads):
    groups = lax.axis_size("grp")
    n = lax.axis_size("seq")
    chips = n // 2
    small = (0, 1, 3, 6, 8, 9, 10, 12, 14)
    large = (11, 13, 7, 4, 2, 5)
    sizes = [grads[i].shape[0] // (groups * n) for i in small]
    packed = jnp.concatenate([grads[i].reshape(groups * n, -1) for i in small], axis=1)
    packed = jnp.pad(packed, ((0, 0), (0, 1024 - packed.shape[1]))).reshape(groups, chips, 2, 8, 128)
    bits = powers(groups)
    forth, back = bits, bits[::-1]
    partials = [grads[i].astype(jnp.bfloat16).reshape(groups, chips, 2, -1, grads[i].shape[1]) for i in large]
    shards = reduce_call(groups, chips, partials + [packed], [forth, back, forth, back, forth, back, forth])
    out = [None] * 15
    for i, shard in zip(large, shards):
        out[i] = shard
    flat = shards[-1].reshape(1024)
    at = 0
    for i, size in zip(small, sizes):
        out[i] = flat[at : at + size]
        at += size
    return tuple(out)


def solution(mesh):
    spread = P("grp", "seq", None)
    both = ("grp", "seq")
    vector, matrix = P(both), P(both, None)
    kinds = (vector, vector, matrix, vector, matrix, matrix, vector, matrix, vector, vector, vector,
             matrix, vector, matrix, vector)
    in_specs = (spread, spread, P("grp", None), spread) + kinds
    out_specs = (spread, spread, spread) + kinds
    return jax.shard_map(body, mesh=mesh, in_specs=in_specs, out_specs=out_specs, check_vma=False)
```

time: 1400 us -> 508 us (0.36)
  waiting for transfers between devices: 827 us -> 0 us
  Pallas kernels: 76.2 us -> 388 us
  matrix products: 258 us -> 49.7 us
  other arithmetic: 56.4 us -> 8.26 us
  local copies, waits for them, and re-layouts: 98.9 us -> 54.9 us
  blocking collectives: 38.6 us -> 0 us
  loops' own time: 23 us -> 0 us
  between operations: 16 us -> 1.51 us
    reduce_scatter x7 -> x0, waiting for transfers between devices: 614 us -> none  [the longest x1 142 us: body(): lax.psum_scatter(grad_expand, ('grp', 'seq'), scatter_dimension=0, tiled=...]
    pallas_call x0 -> x3, Pallas kernels: none -> 312 us  [the longest x1 148 us: reduce_call(): pl.pallas_call(functools.partial(reduce_kernel, groups, chips, orders), o...]
    dot_general x53 -> x15, matrix products: 258 us -> 49.7 us  [the longest x6 18.8 us: product_left(): lax.dot_general(a, b, (((0,), (0,)), ((), ())), preferred_element_type=jn...]
    all_gather x2 -> x0, waiting for transfers between devices: 111 us -> none  [the longest x1 56.2 us: body(): lax.all_gather(values_local, 'seq', axis=1, tiled=True)]
    unnamed x11 -> x0, waiting for transfers between devices: 101 us -> none
    convert_element_type x11 -> x3, local copies, waits for them, and re-layouts: 43.1 us -> 2.44 us  [the longest x1 2.29 us: body(): grad_attended = product_right(grad_branch, whole[7]).astype(jnp.bfloat16)]
    unnamed x1 -> x0, blocking collectives: 38.6 us -> none
    another operation x18 -> x0, loops' own time: 23 us -> none  [the longest x1 11.1 us: attend_backward(): lax.scan(step, start_grad, jnp.arange(total // block))]
  transfers between devices with their start and end apart: 10 -> 0, of which waited for: 10 -> 0; matrix products, arithmetic and copies ran while one was open for 6% -> 0% of each run, Pallas kernels for 0% -> 0%
where the time goes in v2:
time: 508 us; the launch traced here: 502 us
  Pallas kernels  388 us (76%)
  local copies, waits for them, and re-layouts  54.9 us (11%)
  matrix products  49.7 us (10%)
  other arithmetic  8.26 us (2%)
    pallas_call x1, Pallas kernels, reduce_call(): pl.pallas_call(functools.partial(reduce_kernel, groups, chips, orders), o...  148 us
    pallas_call x1, Pallas kernels, backward_call(): pl.pallas_call(functools.partial(backward_kernel, n, heads), out_shape=[s...  83 us
    pallas_call x1, Pallas kernels, forward_call(): pl.pallas_call(functools.partial(forward_kernel, n, heads), out_shape=[sh...  80.2 us
    pallas_call x1, Pallas kernels, gather_call(): pl.pallas_call(functools.partial(gather_kernel, groups, chips, orders), o...  76.2 us
    dot_general x6, matrix products, product_left(): lax.dot_general(a, b, (((0,), (0,)), ((), ())), preferred_element_type=jn...  18.8 us
    dot_general x6, matrix products, product_right(): lax.dot_general(a, b, (((1,), (1,)), ((), ())), preferred_element_type=jn...  18.6 us
    unnamed x50, local copies, waits for them, and re-layouts  14.3 us
    dot_general x3, matrix products, product(): lax.dot_general(a, b, (((1,), (0,)), ((), ())), preferred_element_type=jn...  12.3 us

profile of v2, /device:TPU:0, one launch (start us, length us, event | category | flops | bytes accessed | tf_op | source)
XLA Modules:
  0.0 502.2 jit_solution(5873195662438467032)
XLA Ops:
  0.7 6.1 %concatenate.6 = bf16[276]{0:T(512)(128)(2,1)S(1)} concatenate(bf16[24]{0:T(256)(128)(2,1)} %param.23, bf16[24]{0:T(256)(128)(2,1)} %param.24, bf16[24]{0:T(256)(128)(2,1)} %param.26, bf16[12]{0:T(256)(128)(2,1)} %param.29, bf16[24]{0:T(256)(128)(2,1)} %param.31, bf16[24]{0:T(256)(128)(2,1)} %param.32, bf16[24]{0:T(256)(128)(2,1)} %param.33, bf16[96]{0:T(256)(128)(2,1)} %param.35, ...), dimensions={0} | concatenate | bytes 1104 | tf_op jit(solution)/shard_map/concatenate | solution.py:862
  6.8 1.3 convert_reduce_fusion.1
  8.1 0.6 pad_bitcast_fusion.1.refs_0_
  8.7 76.2 %gather_parameters.1 = (bf16[4,4,2,16,128]{4,3,2,1,0:T(8,128)(2,1)}, bf16[4,4,2,24,768]{4,3,2,1,0:T(8,128)(2,1)}, bf16[4,4,2,24,384]{4,3,2,1,0:T(8,128)(2,1)}, b...) custom-call(bf16[16,128]{1,0:T(8,128)(2,1)} %pad_bitcast_fusion.1.re, ...), custom_call_target="tpu_custom_call" | custom-call | tf_op jit(solution)/shard_map/gather_parameters/pallas_call | solution.py:200
  84.9 0.9 copy.51
  85.9 0.7 broadcast_in_dim_reshape.15.bv
  86.8 0.1 reshape.288
  86.9 0.7 broadcast_in_dim_reshape.14.bq
  87.6 0.7 broadcast_in_dim_reshape.13.shift
  88.3 0.7 broadcast_in_dim_reshape.12.gain
  89.3 80.2 %attention_forward.1 = (bf16[512,768]{1,0:T(8,128)(2,1)}, bf16[3,8,128,128]{3,2,1,0:T(8,128)(2,1)}, bf16[3,8,512,128]{3,2,1,0:T(8,128)(2,1)}, f32[3,8,256,128]{3,2,1,0:T(8,128)}, bf16[12,2,128,128]{3,2,1,0:T(8,128)(2,1)}) custom-call(s32[1,8]{1,0:T(1,128)} %table.3, bf16[512,768]{1,0:T(8,128)(2,1)} %bitcast.110, bf16[512,384]{1,0:T(8,128)(2,1)} %bitcast.136, ...), custom_call_target="tpu_custom_call" | custom-call | tf_op jit(solution)/shard_map/attention_forward/pallas_call | solution.py:669
  169.5 1.6 copy.39
  171.1 0.8 copy.40
  171.9 0.3 reshape.257
  172.2 2.5 fusion.35
  174.8 0.3 multiply_reduce_fusion.2
  175.1 4.9 fusion.29
  180.0 4.9 fusion.19
  184.9 6.7 %convert_reduce_fusion = (f32[3072]{0:T(1024)S(1)}, bf16[512,3072]{1,0:T(8,128)(2,1)S(1)}) fusion(f32[512,3072]{1,0:T(8,128)S(1)} %fusion.29, f32[3072]{0:T(1024)S(1)} %reshape.286, bf16[3072,768]{1,0:T(8,128)(2,1)S(1)} %bitcast.151, bf16[1,512,768]{2,1,0:T(8,128)(2,1)S(1)} %copy-done.4), kind=kOutput, calls=%fused_computation.14 | convolution fusion | flops 2452091904 | bytes 14966784 | tf_op jit(solution)/shard_map/dot_general | solution.py:441
  191.6 5.5 %convolution_convert_fusion = bf16[3072,768]{1,0:T(8,128)(2,1)} fusion(bf16[1,512,768]{2,1,0:T(8,128)(2,1)S(1)} %copy-done.4, f32[512,3072]{1,0:T(8,128)S(1)} %fusion.29, f32[3072]{0:T(1024)S(1)} %reshape.286), kind=kOutput, calls=%fused_computation.16 | convolution fusion | flops 2434007040 | bytes 11808768 | tf_op jit(solution)/shard_map/dot_general | solution.py:445
  197.1 3.0 multiply_reduce_fusion
  200.1 0.7 fusion.32
  200.8 4.9 convolution_convert_fusion.1
  206.0 1.6 convert_reduce_fusion.3
  207.6 0.9 copy-done.11
  208.5 1.7 convolution_convert_fusion.5
  210.2 2.3 copy.41
  212.5 2.9 reshape.261
  215.4 2.2 copy.42
  217.6 2.3 copy.43.do_in
  219.9 83.0 %attention_backward.1 = (bf16[12,2,128,128]{3,2,1,0:T(8,128)(2,1)}, bf16[12,512,128]{2,1,0:T(8,128)(2,1)}) custom-call(s32[1,8]{1,0:T(1,128)} %table.3, bf16[4,3,2,128,128]{4,3,2,1,0:T(8,128)(2,1)} %copy.43.do_in, bf16[3,8,128,128]{3,2,1,0:T(8,128)(2,1)} %get-tuple-element.47.q_all, bf16[3,8,512,128]{3,2,1,0:T(8,128)(2,1)} %get-tuple-element.48.kv_all, ...), custom_call_target="tpu_custom_call" | custom-call | tf_op jit(solution)/shard_map/attention_backward/pallas_call | solution.py:825
  302.9 2.3 copy.44
  305.2 1.3 convert_reduce_fusion.4
  306.5 2.8 copy.45
  309.4 3.1 reshape.264
  312.6 0.1 reshape.276
  312.8 3.6 fusion.36
  316.4 1.8 convolution_convert_fusion.2
  318.2 1.8 convolution_convert_fusion.4
  320.1 2.8 copy.46
  322.9 2.4 fusion.33
  325.3 0.9 copy-done.1
  326.1 0.1 convert_reduce_fusion.5
  326.3 0.1 reshape.275
  326.4 2.5 fusion.37
  328.9 1.1 fusion.30
  330.1 0.8 fusion.17
  330.9 0.3 copy-done.5
  331.2 1.8 add_bitcast_fusion
  333.2 0.1 concatenate.7
  333.3 0.7 copy.49
  334.0 3.3 convolution_convert_fusion.3
  337.3 1.4 convolution_convert_fusion.6
  338.9 1.2 copy.47
  340.0 148.3 %reduce_gradients.1 = (f32[24,3072]{1,0:T(8,128)}, f32[96,768]{1,0:T(8,128)}, f32[24,768]{1,0:T(8,128)}, f32[24,768]{1,0:T(8,128)}, f32[24,768]{1,0:T(8,128)}, /*index=5*/f32[24,384]{1,0:T(8,128)}, f32[8,128]{1,0:T(8,128)}) custom-call(bf16[4,4,2,24,3072]{4,3,2,1,0:T(8,128)(2,1)} %bitcast.119, bf16[4,4,2,96,768]{4,3,2,1,0:T(8,128)(2,1)} %bitcast.118, ...), custom_call_target="tpu_custom_call" | custom-call | tf_op jit(solution)/shard_map/reduce_gradients/pallas_call | solution.py:395
  488.3 1.3 slice.89
  489.6 1.3 slice.85
  490.8 1.5 fusion.34
  492.4 1.5 copy.58
  493.9 1.5 copy.59
  495.4 1.4 copy.60
  496.8 1.5 copy.61
  498.3 1.7 copy.62
  500.0 1.7 copy.63
  (62 shorter events, 1.4 us)
Async XLA Ops:
  171.1 1.1 copy-start
  172.2 2.5 copy-start.8
  174.8 5.2 %slice-start.2 = ((s8[4718592]{0:T(1024)(128)(4,1)}), s8[4194304]{0:T(1024)(128)(4,1)S(1)}, s32[]{:S(2)}) async-start(s8[4718592]{0:T(1024)(128)(4,1)} %bitcast.148), calls=%async_computation.2 | async-start | bytes 8388608
  175.1 4.9 slice-start.3
  180.0 4.9 copy-start.4
  180.0 17.1 %slice-start = ((s8[4718592]{0:T(1024)(128)(4,1)}), s8[4194304]{0:T(1024)(128)(4,1)S(1)}, s32[]{:S(2)}) async-start(s8[4718592]{0:T(1024)(128)(4,1)} %bitcast.145), calls=%async_computation | async-start | bytes 8388608
  184.9 12.2 %slice-start.1 = ((s8[4718592]{0:T(1024)(128)(4,1)}), s8[524288]{0:T(1024)(128)(4,1)S(1)}, s32[]{:S(2)}) async-start(s8[4718592]{0:T(1024)(128)(4,1)} %bitcast.145), calls=%async_computation.1 | async-start | bytes 1048576
  206.0 2.5 copy-start.13
  207.6 0.9 copy-start.11
  312.7 3.6 copy-start.10
  312.8 3.6 copy-start.14
  316.4 1.9 copy-start.9
  316.4 1.9 copy-start.12
  325.3 0.9 copy-start.1
  326.4 2.5 copy-start.2
  326.4 2.5 copy-start.6
  326.4 2.5 copy-start.7
  330.1 1.1 copy-start.5
  334.0 3.3 copy-start.3
  334.0 3.3 copy-start.15

commit v3 on v2

--- a/solution.py
+++ b/solution.py
@@ -209,11 +209,11 @@
 
 
 class Reduce:
-    def __init__(self, groups, chips, bits, partial, shard, own, landed, halves, left, right, sems):
+    def __init__(self, groups, chips, bits, partial, shard, own, landed, halves, finals, sems):
         self.groups, self.chips, self.bits = groups, chips, bits
         self.partial, self.shard, self.own, self.landed = partial, shard, own, landed
-        self.halves, self.left, self.right = halves, left, right
-        self.load, self.pair, self.level_send, self.level_recv, self.chain_send, self.chain_recv = sems
+        self.halves, self.finals = halves, finals
+        self.load, self.pair, self.level_send, self.level_recv, self.chip_send, self.chip_recv = sems
         self.g = lax.axis_index("grp")
         self.s = lax.axis_index("seq")
         self.z, self.c = self.s // 2, self.s % 2
@@ -246,7 +246,7 @@
         self.cross_start(0)
 
     def add(self, a, b):
-        return (a.astype(jnp.float32) + b.astype(jnp.float32)).astype(a.dtype)
+        return a + b
 
     def cross_copies(self, level):
         bit = self.bits[level]
@@ -262,7 +262,8 @@
             for copy in self.cross_copies(level):
                 copy.start()
         else:
-            self.chain_first()
+            for copy in self.chip_copies():
+                copy.start()
 
     def crossed(self, level):
         copies = self.cross_copies(level)
@@ -272,89 +273,37 @@
             self.own[g] = self.add(self.own[g], self.halves[level][where])
         self.cross_start(level + 1)
 
-    def chain_copy(self, block, step):
-        side = 0 if step < 0 else 1
-        return remote(self.own.at[self.g, block], (self.right if step < 0 else self.left).at[block],
-                      self.chain_send.at[block], self.chain_recv.at[1 - side, block],
-                      {"seq": self.s + 2 * step})
-
-    def chain_wait(self, block, side):
-        landed = (self.left if side == 0 else self.right).at[block]
-        pltpu.make_async_copy(landed, landed, self.chain_recv.at[side, block]).wait()
-
-    def chain_first(self):
-        last = self.chips - 1
-
-        @pl.when(self.z == 0)
-        def _():
-            for block in range(last, 0, -1):
-                self.chain_copy(block, 1).start()
-
-        @pl.when(self.z == last)
-        def _():
-            for block in range(last):
-                self.chain_copy(block, -1).start()
-
-    def chained(self, k):
-        last = self.chips - 1
-        block = last - k
-
-        @pl.when((self.z > 0) & (self.z < block))
-        def _():
-            self.chain_wait(block, 0)
-            self.own[self.g, block] = self.add(self.own[self.g, block], self.left[block])
-            self.chain_copy(block, 1).start()
-
-        @pl.when((self.z < last) & (self.z > k))
-        def _():
-            self.chain_wait(k, 1)
-            self.own[self.g, k] = self.add(self.own[self.g, k], self.right[k])
-            self.chain_copy(k, -1).start()
+    def chip_copies(self):
+        out = []
+        for off in range(1, self.chips):
+            chip = lax.rem(self.z + off, self.chips)
+            out.append(remote(self.own.at[self.g, chip], self.finals.at[off - 1], self.chip_send.at[off - 1],
+                              self.chip_recv.at[off - 1], {"seq": 2 * chip + self.c}))
+        return out
 
     def finish(self):
-        last = self.chips - 1
-        self.shard[...] = self.own[self.g, self.z].astype(jnp.float32)
-
-        @pl.when(self.z > 0)
-        def _():
-            self.chain_wait(self.z, 0)
-            self.shard[...] = self.shard[...] + self.left[self.z].astype(jnp.float32)
-
-        @pl.when(self.z < last)
-        def _():
-            self.chain_wait(self.z, 1)
-            self.shard[...] = self.shard[...] + self.right[self.z].astype(jnp.float32)
+        total = self.own[self.g, self.z].astype(jnp.float32)
+        for off, copy in enumerate(self.chip_copies()):
+            copy.wait_recv()
+            total = total + self.finals[off].astype(jnp.float32)
+        self.shard[...] = total
 
     def drain(self):
         self.pair_copy().wait_send()
         for level in range(len(self.bits)):
             for copy in self.cross_copies(level):
                 copy.wait_send()
-        for block in range(self.chips):
-            @pl.when(self.z < block)
-            def _():
-                self.chain_copy(block, 1).wait_send()
-
-            @pl.when(self.z > block)
-            def _():
-                self.chain_copy(block, -1).wait_send()
+        for copy in self.chip_copies():
+            copy.wait_send()
 
 
 def reduce_steps(reduces):
-    chips, levels = reduces[0].chips, len(reduces[0].bits)
+    levels = len(reduces[0].bits)
     stages = [lambda r: r.begin(), lambda r: r.paired()]
     for level in range(levels):
         stages.append(lambda r, level=level: r.crossed(level))
-    for k in range(chips - 1):
-        stages.append(lambda r, k=k: r.chained(k))
-    stages.append(lambda r: r.finish())
-    stages.append(lambda r: r.drain())
-    out = []
-    for time in range(len(stages) + len(reduces) - 1):
-        for i, r in enumerate(reduces):
-            if 0 <= time - i < len(stages):
-                out.append(functools.partial(stages[time - i], r))
-    return out
+    stages += [lambda r: r.finish(), lambda r: r.drain()]
+    return [functools.partial(stage, r) for stage in stages for r in reduces]
 
 
 def reduce_scratch(groups, chips, shapes):
@@ -364,20 +313,21 @@
     for _, _, _, rows, cols, dtype in shapes:
         out += [vmem((groups, chips, rows, cols), dtype), vmem((groups, chips, rows, cols), dtype)]
         out += [vmem((groups >> (level + 1), chips, rows, cols), dtype) for level in range(levels)]
-        out += [vmem((chips, rows, cols), dtype)] * 2
+        out += [vmem((max(chips - 1, 1), rows, cols), dtype)]
         out += [dma((1,)), dma((2,)), dma((max(levels, 1), max(groups // 2, 1))),
-                dma((max(levels, 1), max(groups // 2, 1))), dma((chips,)), dma((2, chips))]
+                dma((max(levels, 1), max(groups // 2, 1))), dma((max(chips - 1, 1),)),
+                dma((max(chips - 1, 1),))]
     return out
 
 
 def make_reduces(groups, chips, orders, partials, shards, scratch):
     levels = len(powers(groups))
-    each = 2 + levels + 2 + 6
+    each = 2 + levels + 1 + 6
     out = []
     for i, (partial, shard) in enumerate(zip(partials, shards)):
         refs = scratch[i * each : (i + 1) * each]
         out.append(Reduce(groups, chips, orders[i], partial, shard, refs[0], refs[1], refs[2 : 2 + levels],
-                          refs[2 + levels], refs[3 + levels], refs[4 + levels :]))
+                          refs[2 + levels], refs[3 + levels :]))
     return out
 
 
@@ -698,18 +648,66 @@
     )(table, x, first, gain, shift, wq, bq, wk, wv, bv)
 
 
+def join_tiles(even, odd, high):
+    low = lanes(even.shape) < 64
+    if high:
+        return jnp.where(low, swap_lanes(even), odd)
+    return jnp.where(low, even, swap_lanes(odd))
+
+
+def join_rows(back):
+    heads, splits = back.shape[0], back.shape[1]
+    tiles = []
+    for tile in range(heads // 2):
+        parts = []
+        for split in range(splits):
+            even = back[2 * tile, split].astype(jnp.float32)
+            odd = back[2 * tile + 1, split].astype(jnp.float32)
+            parts += [join_tiles(even, odd, False), join_tiles(even, odd, True)]
+        tiles.append(jnp.concatenate(parts, axis=0))
+    return jnp.concatenate(tiles, axis=1)
+
+
+def spread_vector(vector, count):
+    size = vector.shape[1]
+    part = size // count
+    lane = lax.broadcasted_iota(jnp.int32, (count, size), 1)
+    row = lax.broadcasted_iota(jnp.int32, (count, size), 0)
+    mine = (lane >= row * part) & (lane < row * part + part)
+    spread = jnp.where(mine, vector, 0.0)
+    at = lax.broadcasted_iota(jnp.int32, (size, 128), 0)
+    to = lax.broadcasted_iota(jnp.int32, (size, 128), 1)
+    pick_part = jnp.where(lax.rem(at, part) == to, 1.0, 0.0)
+    return lax.dot_general(spread, pick_part, (((1,), (0,)), ((), ())), precision=lax.Precision.HIGHEST,
+                           preferred_element_type=jnp.float32)
+
+
 def backward_kernel(
-    n, heads, table, do_in, q_all, kv_all, ol_all,
-    dq_back, dkv_back,
-    do_all, do_work, acc, dq_piece, dq_staged, part_staged, part_all, dkv_staged,
-    do_send, do_recv, dq_send, dq_recv, part_send, part_recv, dkv_send, dkv_recv,
+    n, groups, heads, orders_far, orders_near,
+    table, do_in, q_all, kv_all, ol_all, hidden, x, gain, wq, wk, wv, dmid, s_gain2, s_bias2, s_ob, s_eb, s_rb,
+    *refs,
 ):
+    count = len(orders_far)
+    far_in, refs = refs[:count], refs[count:]
+    token_grad, first_grad = refs[:2]
+    far_out, refs = refs[2 : 2 + count], refs[2 + count :]
+    g_wk, g_wq, g_wv, g_small = refs[:4]
+    do_all, do_work, acc, dq_piece, dq_staged, part_staged, part_all, dkv_staged, dq_back, dkv_back = refs[4:14]
+    p_wk, p_wq, p_wv, p_small = refs[14:18]
+    do_send, do_recv, dq_send, dq_recv, part_send, part_recv, dkv_send, dkv_recv = refs[18:26]
+    scratch = refs[26:]
     ex = Exchange(n)
-    enter(ex.peers())
+    chips = n // 2
+    enter(ex.peers() + [{"grp": ex_g} for ex_g in [lax.axis_index("grp") ^ bit for bit in powers(groups)]])
+    each = len(scratch) // (count + 4)
+    far = make_reduces(groups, chips, orders_far, far_in, far_out, scratch[: count * each])
+    near = make_reduces(groups, chips, orders_near, [p_wk, p_wq, p_wv, p_small], [g_wk, g_wq, g_wv, g_small],
+                        scratch[count * each :])
     splits = ex.splits
     rows = kv_all.shape[2]
     share = rows // splits
     half = n // 2
+    fresh = wv.shape[1]
 
     @pl.loop(0, heads)
     def _(j):
@@ -717,6 +715,8 @@
             copy.start()
         ex.own(j, do_in, do_all, do_recv).start()
 
+    for r in far:
+        r.begin()
     slot = slots_of(table, n)
     column = lax.broadcasted_iota(jnp.int32, (rows, share), 1) + ex.split * share
     own_mask = lax.broadcasted_iota(jnp.int32, (rows, share), 0) <= column
@@ -745,8 +745,8 @@
         for hop in range(1, splits):
             split = lax.rem(ex.split + hop, splits)
             for part in range(PARTS):
-                out.append(remote(part_staged.at[j, split, part], part_all.at[j, ex.split, part],
-                                  part_send.at[j, split, part], part_recv.at[j, ex.split, part],
+                out.append(remote(part_staged.at[j, hop - 1, part], part_all.at[j, hop - 1, part],
+                                  part_send.at[j, hop - 1, part], part_recv.at[j, hop - 1, part],
                                   {"seq": ex.part * splits + split}))
         return out
 
@@ -771,24 +771,28 @@
         def _(c):
             piece(j, half + c, pick(slot[half:], c), [(p, slot[p]) for p in range(half)])
 
+        @pl.when(j == 0)
+        def _():
+            for r in far:
+                r.paired()
+
         for p in range(half):
             piece(j, p, slot[p], [(k, slot[k]) for k in range(p)])
         for hop in range(1, splits):
             split = lax.rem(ex.split + hop, splits)
             for part in range(PARTS):
-                part_staged[j, split, part] = acc[table[0, part * splits + split]].astype(jnp.bfloat16)
+                part_staged[j, hop - 1, part] = acc[table[0, part * splits + split]].astype(jnp.bfloat16)
         for copy in part_copies(j):
             copy.start()
         for t in range(n):
             dq_staged[j, t] = dq_piece[table[0, t]]
         for hop in range(1, splits):
-            split = lax.rem(ex.split + hop, splits)
             for part in range(PARTS):
-                here(part_all.at[j, split, part], part_recv.at[j, split, part])
+                here(part_all.at[j, hop - 1, part], part_recv.at[j, hop - 1, part])
         for part in range(PARTS):
             total = acc[table[0, part * splits + ex.split]]
             for hop in range(1, splits):
-                total = total + part_all[j, lax.rem(ex.split + hop, splits), part].astype(jnp.float32)
+                total = total + part_all[j, hop - 1, part].astype(jnp.float32)
             dkv_staged[j, part] = total.astype(jnp.bfloat16)
         for copy in back_copies(j):
             copy.start()
@@ -797,6 +801,73 @@
         for copy in ex.give_back(j, heads, dq_staged, dq_back, dq_send, dq_recv):
             copy.start()
         ex.keep_own(j, heads, dq_staged, dq_back, dq_recv).start()
+
+        @pl.when(j == min(1, heads - 1))
+        def _():
+            for r in far:
+                r.crossed(0)
+
+    @pl.loop(0, heads)
+    def _(j):
+        for t in range(n):
+            here(dq_back.at[t // splits * heads + j, t % splits], dq_recv.at[j, t])
+        for part in range(PARTS):
+            here(dkv_back.at[part * heads + j], dkv_recv.at[j, part])
+
+    for level in range(1, len(powers(groups))):
+        for r in far:
+            r.crossed(level)
+    low = jnp.bfloat16
+    h_across = jnp.transpose(hidden[...])
+
+    def keep(partial, value):
+        partial[...] = value.reshape(partial.shape).astype(low)
+
+    tiles = range(PARTS * heads // 2)
+    pairs = [(dkv_back[2 * t].astype(jnp.float32), dkv_back[2 * t + 1].astype(jnp.float32)) for t in tiles]
+    dk = jnp.concatenate([join_tiles(a, b, False) for a, b in pairs], axis=1).astype(low)
+    keep(p_wk, product(h_across, dk))
+    near[0].begin()
+    dq = join_rows(dq_back).astype(low)
+    keep(p_wq, product(h_across, dq))
+    near[1].begin()
+    dv = jnp.concatenate([join_tiles(a, b, True) for a, b in pairs], axis=1)
+    first_grad[...] = dv[:, fresh:]
+    dvf = dv[:, :fresh].astype(low)
+    keep(p_wv, product(h_across, dvf))
+    near[2].begin()
+    near[0].paired()
+    near[1].paired()
+    dh = product_right(dq, wq[...]) + product_right(dk, wk[...]) + product_right(dvf, wv[...])
+    near[2].paired()
+    normed, scale = normal_rows(x[...].astype(jnp.float32))
+
+    def total(v):
+        return jnp.sum(v, axis=0, keepdims=True)
+
+    sums = [total(dh * normed), total(dh), total(dq.astype(jnp.float32)), total(dvf.astype(jnp.float32)),
+            s_ob[...], s_gain2[...], s_bias2[...], s_eb[...], s_rb[...]]
+    devices = groups * n
+    spread = [spread_vector(v, devices).reshape(devices, 1, 128) for v in sums]
+    spread.append(jnp.zeros((devices, 16 - len(spread), 128), jnp.float32))
+    p_small[...] = jnp.concatenate(spread, axis=1).reshape(p_small.shape)
+    near[3].begin()
+    for level in range(len(powers(groups))):
+        for r in near[:3]:
+            r.crossed(level)
+    scaled = dh * gain[...].astype(jnp.float32)
+    inner = jnp.mean(scaled, axis=-1, keepdims=True)
+    along = jnp.mean(scaled * normed, axis=-1, keepdims=True)
+    token_grad[...] = dmid[...] + scale * (scaled - inner - normed * along)
+    near[3].paired()
+    for level in range(len(powers(groups))):
+        near[3].crossed(level)
+    for r in far:
+        r.finish()
+    for r in near:
+        r.finish()
+    for r in far + near:
+        r.drain()
 
     @pl.loop(0, heads)
     def _(j):
@@ -808,51 +879,78 @@
             copy.wait_send()
         for copy in ex.give_back(j, heads, dq_staged, dq_back, dq_send, dq_recv):
             copy.wait_send()
-        for t in range(n):
-            here(dq_back.at[t // splits * heads + j, t % splits], dq_recv.at[j, t])
-        for part in range(PARTS):
-            here(dkv_back.at[part * heads + j], dkv_recv.at[j, part])
-
-
-def backward_call(n, table, do_in, q_all, kv_all, ol_all):
+
+
+def backward_call(n, groups, table, do_in, q_all, kv_all, ol_all, hidden, x, gain, wq, wk, wv, dmid, sums, far):
     heads, _, rows, _ = kv_all.shape
     splits = n // PARTS
+    chips = n // 2
     share = rows // splits
+    width, fresh = wv.shape
     low = jnp.bfloat16
     vmem, dma = pltpu.VMEM, pltpu.SemaphoreType.DMA
     inside = pl.BlockSpec(memory_space=vmem)
     shape = jax.ShapeDtypeStruct
+    bits = powers(groups)
+    forth, back = bits, bits[::-1]
+    block = (groups, chips, 2)
+    part = width // (groups * n)
+    near = [block + (part, width, low), block + (part, width, low), block + (part, fresh, low),
+            block + (16, 128, jnp.float32)]
+    shapes = [f.shape + (low,) for f in far] + near
     return pl.pallas_call(
-        functools.partial(backward_kernel, n, heads),
-        out_shape=[
-            shape((PARTS * heads, splits, share // 2, 128), low),
-            shape((PARTS * heads, rows, 128), low),
-        ],
-        in_specs=[pl.BlockSpec(memory_space=pltpu.SMEM)] + [inside] * 4,
-        out_specs=[inside] * 2,
+        functools.partial(backward_kernel, n, groups, heads, [forth, back, forth][: len(far)], [back, forth, back, forth]),
+        out_shape=[shape((rows, width), jnp.float32), shape((rows, width - fresh), jnp.float32)]
+        + [shape(s[3:5], jnp.float32) for s in shapes],
+        in_specs=[pl.BlockSpec(memory_space=pltpu.SMEM)] + [inside] * 16 + [pl.BlockSpec(memory_space=pl.ANY)] * len(far),
+        out_specs=[inside] * (6 + len(far)),
         scratch_shapes=[
             vmem((heads, n, share // 2, 128), low),
             vmem((n, share // 2, 128), low),
             vmem((n, rows, 128), jnp.float32),
             vmem((n, share // 2, 128), low),
             vmem((heads, n, share // 2, 128), low),
-            vmem((heads, splits, PARTS, rows, 128), low),
-            vmem((heads, splits, PARTS, rows, 128), low),
+            vmem((heads, max(splits - 1, 1), PARTS, rows, 128), low),
+            vmem((heads, max(splits - 1, 1), PARTS, rows, 128), low),
             vmem((heads, PARTS, rows, 128), low),
+            vmem((PARTS * heads, splits, share // 2, 128), low),
+            vmem((PARTS * heads, rows, 128), low),
+        ]
+        + [vmem(s[:5], s[5]) for s in near]
+        + [
             dma((heads, n - 1)),
             dma((heads, n)),
             dma((heads, n - 1)),
             dma((heads, n)),
-            dma((heads, splits, PARTS)),
-            dma((heads, splits, PARTS)),
+            dma((heads, max(splits - 1, 1), PARTS)),
+            dma((heads, max(splits - 1, 1), PARTS)),
             dma((heads, PARTS - 1)),
             dma((heads, PARTS)),
-        ],
+        ]
+        + reduce_scratch(groups, chips, shapes),
         compiler_params=pltpu.CompilerParams(
-            collective_id=2, has_side_effects=True, vmem_limit_bytes=64000000
+            collective_id=2, has_side_effects=True, vmem_limit_bytes=67043328
         ),
         name="attention_backward",
-    )(table, do_in, q_all, kv_all, ol_all)
+    )(table, do_in, q_all, kv_all, ol_all, hidden, x, gain, wq, wk, wv, dmid, *sums, *far)
+
+
+def hand_over_kernel(count, sizes, *refs):
+    ins, outs = refs[: count + 1], refs[count + 1 :]
+    for i in range(count):
+        outs[i][...] = ins[i][...]
+    for row, size in enumerate(sizes):
+        outs[count + row][...] = ins[count][row : row + 1, :size]
+
+
+def hand_over(arrays, small, sizes):
+    shape = jax.ShapeDtypeStruct
+    return pl.pallas_call(
+        functools.partial(hand_over_kernel, len(arrays), sizes),
+        out_shape=[shape(a.shape, a.dtype) for a in arrays] + [shape((1, size), jnp.float32) for size in sizes],
+        compiler_params=pltpu.CompilerParams(vmem_limit_bytes=40000000),
+        name="hand_over",
+    )(*arrays, small)
 
 
 def collect(parts):
@@ -947,56 +1045,33 @@
     grad_output_bias = jnp.sum(grad_branch.astype(jnp.float32), axis=0)
     grad_output = product_left(attended_low, grad_branch)
     grad_attended = product_right(grad_branch, whole[7]).astype(jnp.bfloat16)
-    dq_back, dkv_back = backward_call(n, placement, pack_rows(grad_attended, splits), q_all, kv_all, ol_all)
-    grad_query_all = unpack_rows(dq_back)
-    heads = width // 64
-    pair = jnp.transpose(dkv_back.reshape(heads, rows, 2, 64), (2, 1, 0, 3)).reshape(2, rows, width)
-    fresh_width = whole[5].shape[1]
-    grad_key, grad_fresh = pair[0], pair[1][:, :fresh_width]
-    first_values_grad = pair[1][:, fresh_width:].astype(jnp.float32)[None]
-    grad_query_bias = jnp.sum(grad_query_all.astype(jnp.float32), axis=0)
-    grad_query_weight = product_left(hidden, grad_query_all)
-    grad_key_weight = product_left(hidden, grad_key)
-    grad_value_weight = product_left(hidden, grad_fresh)
-    grad_value_bias = jnp.sum(grad_fresh.astype(jnp.float32), axis=0)
-    grad_hidden = (
-        product_right(grad_query_all, whole[2])
-        + product_right(grad_key, whole[4])
-        + product_right(grad_fresh, whole[5])
+    block = (lax.axis_size("grp"), n // 2, 2)
+
+    def blocks(v):
+        return v.astype(jnp.bfloat16).reshape(block + (-1, v.shape[1]))
+
+    sums = [v[None] for v in (grad_gain_two, grad_bias_two, grad_output_bias, grad_expand_bias, grad_reduce_bias)]
+    far = [blocks(grad_expand), blocks(grad_reduce), blocks(grad_output)]
+    inside = far if n <= 8 else []
+    done = backward_call(
+        n, block[0], placement, pack_rows(grad_attended, splits), q_all, kv_all, ol_all, hidden, tokens[0],
+        whole[0][None], whole[2], whole[4], whole[5], grad_mid, sums,
+        inside,
     )
-    _, norm_one_back = jax.vjp(normalize, flat, gain_one, bias_one)
-    grad_in, grad_gain_one, grad_bias_one = norm_one_back(grad_hidden)
-    token_grad = (grad_in + grad_mid)[None]
-    owned = reduce_gradients((
-        grad_gain_one, grad_bias_one, grad_query_weight, grad_query_bias, grad_key_weight,
-        grad_value_weight, grad_value_bias, grad_output, grad_output_bias, grad_gain_two, grad_bias_two,
-        grad_expand, grad_expand_bias, grad_reduce, grad_reduce_bias,
-    ))
-    return (layer_output, token_grad, first_values_grad) + owned
-
-
-def reduce_gradients(grads):
-    groups = lax.axis_size("grp")
-    n = lax.axis_size("seq")
-    chips = n // 2
+    token_grad, first_grad = done[:2]
+    if not inside:
+        forth = powers(block[0])
+        done = done[:2] + reduce_call(block[0], block[1], far, [forth, forth[::-1], forth]) + done[2:]
+    g_we, g_wr, g_wo, g_wk, g_wq, g_wv, g_small = done[2:]
     small = (0, 1, 3, 6, 8, 9, 10, 12, 14)
-    large = (11, 13, 7, 4, 2, 5)
-    sizes = [grads[i].shape[0] // (groups * n) for i in small]
-    packed = jnp.concatenate([grads[i].reshape(groups * n, -1) for i in small], axis=1)
-    packed = jnp.pad(packed, ((0, 0), (0, 1024 - packed.shape[1]))).reshape(groups, chips, 2, 8, 128)
-    bits = powers(groups)
-    forth, back = bits, bits[::-1]
-    partials = [grads[i].astype(jnp.bfloat16).reshape(groups, chips, 2, -1, grads[i].shape[1]) for i in large]
-    shards = reduce_call(groups, chips, partials + [packed], [forth, back, forth, back, forth, back, forth])
-    out = [None] * 15
-    for i, shard in zip(large, shards):
-        out[i] = shard
-    flat = shards[-1].reshape(1024)
-    at = 0
-    for i, size in zip(small, sizes):
-        out[i] = flat[at : at + size]
-        at += size
-    return tuple(out)
+    sizes = [parts[i].shape[0] for i in small]
+    out = hand_over([token_grad, first_grad, g_wq, g_wk, g_wv, g_wo, g_we, g_wr], g_small, sizes)
+    owned = [None] * 15
+    for i, v in zip((2, 4, 5, 7, 11, 13), out[2:8]):
+        owned[i] = v
+    for i, v in zip(small, out[8:]):
+        owned[i] = v.reshape(-1)
+    return (layer_output, out[0][None], out[1][None]) + tuple(owned)
 
 
 def solution(mesh):

time: 508 us -> 369 us (0.73)
  Pallas kernels: 388 us -> 295 us
  local copies, waits for them, and re-layouts: 54.9 us -> 29.7 us
  matrix products: 49.7 us -> 36.3 us
  other arithmetic: 8.26 us -> 1.47 us
    pallas_call x2, Pallas kernels: 231 us -> 139 us  [the longest x1 137 us: backward_call(): pl.pallas_call(functools.partial(backward_kernel, n, groups, heads, [fort...]
    dot_general x6 -> x3, matrix products: 18.8 us -> 12.3 us  [product_left(): lax.dot_general(a, b, (((0,), (0,)), ((), ())), preferred_element_type=jn...]
    dot_general x6 -> x3, matrix products: 18.6 us -> 12.1 us  [product_right(): lax.dot_general(a, b, (((1,), (1,)), ((), ())), preferred_element_type=jn...]
    slice x4 -> x0, local copies, waits for them, and re-layouts: 6.44 us -> none  [the longest x3 4.08 us: reduce_gradients(): out[i] = flat[at:at + size]]
    pallas_call x2 -> x0, local copies, waits for them, and re-layouts: 5.1 us -> none  [backward_call(): pl.pallas_call(functools.partial(backward_kernel, n, heads), out_shape=[s...]
    unnamed x50 -> x35, local copies, waits for them, and re-layouts: 14.3 us -> 9.87 us
where the time goes in v3:
time: 369 us; the launch traced here: 364 us
  Pallas kernels  295 us (80%)
  matrix products  36.3 us (10%)
  local copies, waits for them, and re-layouts  29.7 us (8%)
    pallas_call x1, Pallas kernels, backward_call(): pl.pallas_call(functools.partial(backward_kernel, n, groups, heads, [fort...  137 us
    pallas_call x1, Pallas kernels, forward_call(): pl.pallas_call(functools.partial(forward_kernel, n, heads), out_shape=[sh...  79.9 us
    pallas_call x1, Pallas kernels, gather_call(): pl.pallas_call(functools.partial(gather_kernel, groups, chips, orders), o...  76.2 us
    dot_general x3, matrix products, product_left(): lax.dot_general(a, b, (((0,), (0,)), ((), ())), preferred_element_type=jn...  12.3 us
    dot_general x3, matrix products, product_right(): lax.dot_general(a, b, (((1,), (1,)), ((), ())), preferred_element_type=jn...  12.1 us
    dot_general x3, matrix products, product(): lax.dot_general(a, b, (((1,), (0,)), ((), ())), preferred_element_type=jn...  12 us
    unnamed x35, local copies, waits for them, and re-layouts  9.87 us

profile of v3, /device:TPU:0, one launch (start us, length us, event | category | flops | bytes accessed | tf_op | source)
XLA Modules:
  0.0 363.5 jit_solution(18422212788316921235)
XLA Ops:
  0.7 6.1 %concatenate.3 = bf16[276]{0:T(512)(128)(2,1)S(1)} concatenate(bf16[24]{0:T(256)(128)(2,1)} %param.23, bf16[24]{0:T(256)(128)(2,1)} %param.24, bf16[24]{0:T(256)(128)(2,1)} %param.26, bf16[12]{0:T(256)(128)(2,1)} %param.29, bf16[24]{0:T(256)(128)(2,1)} %param.31, bf16[24]{0:T(256)(128)(2,1)} %param.32, bf16[24]{0:T(256)(128)(2,1)} %param.33, bf16[96]{0:T(256)(128)(2,1)} %param.35, ...), dimensions={0} | concatenate | bytes 1104 | tf_op jit(solution)/shard_map/concatenate | solution.py:960
  6.8 0.6 pad_bitcast_fusion.refs_0_
  7.4 76.2 %gather_parameters.1 = (bf16[4,4,2,16,128]{4,3,2,1,0:T(8,128)(2,1)}, bf16[4,4,2,24,768]{4,3,2,1,0:T(8,128)(2,1)}, bf16[4,4,2,24,384]{4,3,2,1,0:T(8,128)(2,1)}, b...) custom-call(bf16[16,128]{1,0:T(8,128)(2,1)} %pad_bitcast_fusion.refs, ...), custom_call_target="tpu_custom_call" | custom-call | tf_op jit(solution)/shard_map/gather_parameters/pallas_call | solution.py:200
  83.6 0.9 copy.45
  84.5 0.1 slice.39
  84.6 0.7 broadcast_in_dim_reshape.16.bv
  85.3 0.1 slice_convert_fusion.1
  85.3 0.1 slice_convert_fusion.3
  85.4 0.1 reshape.211
  85.5 0.1 reshape.209
  85.6 0.7 broadcast_in_dim_reshape.13.gain
  86.3 0.7 broadcast_in_dim_reshape.15.bq
  86.9 0.7 broadcast_in_dim_reshape.14.shift
  87.6 0.1 reshape.210
  87.7 0.1 reshape.212
  87.8 0.1 reshape.208
  87.9 79.9 %attention_forward.1 = (bf16[512,768]{1,0:T(8,128)(2,1)}, bf16[3,8,128,128]{3,2,1,0:T(8,128)(2,1)}, bf16[3,8,512,128]{3,2,1,0:T(8,128)(2,1)}, f32[3,8,256,128]{3,2,1,0:T(8,128)}, bf16[12,2,128,128]{3,2,1,0:T(8,128)(2,1)}) custom-call(s32[1,8]{1,0:T(1,128)} %table.3, bf16[512,768]{1,0:T(8,128)(2,1)} %bitcast.82, bf16[512,384]{1,0:T(8,128)(2,1)} %bitcast.89, ...), custom_call_target="tpu_custom_call" | custom-call | tf_op jit(solution)/shard_map/attention_forward/pallas_call | solution.py:619
  167.8 0.0 copy-start.10
  167.8 1.6 copy.38
  169.4 0.8 copy.39
  170.2 0.3 reshape.188
  170.5 0.0 copy-done.10
  170.5 2.2 fusion.18
  172.8 0.0 slice-start.2
  172.8 0.3 multiply_reduce_fusion.2
  173.1 0.0 slice-start.3
  173.1 4.9 %fusion.16 = f32[512,3072]{1,0:T(8,128)S(1)} fusion(bf16[768,3072]{1,0:T(8,128)(2,1)} %bitcast.95, f32[512,768]{1,0:T(8,128)S(1)} %get-tuple-element.110, f32[768]{0:T(1024)S(1)} %reshape.210, f32[768]{0:T(1024)S(1)} %reshape.209, f32[512]{0:T(512)S(1)} %fusion.13, f32[512]{0:T(512)S(1)} %broadcast_multiply_fusion), kind=kOutput, calls=%fused_computation.47 | convolution fusion | flops 2417885184 | bytes 12593152 | tf_op jit(solution)/shard_map/dot_general | solution.py:387
  178.0 0.0 slice-done.2
  178.0 0.0 slice-done.3
  178.0 0.0 copy-start.11
  178.0 0.0 slice-start
  178.0 4.9 %fusion.10 = bf16[1,512,768]{2,1,0:T(8,128)(2,1)} fusion(f32[512,768]{1,0:T(8,128)S(1)} %get-tuple-element.110, bf16[3072,768]{1,0:T(8,128)(2,1)S(1)} %bitcast.101, f32[768]{0:T(1024)S(1)} %reshape.212, f32[512,3072]{1,0:T(8,128)S(1)} %fusion.16, f32[3072]{0:T(1024)S(1)} %reshape.211), kind=kOutput, calls=%fused_computation.30 | convolution fusion | flops 2432827392 | bytes 13384704 | tf_op jit(solution)/shard_map/dot_general | solution.py:387
  182.9 0.0 copy-done.11
  182.9 7.4 %convert_reduce_fusion = (f32[3072]{0:T(1024)}, bf16[512,3072]{1,0:T(8,128)(2,1)S(1)}) fusion(f32[512,3072]{1,0:T(8,128)S(1)} %fusion.16, f32[3072]{0:T(1024)S(1)} %reshape.211, bf16[3072,768]{1,0:T(8,128)(2,1)S(1)} %bitcast.102, bf16[1,512,768]{2,1,0:T(8,128)(2,1)S(1)} %copy-done.11), kind=kOutput, calls=%fused_computation.14 | convolution fusion | flops 2452091904 | bytes 14966784 | tf_op jit(solution)/shard_map/dot_general | solution.py:391
  190.3 5.5 %convolution_convert_fusion = bf16[3072,768]{1,0:T(8,128)(2,1)} fusion(bf16[1,512,768]{2,1,0:T(8,128)(2,1)S(1)} %copy-done.11, f32[512,3072]{1,0:T(8,128)S(1)} %fusion.16, f32[3072]{0:T(1024)S(1)} %reshape.211), kind=kOutput, calls=%fused_computation.16 | convolution fusion | flops 2434007040 | bytes 11808768 | tf_op jit(solution)/shard_map/dot_general | solution.py:395
  195.8 0.0 slice-done
  195.8 0.0 slice-done.1
  195.8 3.0 multiply_reduce_fusion
  198.8 0.6 reshape.194.s_gain2
  199.4 0.6 fusion.17
  200.1 5.0 %convolution_convert_fusion.1 = bf16[768,3072]{1,0:T(8,128)(2,1)} fusion(bf16[512,3072]{1,0:T(8,128)(2,1)S(1)} %get-tuple-element.113, f32[512,768]{1,0:T(8,128)S(1)} %get-tuple-element.110, f32[768]{0:T(1024)S(1)} %reshape.210, f32[768]{0:T(1024)S(1)} %reshape.209, f32[512]{0:T(512)S(1)} %fusion.13, f32[512]{0:T(512)S(1)} %broadcast_multiply_fusion), kind=kOutput, calls=%fused_computation.17 | convolution fusion | flops 2420244480 | bytes 9447424 | tf_op jit(solution)/shard_map/dot_general | solution.py:395
  205.0 0.6 reshape.195.s_bias2
  205.6 0.3 convert_reduce_fusion.2
  206.0 0.0 copy-start.9
  206.0 0.3 copy-done.12
  206.3 1.7 convolution_convert_fusion.3
  208.0 1.4 copy.40
  209.4 1.1 reshape.192
  210.5 1.3 copy.41
  211.8 1.2 copy.42.do_in
  213.0 0.6 broadcast_in_dim.36.s_ob
  213.6 0.6 broadcast_in_dim.38.s_rb
  214.2 1.8 convolution_convert_fusion.2
  216.0 136.9 %attention_backward.1 = (f32[512,768]{1,0:T(8,128)}, f32[512,384]{1,0:T(8,128)}, f32[24,3072]{1,0:T(8,128)}, f32[96,768]{1,0:T(8,128)}, f32[24,768]{1,0:T(8,128)...) custom-call(s32[1,8]{1,0:T(1,128)} %table.3, ...), custom_call_target="tpu_custom_call" | custom-call | tf_op jit(solution)/shard_map/attention_backward/pallas_call | solution.py:901
  352.9 1.4 copy-done
  354.3 1.1 copy-done.1
  355.4 1.0 copy-done.2
  356.4 1.0 copy-done.3
  357.3 0.9 copy-done.4
  358.2 0.9 copy-done.5
  359.1 0.9 copy-done.6
  360.0 0.8 copy-done.7
  360.7 0.7 copy-done.8
  361.4 1.9 hand_over.1
  (18 shorter events, 0.0 us)
Async XLA Ops:
  167.8 2.7 copy-start.10
  172.8 5.2 %slice-start.2 = ((s8[4718592]{0:T(1024)(128)(4,1)}), s8[4194304]{0:T(1024)(128)(4,1)S(1)}, s32[]{:S(2)}) async-start(s8[4718592]{0:T(1024)(128)(4,1)} %bitcast.99), calls=%async_computation.2 | async-start | bytes 8388608
  173.1 4.9 %slice-start.3 = ((s8[4718592]{0:T(1024)(128)(4,1)}), s8[524288]{0:T(1024)(128)(4,1)S(1)}, s32[]{:S(2)}) async-start(s8[4718592]{0:T(1024)(128)(4,1)} %bitcast.99), calls=%async_computation.3 | async-start | bytes 1048576
  178.0 4.9 %copy-start.11 = (bf16[1,512,768]{2,1,0:T(8,128)(2,1)S(1)}, bf16[1,512,768]{2,1,0:T(8,128)(2,1)}, u32[]{:S(2)}) copy-start(bf16[1,512,768]{2,1,0:T(8,128)(2,1)} %param.22) | copy-start | bytes 2359300
  178.0 17.8 %slice-start = ((s8[4718592]{0:T(1024)(128)(4,1)}), s8[4194304]{0:T(1024)(128)(4,1)S(1)}, s32[]{:S(2)}) async-start(s8[4718592]{0:T(1024)(128)(4,1)} %bitcast.96), calls=%async_computation | async-start | bytes 8388608
  182.9 12.9 %slice-start.1 = ((s8[4718592]{0:T(1024)(128)(4,1)}), s8[524288]{0:T(1024)(128)(4,1)S(1)}, s32[]{:S(2)}) async-start(s8[4718592]{0:T(1024)(128)(4,1)} %bitcast.96), calls=%async_computation.1 | async-start | bytes 1048576
  205.0 1.3 copy-start.12
  206.0 8.2 %copy-start.9 = (f32[512,768]{1,0:T(8,128)}, f32[512,768]{1,0:T(8,128)S(1)}, u32[]{:S(2)}) copy-start(f32[512,768]{1,0:T(8,128)S(1)} %get-tuple-element.98.dmid) | copy-start | bytes 4718596
  352.8 1.4 copy-start
  354.3 1.1 copy-start.1
  355.4 1.0 copy-start.2
  356.3 1.0 copy-start.3
  357.3 0.9 copy-start.4
  358.2 0.9 copy-start.5
  359.1 0.9 copy-start.6
  360.0 0.8 copy-start.7
  360.7 0.7 copy-start.8

commit v4 on v3

--- a/solution.py
+++ b/solution.py
@@ -1,4 +1,5 @@
 import functools
+import math
 
 import jax
 import jax.numpy as jnp
@@ -70,6 +71,10 @@
         pltpu.make_async_copy(self.block(g, z, self.c), self.block(g, z, self.c), self.recv.at[g, z]).wait()
 
     def begin(self):
+        self.begin_chain()
+        self.begin_cross()
+
+    def begin_chain(self):
         copy = pltpu.make_async_copy(self.shard, self.block(self.g, self.z, self.c), self.own)
         copy.start()
 
@@ -81,6 +86,7 @@
         def _():
             self.chain(self.z, 1, True).start()
 
+    def begin_cross(self):
         for level in range(len(self.bits)):
             self.cross(level, 0, self.z, True).start()
 
@@ -98,6 +104,10 @@
             body(self.z + distance, -1)
 
     def along(self, distance):
+        self.along_chain(distance)
+        self.along_cross(distance)
+
+    def along_chain(self, distance):
         def body(z, step):
             self.here(0, z)
             onward = self.z < self.chips - 1 if step > 0 else self.z > 0
@@ -106,11 +116,14 @@
             def _():
                 self.chain(z, step, False).start()
 
+        self.at(distance, body)
+
+    def along_cross(self, distance):
+        def body(z, step):
             for level in range(len(self.bits)):
                 self.cross(level, 0, z, False).start()
 
-        if distance > 0:
-            self.at(distance, body)
+        self.at(distance, body)
 
     def over(self, level, distance):
         def body(z, step):
@@ -491,25 +504,97 @@
     pltpu.make_async_copy(ref, ref, sem).wait()
 
 
-def forward_kernel(
-    n, heads, table, x, first, gain, shift, wq, bq, wk, wv, bv,
-    hidden_out, q_all, kv_all, ol_all, back,
-    q_staged, kv_staged, o_staged, q_work, kv_work,
-    q_send, kv_send, relay_send, o_send, q_recv, kv_recv, o_recv,
-):
+def gather_vector(full, row, size):
+    count = full.shape[0]
+    part = size // count
+    rows = full[:, row, :].astype(jnp.bfloat16)
+    at = lax.broadcasted_iota(jnp.int32, (128, size), 0)
+    to = lax.broadcasted_iota(jnp.int32, (128, size), 1)
+    place = jnp.where(lax.rem(to, part) == at, 1.0, 0.0).astype(jnp.bfloat16)
+    spread = product(rows, place)
+    lane = lax.broadcasted_iota(jnp.int32, (count, size), 1)
+    owner = lax.broadcasted_iota(jnp.int32, (count, size), 0)
+    mine = (lane >= owner * part) & (lane < owner * part + part)
+    return jnp.sum(jnp.where(mine, spread, 0.0), axis=0, keepdims=True)
+
+
+def forward_kernel(n, groups, heads, orders, sizes, table, x, first, *refs):
+    vectors, shards, refs = refs[:9], refs[9:15], refs[15:]
+    hidden_out, q_all, kv_all, ol_all, back = refs[:5]
+    fulls, vectors_out, refs = refs[5:11], refs[11:20], refs[20:]
+    packed, small_full, q_staged, kv_staged, o_staged, q_work, kv_work = refs[:7]
+    q_send, kv_send, relay_send, o_send, q_recv, kv_recv, o_recv = refs[7:14]
+    sems = refs[14:]
     ex = Exchange(n)
-    enter(ex.peers())
+    chips = n // 2
+    bits = powers(groups)
+    levels = len(bits)
+    enter(ex.peers() + [{"grp": lax.axis_index("grp") ^ bit} for bit in bits])
+    gathers = [
+        Gather(groups, chips, order, shard, full, *[s.at[i] for s in sems])
+        for i, (order, shard, full) in enumerate(zip(orders, (packed,) + shards, (small_full,) + fulls))
+    ]
+    near, far = gathers[:4], gathers[4:]
+    packed[...] = jnp.zeros(packed.shape, jnp.float32)
+    for row, vector in enumerate(vectors):
+        packed[row : row + 1, : vector.shape[1]] = vector[...].astype(jnp.float32)
+    for g in (near[1], near[2], near[3], near[0]):
+        g.begin()
     splits = ex.splits
     rows, width = x.shape
     share = rows // splits
     half = n // 2
-    fresh = wv.shape[1]
+    fresh = width - first.shape[1]
     normed, _ = normal_rows(x[...].astype(jnp.float32))
-    hidden = (normed * gain[...].astype(jnp.float32) + shift[...].astype(jnp.float32)).astype(jnp.bfloat16)
+
+    def steps(some, along=1):
+        out = []
+        for distance in range(chips + levels):
+            for g in some:
+                if along == 1 and distance + 1 < chips:
+                    out.append(functools.partial(g.along, distance + 1))
+                if along == 2 and 2 <= distance + 1 < chips:
+                    out.append(functools.partial(g.along_cross, distance + 1))
+                for level in range(levels):
+                    if 0 <= distance - level < chips:
+                        out.append(functools.partial(g.over, level, distance - level))
+        return out
+
+    order = steps(near)
+    cut = (min(len(order), len(near) * (1 + levels)), 3 * len(order) // 4)
+    for step in order[: cut[0]]:
+        step()
+    for g in far:
+        g.begin_chain()
+    for step in order[cut[0] : cut[1]]:
+        step()
+    if chips > 1:
+        for g in far:
+            g.along_chain(1)
+    for step in order[cut[1] :]:
+        step()
+    for g in near:
+        g.swap()
+    for g in far:
+        g.begin_cross()
+    for distance in range(1, min(2, chips)):
+        for g in far:
+            g.along_cross(distance)
+    for distance in range(2, chips):
+        for g in far:
+            g.along_chain(distance)
+    for g in near:
+        g.finish()
+    small = small_full[...].reshape((2 * chips * groups,) + packed.shape)
+    for row in range(4):
+        vectors_out[row][...] = gather_vector(small, row, sizes[row])
+    gain, shift, bq, bv = vectors_out[:4]
+    wq, wk, wv = [fulls[i][...].reshape(width, -1) for i in range(3)]
+    hidden = (normed * gain[...] + shift[...]).astype(jnp.bfloat16)
     hidden_out[...] = hidden
     for step in range(width // 256):
         cols = slice(step * 256, (step + 1) * 256)
-        q = product(hidden, wq[:, cols]) + bq[:, cols].astype(jnp.float32)
+        q = product(hidden, wq[:, cols]) + bq[:, cols]
 
         def store(head, split, v, step=step):
             head = head + 4 * step
@@ -520,7 +605,7 @@
         for tile in range(2):
             at = step * 256 + tile * 128
             if at < fresh:
-                v = product(hidden, wv[:, at : at + 128]) + bv[:, at : at + 128].astype(jnp.float32)
+                v = product(hidden, wv[:, at : at + 128]) + bv[:, at : at + 128]
             else:
                 v = first[:, at - fresh : at - fresh + 128].astype(jnp.float32)
             kt = k[:, tile * 128 : (tile + 1) * 128]
@@ -562,6 +647,13 @@
         out = out / denom
         ol_all[j, place] = jnp.where(lanes(out.shape) < 64, top + jnp.log(denom), out)
 
+    later = steps(far, 2)
+    cut = (len(later) // 2, 3 * len(later) // 4)
+    for step in later[: cut[0]]:
+        step()
+    for row in range(4, 9):
+        vectors_out[row][...] = gather_vector(small, row, sizes[row])
+
     @pl.loop(0, heads)
     def _(j):
         for off in range(PARTS):
@@ -591,6 +683,18 @@
             copy.start()
         ex.keep_own(j, heads, o_staged, back, o_recv).start()
 
+        @pl.when(j == 0)
+        def _():
+            for step in later[cut[0] : cut[1]]:
+                step()
+
+        @pl.when(j == min(1, heads - 1))
+        def _():
+            for step in later[cut[1] :]:
+                step()
+            for g in far:
+                g.swap()
+
     @pl.loop(0, heads)
     def _(j):
         for copy in ex.spread(j, kv_staged, kv_all, kv_send, kv_recv):
@@ -605,29 +709,40 @@
         for t in range(n):
             landed = back.at[t // splits * heads + j, t % splits]
             here(landed, o_recv.at[j, t])
-
-
-def forward_call(n, table, x, first, gain, shift, wq, bq, wk, wv, bv):
+    for g in far:
+        g.finish()
+
+
+def forward_call(n, groups, table, x, first, vectors, shards):
     rows, width = x.shape
     splits = n // PARTS
+    chips = n // 2
     heads = width // 64 // PARTS
     share = rows // splits
     low = jnp.bfloat16
     vmem, dma = pltpu.VMEM, pltpu.SemaphoreType.DMA
-    inside = pl.BlockSpec(memory_space=vmem)
+    inside, outside = pl.BlockSpec(memory_space=vmem), pl.BlockSpec(memory_space=pl.ANY)
     shape = jax.ShapeDtypeStruct
+    bits = powers(groups)
+    forth, behind = bits, bits[::-1]
+    sizes = [v.shape[1] * groups * n for v in vectors]
+    block = (groups, chips, 2)
     return pl.pallas_call(
-        functools.partial(forward_kernel, n, heads),
+        functools.partial(forward_kernel, n, groups, heads, [forth, forth, behind, forth, behind, forth, behind], sizes),
         out_shape=[
             shape((rows, width), low),
             shape((heads, n, share // 2, 128), low),
             shape((heads, n, rows, 128), low),
             shape((heads, n, share, 128), jnp.float32),
             shape((PARTS * heads, splits, share // 2, 128), low),
-        ],
-        in_specs=[pl.BlockSpec(memory_space=pltpu.SMEM)] + [inside] * 9,
-        out_specs=[inside] * 5,
+        ]
+        + [shape(block + w.shape, low) for w in shards]
+        + [shape((1, size), jnp.float32) for size in sizes],
+        in_specs=[pl.BlockSpec(memory_space=pltpu.SMEM)] + [inside] * 11 + [outside] * 6,
+        out_specs=[inside] * 8 + [outside] * 3 + [inside] * 9,
         scratch_shapes=[
+            vmem((16, 128), jnp.float32),
+            vmem(block + (16, 128), jnp.float32),
             vmem((PARTS, heads, splits, share // 2, 128), low),
             vmem((PARTS, heads, rows, 128), low),
             vmem((heads, n, share // 2, 128), low),
@@ -640,12 +755,13 @@
             dma((heads, n)),
             dma((heads, n)),
             dma((heads, n)),
-        ],
+        ]
+        + gather_semaphores(7, groups, chips),
         compiler_params=pltpu.CompilerParams(
             collective_id=1, has_side_effects=True, vmem_limit_bytes=64000000
         ),
         name="attention_forward",
-    )(table, x, first, gain, shift, wq, bq, wk, wv, bv)
+    )(table, x, first, *vectors, *shards)
 
 
 def join_tiles(even, odd, high):
@@ -936,69 +1052,159 @@
 
 
 def hand_over_kernel(count, sizes, *refs):
-    ins, outs = refs[: count + 1], refs[count + 1 :]
+    ins, outs = refs[:count], refs[count + 1 : 2 * count + 1]
+    held, loads, stores = refs[2 * count + 1 + len(sizes) : -2], refs[-2], refs[-1]
     for i in range(count):
-        outs[i][...] = ins[i][...]
+        pltpu.make_async_copy(ins[i], held[i], loads.at[i]).start()
     for row, size in enumerate(sizes):
-        outs[count + row][...] = ins[count][row : row + 1, :size]
+        refs[2 * count + 1 + row][...] = refs[count][row : row + 1, :size]
+    for i in range(count):
+        pltpu.make_async_copy(ins[i], held[i], loads.at[i]).wait()
+        pltpu.make_async_copy(held[i], outs[i], stores.at[i]).start()
+    for i in range(count):
+        pltpu.make_async_copy(held[i], outs[i], stores.at[i]).wait()
 
 
 def hand_over(arrays, small, sizes):
     shape = jax.ShapeDtypeStruct
+    count = len(arrays)
+    inside, outside = pl.BlockSpec(memory_space=pltpu.VMEM), pl.BlockSpec(memory_space=pl.ANY)
     return pl.pallas_call(
-        functools.partial(hand_over_kernel, len(arrays), sizes),
+        functools.partial(hand_over_kernel, count, sizes),
         out_shape=[shape(a.shape, a.dtype) for a in arrays] + [shape((1, size), jnp.float32) for size in sizes],
-        compiler_params=pltpu.CompilerParams(vmem_limit_bytes=40000000),
+        in_specs=[outside] * count + [inside],
+        out_specs=[outside] * count + [inside] * len(sizes),
+        scratch_shapes=[pltpu.VMEM(a.shape, a.dtype) for a in arrays]
+        + [pltpu.SemaphoreType.DMA((count,)), pltpu.SemaphoreType.DMA((count,))],
+        compiler_params=pltpu.CompilerParams(vmem_limit_bytes=60000000),
         name="hand_over",
     )(*arrays, small)
 
 
-def collect(parts):
-    groups = lax.axis_size("grp")
-    n = lax.axis_size("seq")
-    small = (0, 1, 3, 6, 8, 9, 10, 12, 14)
-    packed = jnp.concatenate([parts[i] for i in small])
-    sizes = [parts[i].shape[0] for i in small]
-    length = packed.shape[0]
-    packed = jnp.pad(packed, (0, 2048 - length)).reshape(16, 128)
-    bits = powers(groups)
-    forth, back = bits, bits[::-1]
-    shards = [packed, parts[2], parts[5], parts[4], parts[7], parts[11], parts[13]]
-    fulls = gather_call(groups, n // 2, shards, [forth, forth, forth, back, back, forth, back])
-    flat = fulls[0].reshape(groups * n, 2048)
-    whole = [None] * 15
-    at = 0
-    for i, size in zip(small, sizes):
-        whole[i] = flat[:, at : at + size].reshape(groups * n * size)
-        at += size
-    for i, full in zip((2, 5, 4, 7, 11, 13), fulls[1:]):
-        whole[i] = full.reshape(-1, full.shape[-1])
-    return tuple(whole)
-
-
-def normalize(v, gain, shift):
-    mean = jnp.mean(v, axis=-1, keepdims=True)
-    centred = v - mean
-    var = jnp.mean(centred * centred, axis=-1, keepdims=True)
-    return centred * lax.rsqrt(var + EPS) * gain + shift
-
-
-def gelu_tanh(v):
-    return jax.nn.gelu(v, approximate=True)
-
-
-def unpack_rows(v):
-    heads, splits, size, _ = v.shape
-    v = v.reshape(heads, splits, size, 2, 64)
-    return jnp.transpose(v, (1, 3, 2, 0, 4)).reshape(splits * 2 * size, heads * 64)
-
-
-def pack_rows(v, splits):
-    rows, width = v.shape
-    heads = width // 64
-    v = v.reshape(splits, 2, rows // splits // 2, heads, 64)
-    v = jnp.transpose(v, (3, 0, 2, 1, 4))
-    return v.reshape(PARTS, heads // PARTS, splits, rows // splits // 2, 128)
+def feed_kernel(
+    parts, heads, back, x, dy, bo, gain, shift, be, br, wo_in, we_in, wr_in,
+    out, dmid_out, do_staged, s_gain, s_shift, s_ob, s_eb, s_rb, g_we, g_wr, g_wo,
+    wo, we, wr, k_we, k_wr, k_wo, dh, load, keep,
+):
+    low = jnp.bfloat16
+    rows, width = x.shape
+    step = we.shape[1] // parts
+    splits = back.shape[1]
+
+    def total(v):
+        return jnp.sum(v, axis=0, keepdims=True)
+
+    def columns(c):
+        return pl.ds(pl.multiple_of(c * step, 128), step)
+
+    def fetch(c):
+        return (pltpu.make_async_copy(we_in.at[:, columns(c)], we.at[:, columns(c)], load.at[c]),
+                pltpu.make_async_copy(wr_in.at[columns(c)], wr.at[columns(c)], load.at[parts + c]))
+
+    def store(c):
+        return (pltpu.make_async_copy(k_we.at[:, columns(c)], g_we.at[:, columns(c)], keep.at[c]),
+                pltpu.make_async_copy(k_wr.at[columns(c)], g_wr.at[columns(c)], keep.at[parts + c]))
+
+    first = pltpu.make_async_copy(wo_in, wo, load.at[2 * parts])
+    first.start()
+    for c in range(parts):
+        for copy in fetch(c):
+            copy.start()
+    att = join_rows(back).astype(low)
+    first.wait()
+    mid = x[...].astype(jnp.float32) + product(att, wo[...]) + bo[...]
+    normed, scale = normal_rows(mid)
+    second = (normed * gain[...] + shift[...]).astype(low)
+    second_across = jnp.transpose(second)
+    seed = dy[...]
+    seed_full = seed.astype(jnp.float32)
+    s_rb[...] = total(seed_full)
+    dmid_out[...] = mid + br[...]
+    dh[...] = jnp.zeros((rows, width), jnp.float32)
+
+    @pl.loop(0, parts)
+    def _(c):
+        for copy in fetch(c):
+            copy.wait()
+        expand, reduce = we[:, columns(c)], wr[columns(c)]
+        u = product(second, expand) + be[:, columns(c)]
+        square = u * u
+        t = jnp.tanh(math.sqrt(2 / math.pi) * (u + 0.044715 * (u * square)))
+        z = (0.5 * u * (1.0 + t)).astype(low)
+        slope = 0.5 * (1.0 + t) + (0.5 * math.sqrt(2 / math.pi)) * u * (1.0 - t * t) * (1.0 + (3 * 0.044715) * square)
+        du_full = (slope * product_right(seed, reduce)).astype(low)
+        s_eb[:, columns(c)] = total(du_full.astype(jnp.float32))
+        dmid_out[...] += product(z, reduce)
+        dh[...] += product_right(du_full, expand)
+        k_wr[columns(c)] = product(jnp.transpose(z), seed).astype(low)
+        k_we[:, columns(c)] = product(second_across, du_full).astype(low)
+        for copy in store(c):
+            copy.start()
+
+    out[...] = dmid_out[...].astype(low)
+    back_normed = dh[...]
+    s_gain[...] = total(back_normed * normed)
+    s_shift[...] = total(back_normed)
+    scaled = back_normed * gain[...]
+    inner = jnp.mean(scaled, axis=-1, keepdims=True)
+    along = jnp.mean(scaled * normed, axis=-1, keepdims=True)
+    dmid = seed_full + scale * (scaled - inner - normed * along)
+    dmid_out[...] = dmid
+    branch = dmid.astype(low)
+    s_ob[...] = total(branch.astype(jnp.float32))
+    k_wo[...] = product(jnp.transpose(att), branch).astype(low)
+    last = pltpu.make_async_copy(k_wo, g_wo, keep.at[2 * parts])
+    last.start()
+    for group in range(width // 256):
+        datt = product_right(branch, wo[group * 256 : (group + 1) * 256, :])
+
+        def put(head, split, v, group=group):
+            head = head + 4 * group
+            do_staged[head // heads, head % heads, split] = v.astype(low)
+
+        pack_heads(datt, splits, put)
+    for c in range(parts):
+        for copy in store(c):
+            copy.wait()
+    last.wait()
+
+
+def feed_call(back, x, dy, bo, gain, shift, be, br, wo, we, wr):
+    rows, width = x.shape
+    inner = we.shape[1]
+    parts = inner // width
+    heads = back.shape[0] // PARTS
+    splits = back.shape[1]
+    low, full = jnp.bfloat16, jnp.float32
+    vmem, dma = pltpu.VMEM, pltpu.SemaphoreType.DMA
+    inside, outside = pl.BlockSpec(memory_space=vmem), pl.BlockSpec(memory_space=pl.ANY)
+    shape = jax.ShapeDtypeStruct
+    return pl.pallas_call(
+        functools.partial(feed_kernel, parts, heads),
+        out_shape=[
+            shape((rows, width), low),
+            shape((rows, width), full),
+            shape((PARTS, heads) + back.shape[1:], low),
+            shape((1, width), full),
+            shape((1, width), full),
+            shape((1, width), full),
+            shape((1, inner), full),
+            shape((1, width), full),
+            shape(we.shape, low),
+            shape(wr.shape, low),
+            shape(wo.shape, low),
+        ],
+        in_specs=[inside] * 8 + [outside] * 3,
+        out_specs=[inside] * 8 + [outside] * 3,
+        scratch_shapes=[
+            vmem(wo.shape, low), vmem(we.shape, low), vmem(wr.shape, low),
+            vmem(we.shape, low), vmem(wr.shape, low), vmem(wo.shape, low),
+            vmem((rows, width), full),
+            dma((2 * parts + 1,)), dma((2 * parts + 1,)),
+        ],
+        compiler_params=pltpu.CompilerParams(vmem_limit_bytes=64000000),
+        name="feed_forward",
+    )(back, x, dy, bo, gain, shift, be, br, wo, we, wr)
 
 
 def body(
@@ -1010,52 +1216,26 @@
 ):
     groups, rows, width = tokens.shape
     n = lax.axis_size("seq")
-    splits = n // PARTS
-    whole = collect(parts)
-    gain_one = whole[0].astype(jnp.float32)
-    bias_one = whole[1].astype(jnp.float32)
-    gain_two = whole[9].astype(jnp.float32)
-    bias_two = whole[10].astype(jnp.float32)
-    hidden, q_all, kv_all, ol_all, back = forward_call(
-        n, placement, tokens[0], first_values[0], whole[0][None], whole[1][None],
-        whole[2], whole[3][None], whole[4], whole[5], whole[6][None],
+    small = (0, 1, 3, 6, 8, 9, 10, 12, 14)
+    large = (2, 4, 5, 7, 11, 13)
+    done = forward_call(n, lax.axis_size("grp"), placement, tokens[0], first_values[0],
+                        [parts[i][None] for i in small], [parts[i] for i in large])
+    hidden, q_all, kv_all, ol_all, back = done[:5]
+    whole = [None] * 15
+    for i, v in zip(large, done[5:11]):
+        whole[i] = v.reshape(-1, v.shape[-1])
+    for i, v in zip(small, done[11:]):
+        whole[i] = v[0]
+    layer_output, dmid, do_staged, *sums, g_we, g_wr, g_wo = feed_call(
+        back, tokens[0], cotangent[0], whole[8][None], whole[9][None], whole[10][None], whole[12][None],
+        whole[14][None], whole[7], whole[11], whole[13],
     )
-    attended_low = unpack_rows(back)
-    flat = tokens[0].astype(jnp.float32)
-    middle = flat + product(attended_low, whole[7]) + whole[8].astype(jnp.float32)
-    normed_two, norm_two_back = jax.vjp(normalize, middle, gain_two, bias_two)
-    second = normed_two.astype(jnp.bfloat16)
-    pre = product(second, whole[11]) + whole[12].astype(jnp.float32)
-    post_full, gelu_back = jax.vjp(gelu_tanh, pre)
-    post = post_full.astype(jnp.bfloat16)
-    result = middle + product(post, whole[13]) + whole[14].astype(jnp.float32)
-    layer_output = result.astype(jnp.bfloat16)[None]
-    seed = cotangent[0]
-    seed_full = seed.astype(jnp.float32)
-    grad_reduce_bias = jnp.sum(seed_full, axis=0)
-    grad_reduce = product_left(post, seed)
-    grad_post = product_right(seed, whole[13])
-    grad_pre = gelu_back(grad_post)[0].astype(jnp.bfloat16)
-    grad_expand_bias = jnp.sum(grad_pre.astype(jnp.float32), axis=0)
-    grad_expand = product_left(second, grad_pre)
-    grad_second = product_right(grad_pre, whole[11])
-    grad_mid_norm, grad_gain_two, grad_bias_two = norm_two_back(grad_second)
-    grad_mid = grad_mid_norm + seed_full
-    grad_branch = grad_mid.astype(jnp.bfloat16)
-    grad_output_bias = jnp.sum(grad_branch.astype(jnp.float32), axis=0)
-    grad_output = product_left(attended_low, grad_branch)
-    grad_attended = product_right(grad_branch, whole[7]).astype(jnp.bfloat16)
     block = (lax.axis_size("grp"), n // 2, 2)
-
-    def blocks(v):
-        return v.astype(jnp.bfloat16).reshape(block + (-1, v.shape[1]))
-
-    sums = [v[None] for v in (grad_gain_two, grad_bias_two, grad_output_bias, grad_expand_bias, grad_reduce_bias)]
-    far = [blocks(grad_expand), blocks(grad_reduce), blocks(grad_output)]
+    far = [v.reshape(block + (-1, v.shape[1])) for v in (g_we, g_wr, g_wo)]
     inside = far if n <= 8 else []
     done = backward_call(
-        n, block[0], placement, pack_rows(grad_attended, splits), q_all, kv_all, ol_all, hidden, tokens[0],
-        whole[0][None], whole[2], whole[4], whole[5], grad_mid, sums,
+        n, block[0], placement, do_staged, q_all, kv_all, ol_all, hidden, tokens[0],
+        whole[0][None], whole[2], whole[4], whole[5], dmid, [sums[0], sums[1], sums[2], sums[3], sums[4]],
         inside,
     )
     token_grad, first_grad = done[:2]
@@ -1063,7 +1243,6 @@
         forth = powers(block[0])
         done = done[:2] + reduce_call(block[0], block[1], far, [forth, forth[::-1], forth]) + done[2:]
     g_we, g_wr, g_wo, g_wk, g_wq, g_wv, g_small = done[2:]
-    small = (0, 1, 3, 6, 8, 9, 10, 12, 14)
     sizes = [parts[i].shape[0] for i in small]
     out = hand_over([token_grad, first_grad, g_wq, g_wk, g_wv, g_wo, g_we, g_wr], g_small, sizes)
     owned = [None] * 15
@@ -1071,7 +1250,7 @@
         owned[i] = v
     for i, v in zip(small, out[8:]):
         owned[i] = v.reshape(-1)
-    return (layer_output, out[0][None], out[1][None]) + tuple(owned)
+    return (layer_output[None], out[0][None], out[1][None]) + tuple(owned)
 
 
 def solution(mesh):

time: 369 us -> 282 us (0.76); the launches traced: 364 us -> 282 us
  matrix products: 36.3 us -> 0 us
  local copies, waits for them, and re-layouts: 29.7 us -> 0 us
  Pallas kernels: 295 us -> 281 us
    dot_general x9 -> x0, matrix products: 36.3 us -> none  [the longest x3 12.3 us: product_left(): lax.dot_general(a, b, (((0,), (0,)), ((), ())), preferred_element_type=jn...]
    pallas_call x3, Pallas kernels: 158 us -> 144 us  [the longest x1 114 us: forward_call(): pl.pallas_call(functools.partial(forward_kernel, n, groups, heads, [forth...]
    unnamed x35 -> x0, local copies, waits for them, and re-layouts: 9.87 us -> none
    concatenate x1 -> x0, local copies, waits for them, and re-layouts: 6.1 us -> none  [collect(): packed = jnp.concatenate([parts[i] for i in small])]
    reshape x6 -> x0, local copies, waits for them, and re-layouts: 4.31 us -> none  [the longest x1 1.18 us: pack_rows(): return v.reshape(PARTS, heads // PARTS, splits, rows // splits // 2, 128)]
where the time goes in v4:
time: 282 us
  Pallas kernels  281 us (100%)
    pallas_call x1, Pallas kernels, backward_call(): pl.pallas_call(functools.partial(backward_kernel, n, groups, heads, [fort...  137 us
    pallas_call x1, Pallas kernels, forward_call(): pl.pallas_call(functools.partial(forward_kernel, n, groups, heads, [forth...  114 us
    pallas_call x1, Pallas kernels, feed_call(): pl.pallas_call(functools.partial(feed_kernel, parts, heads), out_shape=[s...  25.4 us

profile of v4, /device:TPU:0, one launch (start us, length us, event | category | flops | bytes accessed | tf_op | source)
XLA Modules:
  0.0 282.2 jit_solution(5699996736578413191)
XLA Ops:
  0.7 114.2 %attention_forward.1 = (bf16[512,768]{1,0:T(8,128)(2,1)}, bf16[3,8,128,128]{3,2,1,0:T(8,128)(2,1)}, bf16[3,8,512,128]{3,2,1,0:T(8,128)(2,1)}, f32[3,8,256,128]{3...) custom-call(s32[1,8]{1,0:T(1,128)} %table.3, ...), custom_call_target="tpu_custom_call" | custom-call | tf_op jit(solution)/shard_map/attention_forward/pallas_call | solution.py:730
  114.9 25.4 %feed_forward.1 = (bf16[512,768]{1,0:T(8,128)(2,1)}, f32[512,768]{1,0:T(8,128)}, bf16[4,3,2,128,128]{4,3,2,1,0:T(8,128)(2,1)}, f32[1,768]{1,0:T(1,128)}, f32[1,7...) custom-call(bf16[12,2,128,128]{3,2,1,0:T(8,128)(2,1)} %get-tuple-ele, ...), custom_call_target="tpu_custom_call" | custom-call | tf_op jit(solution)/shard_map/feed_forward/pallas_call | solution.py:1182
  140.3 137.2 %attention_backward.1 = (f32[512,768]{1,0:T(8,128)}, f32[512,384]{1,0:T(8,128)}, f32[24,3072]{1,0:T(8,128)}, f32[96,768]{1,0:T(8,128)}, f32[24,768]{1,0:T(8,128)...) custom-call(s32[1,8]{1,0:T(1,128)} %table.3, ...), custom_call_target="tpu_custom_call" | custom-call | tf_op jit(solution)/shard_map/attention_backward/pallas_call | solution.py:1017
  277.6 4.5 %hand_over.1 = (f32[512,768]{1,0:T(8,128)}, f32[512,384]{1,0:T(8,128)}, f32[24,768]{1,0:T(8,128)}, f32[24,768]{1,0:T(8,128)}, f32[24,384]{1,0:T(8,128)}, /*index...) custom-call(f32[512,768]{1,0:T(8,128)} %get-tuple-element.100.refs_0, ...), custom_call_target="tpu_custom_call" | custom-call | tf_op jit(solution)/shard_map/hand_over/pallas_call | solution.py:1072
